TPU v7x, 32 devices: a whole 2x2x4 slice. The times are simulated.
32 devices in a mesh: gx: 4 (over z), gy: 2 (over x), gz: 4 (over y, core).
Axes of the slice: x: 2, y: 2, z: 4, core: 2. Of those that a mesh axis runs over, the one named last changes fastest.
Arguments:
- coords: float32 [3, 4, 2, 4, 2048], P(None, 'gx', 'gy', 'gz'), may hold values from 0 to 6
- charges: float32 [2, 4, 2, 4, 2048], P(None, 'gx', 'gy', 'gz'), may hold values from -8 to 8
- dipoles: float32 [6, 4, 2, 4, 2048], P(None, 'gx', 'gy', 'gz'), may hold values from -6 to 6
- polar: float32 [2, 4, 2, 4, 2048], P(None, 'gx', 'gy', 'gz'), may hold values from 0.08 to 0.25
- perturbed: int32 [4, 2, 4, 2048], P('gx', 'gy', 'gz'), may hold values 0 or 1
- cluster_order: int32 [4, 2, 4, 2048], P('gx', 'gy', 'gz'), may hold values from 0 to 2047, each once within a row
- border_clusters: int32 [4, 2, 4, 4], P('gx', 'gy', 'gz'), may hold values from 0 to 15, as said below
- tile_list: int32 [3, 4, 2, 4, 128], P(None, 'gx', 'gy', 'gz'), may hold values from 0 to 26, as said below
- tile_count: int32 [4, 2, 4], P('gx', 'gy', 'gz'), may hold values from 112 to 128, as said below
Outputs:
- induced: float32 [6, 4, 2, 4, 2048], P(None, 'gx', 'gy', 'gz')
Inputs may be any that keep to these rules, and one draw needn't show every extreme that they name: `border_clusters`: each brick's entries are distinct cluster numbers of that brick. `tile_list`: row 0 is a cluster of the brick itself (0 to 15); row 1 a neighbour slot (0 to 26, 13 is the brick itself); row 2 is a cluster of the brick itself (0 to 15) where row 1 is 13, else a position (0 to 3) in the neighbour's border_clusters. Among the first 104 tiles of each brick, every pair of a neighbour slot other than 13 and a border position appears exactly once. `tile_count`: some brick uses all 128 tiles in every draw.
All inputs are finite; a program needn't handle non-finite values. No bound on the sum of `perturbed` on one device may be relied on, other than what follows from the above.
Results may differ from a plain program's by a relative error of at most 0.0003.
Values sent between devices are 32-bit elements; how exact they have to be, the bound alone decides.
No kernel may reach another device: no remote copies, remote signals or barrier semaphores. Data moves between devices by JAX's collectives and lax.ppermute only.
A program may use at most 64 MiB of HBM per device.

v0:
```python
import jax
import jax.numpy as jnp
from jax import lax
from jax.sharding import PartitionSpec as P

ITERS = 3


brick_len = 6.0
damping = 1.0
tile_block = 8


def padded(cells, sides, width):
    for axis, dim in sides:
        count = lax.axis_size(axis)
        head = lax.slice_in_dim(cells, 0, width, axis=dim)
        tail = lax.slice_in_dim(cells, cells.shape[dim] - width, cells.shape[dim], axis=dim)
        cells = jnp.concatenate(
            [
                lax.ppermute(tail, axis, [(i, (i + 1) % count) for i in range(count)]),
                cells,
                lax.ppermute(head, axis, [((i + 1) % count, i) for i in range(count)]),
            ],
            axis=dim,
        )
    return cells


def tile_fields(recv_places, source_places, source_data, tile_rows, tile_total, charged):
    clusters = recv_places.shape[1]
    border = (source_places.shape[1] - clusters) // 27
    tile_num = tile_rows.shape[1]
    blocks = tile_num // tile_block
    recv_id = tile_rows[0]
    slot_id = tile_rows[1]
    source = tile_rows[2]
    source_row = jnp.where(slot_id == 13, source, clusters + slot_id * border + source)
    shifts = (
        jnp.stack([slot_id // 9 - 1, slot_id // 3 % 3 - 1, slot_id % 3 - 1], axis=1).astype(
            jnp.float32
        )
        * brick_len
    )
    usable = (jnp.arange(tile_num, dtype=jnp.int32) < tile_total).astype(jnp.float32)
    same_tile = ((slot_id == 13) & (recv_id == source)).astype(jnp.float32)
    identity = jnp.eye(128, dtype=jnp.float32)

    def one_block(block_args):
        block_recv, block_row, block_shift, block_use, block_same = block_args
        recv_xyz = jnp.take(recv_places, block_recv, axis=1)
        source_xyz = jnp.take(source_places, block_row, axis=1) + block_shift.T[:, :, None]
        values = jnp.take(source_data, block_row, axis=1)
        separation = recv_xyz[:, :, :, None] - source_xyz[:, :, None, :]
        squared = jnp.sum(separation * separation, axis=0) + damping
        inverse = lax.rsqrt(squared)
        weight_mask = block_use[:, None, None] * (1.0 - block_same[:, None, None] * identity)
        third_power = inverse * inverse * inverse * weight_mask
        fifth_power = third_power * inverse * inverse
        pieces = []
        for which_state in range(2):
            first_row = 2 + 3 * which_state if charged else 3 * which_state
            moment = values[first_row : first_row + 3][:, :, None, :]
            projection = jnp.sum(moment * separation, axis=0)
            radial = 3.0 * projection * fifth_power
            if charged:
                radial = radial + values[which_state][:, None, :] * third_power
            pieces.append(jnp.sum(radial[None] * separation - moment * third_power[None], axis=3))
        return jnp.concatenate(pieces, axis=0)

    shaped = (
        recv_id.reshape(blocks, tile_block),
        source_row.reshape(blocks, tile_block),
        shifts.reshape(blocks, tile_block, 3),
        usable.reshape(blocks, tile_block),
        same_tile.reshape(blocks, tile_block),
    )
    block_sums = lax.map(one_block, shaped)
    block_sums = jnp.transpose(block_sums, (0, 2, 1, 3)).reshape(tile_num, 6 * 128)
    member = (recv_id[:, None] == jnp.arange(clusters, dtype=jnp.int32)[None, :]).astype(
        jnp.float32
    )
    summed = jnp.dot(member.T, block_sums, precision=lax.Precision.HIGHEST)
    return jnp.transpose(summed.reshape(clusters, 6, 128), (1, 0, 2))


def state_sums(vector):
    return jnp.sum(vector.reshape(2, -1), axis=1)


def spread(values):
    return jnp.repeat(values, 3)[:, None]


def joint_sums(first_vec, second_vec, third_vec, fourth_vec):
    return lax.psum(
        (
            state_sums(first_vec),
            state_sums(second_vec),
            state_sums(third_vec),
            state_sums(fourth_vec),
        ),
        ("gx", "gy", "gz"),
    )


def shards(
    coords,
    charges,
    dipoles,
    polar,
    perturbed,
    cluster_order,
    border_clusters,
    tile_list,
    tile_count,
):
    atoms = coords.shape[-1]
    clusters = atoms // 128
    border = border_clusters.shape[-1]
    arrangement = cluster_order.reshape(atoms)
    changed = perturbed.reshape(1, atoms) == 1
    charge_flat = charges.reshape(2, atoms)
    dipole_flat = dipoles.reshape(6, atoms)
    polar_flat = polar.reshape(2, atoms)
    charge_both = jnp.concatenate(
        [charge_flat[:1], jnp.where(changed, charge_flat[1:], charge_flat[:1])], 0
    )
    moments = jnp.concatenate(
        [dipole_flat[:3], jnp.where(changed, dipole_flat[3:], dipole_flat[:3])], 0
    )
    polar_both = jnp.concatenate(
        [polar_flat[:1], jnp.where(changed, polar_flat[1:], polar_flat[:1])], 0
    )
    places = coords.reshape(3, atoms)[:, arrangement]
    multipoles = jnp.concatenate([charge_both, moments], 0)[:, arrangement]
    response = jnp.repeat(polar_both, 3, axis=0)[:, arrangement]
    border_atoms = (
        border_clusters.reshape(border, 1) * 128 + jnp.arange(128, dtype=jnp.int32)
    ).reshape(-1)
    tile_rows = tile_list.reshape(3, -1)
    tile_total = tile_count.reshape(())
    recv_places = places.reshape(3, clusters, 128)
    outgoing = jnp.concatenate([places, multipoles], 0)[:, border_atoms].reshape(
        11, 1, 1, 1, border * 128
    )
    incoming = padded(outgoing, (("gx", 1), ("gy", 2), ("gz", 3)), 1)
    incoming = incoming.reshape(11, 27 * border, 128)
    source_places = jnp.concatenate([recv_places, incoming[:3]], 1)
    multipole_source = jnp.concatenate([multipoles.reshape(8, clusters, 128), incoming[3:]], 1)
    permanent = tile_fields(
        recv_places, source_places, multipole_source, tile_rows, tile_total, True
    ).reshape(6, atoms)

    def operator_t(vector):
        outgoing_vec = vector[:, border_atoms].reshape(6, 1, 1, 1, border * 128)
        arrived = padded(outgoing_vec, (("gx", 1), ("gy", 2), ("gz", 3)), 1)
        source_vec = jnp.concatenate(
            [vector.reshape(6, clusters, 128), arrived.reshape(6, 27 * border, 128)], 1
        )
        return tile_fields(
            recv_places, source_places, source_vec, tile_rows, tile_total, False
        ).reshape(6, atoms)

    induced = response * permanent
    residual = operator_t(induced)
    scaled = response * residual
    image = scaled / response - operator_t(scaled)
    norm_now, curve_now, unused_one, unused_two = joint_sums(
        residual * scaled, scaled * image, scaled * image, scaled * image
    )
    step_len = norm_now / curve_now
    direction = scaled
    along = image
    for sweep in range(ITERS):
        induced = induced + spread(step_len) * direction
        residual = residual - spread(step_len) * along
        if sweep + 1 < ITERS:
            scaled = response * residual
            image = scaled / response - operator_t(scaled)
            norm_next, plain_curve, cross_old, cross_new = joint_sums(
                residual * scaled, scaled * image, scaled * along, direction * image
            )
            ratio = norm_next / norm_now
            curve_now = plain_curve + ratio * (cross_old + cross_new) + ratio * ratio * curve_now
            step_len = norm_next / curve_now
            direction = scaled + spread(ratio) * direction
            along = image + spread(ratio) * along
            norm_now = norm_next
    result = jnp.zeros_like(induced).at[:, arrangement].set(induced)
    return result.reshape(6, 1, 1, 1, atoms)


def solution(mesh):
    placed = (
        P(None, "gx", "gy", "gz", None),
        P(None, "gx", "gy", "gz", None),
        P(None, "gx", "gy", "gz", None),
        P(None, "gx", "gy", "gz", None),
        P("gx", "gy", "gz", None),
        P("gx", "gy", "gz", None),
        P("gx", "gy", "gz", None),
        P(None, "gx", "gy", "gz", None),
        P("gx", "gy", "gz"),
    )
    return jax.shard_map(
        shards,
        mesh=mesh,
        in_specs=placed,
        out_specs=P(None, "gx", "gy", "gz", None),
        check_vma=False,
    )
```

profile of v0, /device:TPU:0, one launch (start us, length us, event | category | flops | bytes accessed | tf_op | source)
XLA Modules:
  0.0 660.0 jit_solution(9498030858751108781)
XLA Ops:
  3.9 5.5 gather_fusion.16
  9.3 5.5 gather_fusion.17
  16.3 3.1 collective-permute-start
  19.4 2.1 collective-permute-start.1
  23.8 4.8 collective-permute-done
  28.8 4.0 collective-permute-done.1
  35.6 5.5 gather_fusion.15
  41.7 1.7 collective-permute-start.5
  43.4 3.8 collective-permute-done.4
  49.8 76.4 %while.55 = (s32[]{:T(128)}, f32[16,6,8,128]{3,2,1,0:T(8,128)S(1)}, s32[16,8]{1,0:T(8,128)S(1)}, f32[8,124,128]{2,0,1:T(8,128)S(1)}, s32[16,8]{1,0:T(8,128)S(1)}...) while((s32[]{:T(128)}, f32[16,6,8,128]{3,2,1,0:T(8,128)S(1)}, ...), condition=%wide.region_6.9_spmd.clone, body=%wide.region_0.8_spmd.clone.sunk | while | flops 8179834 | bytes 7009481 | solution.py:78
  52.9 1.6 fusion.166
  57.7 1.6 fusion.166
  62.5 1.6 fusion.166
  67.3 1.6 fusion.166
  91.1 1.6 fusion.166
  95.9 1.6 fusion.166
  100.7 1.6 fusion.166
  105.5 1.6 fusion.166
  110.2 1.6 fusion.166
  129.3 2.7 collective-permute-start.7
  132.1 7.1 %collective-permute-done.6 = f32[6,1,1,1,512]{0,4,3,2,1:T(8,128)S(1)} collective-permute-done((f32[6,1,1,1,512]{0,4,3,2,1:T(8,128)S(1)}, f32[6,1,1,1,512]{0,4,3,2,1:T(8,128)S(1)}, u32[]{:S(2)}, u32[]{:S(2)}) %collective-permute-start.6) | collective-permute-done | bytes 12320 | tf_op jit(solution)/shard_map/ppermute | solution.py:21
  139.3 4.3 collective-permute-done.7
  145.8 2.2 collective-permute-done.8
  149.4 1.7 collective-permute-start.11
  151.2 2.4 collective-permute-done.10
  154.0 74.4 %while.56 = (s32[]{:T(128)}, f32[16,6,8,128]{3,2,1,0:T(8,128)S(1)}, s32[16,8]{1,0:T(8,128)S(1)}, f32[6,124,128]{2,0,1:T(8,128)S(1)}, s32[16,8]{1,0:T(8,128)S(1)}...) while((s32[]{:T(128)}, f32[16,6,8,128]{3,2,1,0:T(8,128)S(1)}, ...), condition=%wide.region_13.17_spmd.clone, body=%wide.region_7.16_spmd.clone.sunk | while | flops 7652450 | bytes 6947941 | solution.py:78
  161.7 1.6 fusion.172
  166.3 1.6 fusion.172
  175.6 1.6 fusion.172
  180.3 1.6 fusion.172
  189.6 1.6 fusion.172
  203.5 1.6 fusion.172
  212.8 1.6 fusion.172
  217.5 1.6 fusion.172
  226.8 1.6 fusion.172
  231.2 3.0 collective-permute-start.13
  234.3 6.7 %collective-permute-done.12 = f32[6,1,1,1,512]{0,4,3,2,1:T(8,128)S(1)} collective-permute-done((f32[6,1,1,1,512]{0,4,3,2,1:T(8,128)S(1)}, f32[6,1,1,1,512]{0,4,3,2,1:T(8,128)S(1)}, u32[]{:S(2)}, u32[]{:S(2)}) %collective-permute-start.12) | collective-permute-done | bytes 12320 | tf_op jit(solution)/shard_map/ppermute | solution.py:21
  241.1 4.8 collective-permute-done.13
  248.1 1.9 collective-permute-done.14
  250.8 1.7 collective-permute-start.17
  252.5 2.4 collective-permute-done.16
  255.1 74.4 %while.57 = (s32[]{:T(128)}, f32[16,6,8,128]{3,2,1,0:T(8,128)S(1)}, s32[16,8]{1,0:T(8,128)S(1)}, f32[6,124,128]{2,0,1:T(8,128)S(1)}, s32[16,8]{1,0:T(8,128)S(1)}...) while((s32[]{:T(128)}, f32[16,6,8,128]{3,2,1,0:T(8,128)S(1)}, ...), condition=%wide.region_23.27_spmd.clone, body=%wide.region_17.26_spmd.clone.sunk | while | flops 7652450 | bytes 6947941 | solution.py:78
  258.2 1.6 fusion.178
  262.8 1.6 fusion.178
  330.5 40.0 %all-reduce.2 = (f32[2]{0:T(128)S(1)}, f32[2]{0:T(128)S(1)}) all-reduce(f32[2]{0:T(128)S(1)} %reduce_sum.387, f32[2]{0:T(128)S(1)} %reduce_sum.390), channel_id=1, replica_groups=mesh['gx'=4,'gy'=2,'gz'=4] {'gx','gy','gz'}, use_global_device_ids=true, to_apply=%region_16.20 | all-reduce | flops 4 | bytes 32 | tf_op jit(solution)/shard_map/psum | solution.py:96
  373.1 3.0 collective-permute-start.19
  376.2 7.0 %collective-permute-done.18 = f32[6,1,1,1,512]{0,4,3,2,1:T(8,128)S(1)} collective-permute-done((f32[6,1,1,1,512]{0,4,3,2,1:T(8,128)S(1)}, f32[6,1,1,1,512]{0,4,3,2,1:T(8,128)S(1)}, u32[]{:S(2)}, u32[]{:S(2)}) %collective-permute-start.18) | collective-permute-done | bytes 12320 | tf_op jit(solution)/shard_map/ppermute | solution.py:21
  383.4 2.3 collective-permute-done.19
  387.9 1.9 collective-permute-done.20
  391.3 1.7 collective-permute-start.23
  393.2 2.3 collective-permute-done.22
  395.9 74.4 %while.58 = (s32[]{:T(128)}, f32[16,6,8,128]{3,2,1,0:T(8,128)S(1)}, s32[16,8]{1,0:T(8,128)S(1)}, f32[6,124,128]{2,0,1:T(8,128)S(1)}, s32[16,8]{1,0:T(8,128)S(1)}...) while((s32[]{:T(128)}, f32[16,6,8,128]{3,2,1,0:T(8,128)S(1)}, ...), condition=%wide.region_36.40_spmd.clone, body=%wide.region_30.39_spmd.clone.sunk | while | flops 7652450 | bytes 6947941 | solution.py:78
  471.7 39.4 %all-reduce.1 = (f32[2]{0:T(128)S(1)}, f32[2]{0:T(128)S(1)}, f32[2]{0:T(128)S(1)}) all-reduce(f32[2]{0:T(128)S(1)} %reduce_sum.393, f32[2]{0:T(128)S(1)} %reduce_sum.396, f32[2]{0:T(128)S(1)} %add.403), channel_id=1, replica_groups=mesh['gx'=4,'gy'=2,'gz'=4] {'gx','gy','gz'}, use_global_device_ids=true, to_apply=%region_29.33 | all-reduce | flops 6 | bytes 48 | tf_op jit(solution)/shard_map/psum | solution.py:96
  513.6 3.2 collective-permute-start.25
  516.9 7.1 %collective-permute-done.24 = f32[6,1,1,1,512]{0,4,3,2,1:T(8,128)S(1)} collective-permute-done((f32[6,1,1,1,512]{0,4,3,2,1:T(8,128)S(1)}, f32[6,1,1,1,512]{0,4,3,2,1:T(8,128)S(1)}, u32[]{:S(2)}, u32[]{:S(2)}) %collective-permute-start.24) | collective-permute-done | bytes 12320 | tf_op jit(solution)/shard_map/ppermute | solution.py:21
  524.0 2.1 collective-permute-done.25
  526.3 2.3 collective-permute-start.26
  528.7 1.9 collective-permute-done.26
  530.6 2.0 collective-permute-done.27
  532.8 1.7 collective-permute-start.29
  534.6 2.6 collective-permute-done.28
  537.4 74.4 %while.59 = (s32[]{:T(128)}, f32[16,6,8,128]{3,2,1,0:T(8,128)S(1)}, s32[16,8]{1,0:T(8,128)S(1)}, f32[6,124,128]{2,0,1:T(8,128)S(1)}, s32[16,8]{1,0:T(8,128)S(1)}...) while((s32[]{:T(128)}, f32[16,6,8,128]{3,2,1,0:T(8,128)S(1)}, ...), condition=%wide.region_55.59_spmd.clone, body=%wide.region_49.58_spmd.clone.sunk | while | flops 7652450 | bytes 6947941 | solution.py:78
  613.2 39.2 %all-reduce = (f32[2]{0:T(128)S(1)}, f32[2]{0:T(128)S(1)}, f32[2]{0:T(128)S(1)}) all-reduce(f32[2]{0:T(128)S(1)} %reduce_sum.405, f32[2]{0:T(128)S(1)} %reduce_sum.408, f32[2]{0:T(128)S(1)} %add.411), channel_id=1, replica_groups=mesh['gx'=4,'gy'=2,'gz'=4] {'gx','gy','gz'}, use_global_device_ids=true, to_apply=%region_48.52 | all-reduce | flops 6 | bytes 48 | tf_op jit(solution)/shard_map/psum | solution.py:96
  653.2 5.8 scatter_custom_fusion
  (1992 shorter events, 372.8 us)
Async XLA Ops:
  0.0 3.4 copy-start.2
  0.0 3.5 copy-start.1
  3.5 11.4 %copy-start.4 = (s32[1,1,1,4]{3,2,1,0:T(1,128)S(1)}, s32[1,1,1,4]{3,2,1,0:T(1,128)}, u32[]{:S(2)}) copy-start(s32[1,1,1,4]{3,2,1,0:T(1,128)} %param.31) | copy-start | bytes 52
  14.9 6.6 %copy-start.3 = (s32[3,1,1,1,128]{4,3,2,1,0:T(1,128)S(1)}, s32[3,1,1,1,128]{4,3,2,1,0:T(1,128)}, u32[]{:S(2)}) copy-start(s32[3,1,1,1,128]{4,3,2,1,0:T(1,128)} %param.32) | copy-start | bytes 4612
  14.9 6.7 %copy-start = (f32[2,1,1,1,2048]{4,3,2,1,0:T(1,128)S(1)}, f32[2,1,1,1,2048]{4,3,2,1,0:T(1,128)}, u32[]{:S(2)}) copy-start(f32[2,1,1,1,2048]{4,3,2,1,0:T(1,128)} %param.28) | copy-start | bytes 49156
  16.3 12.3 %collective-permute-start = (f32[11,1,1,1,512]{0,4,3,2,1:T(8,128)S(1)}, f32[11,1,1,1,512]{0,4,3,2,1:T(8,128)S(1)}, u32[]{:S(2)}, u32[]{:S(2)}) collective-permute-start(f32[11,1,1,1,512]{0,4,3,2,1:T(8,128)S(1)} %bitcast.468), channel_id=1, source_target_pairs={{0,8},{8,16},{16,24},{24,0},{1,9},{9,17},{17,25},{25,1},{2,10},{10... | collective-permute-start | bytes 67592 | tf_op jit(solution)/shard_map/ppermute | solution.py:21
  19.4 13.4 %collective-permute-start.1 = (f32[11,1,1,1,512]{0,4,3,2,1:T(8,128)S(1)}, f32[11,1,1,1,512]{0,4,3,2,1:T(8,128)S(1)}, u32[]{:S(2)}, u32[]{:S(2)}) collective-permute-start(f32[11,1,1,1,512]{0,4,3,2,1:T(8,128)S(1)} %bitcast.469), channel_id=1, source_target_pairs={{8,0},{16,8},{24,16},{0,24},{9,1},{17,9},{25,17},{1,25},{10,2},{18... | collective-permute-start | bytes 67592 | tf_op jit(solution)/shard_map/ppermute | solution.py:23
  33.0 8.4 %collective-permute-start.2 = (f32[11,3,1,1,512]{4,3,2,1,0:T(1,128)S(1)}, f32[11,3,1,1,512]{4,3,2,1,0:T(1,128)S(1)}, u32[]{:S(2)}, u32[]{:S(2)}) collective-permute-start(f32[11,3,1,1,512]{4,3,2,1,0:T(1,128)S(1)} %pad_maximum_fusion.18), channel_id=1, source_target_pairs={{0,4},{4,0},{1,5},{5,1},{2,6},{6,2},{3,7},{7,3},{8,12},{12,8},{9,1... | collective-permute-start | bytes 202760 | tf_op jit(solution)/shard_map/ppermute | solution.py:21
  34.6 6.9 %collective-permute-start.3 = (f32[11,3,1,1,512]{4,3,2,1,0:T(1,128)S(1)}, f32[11,3,1,1,512]{4,3,2,1,0:T(1,128)S(1)}, u32[]{:S(2)}, u32[]{:S(2)}) collective-permute-start(f32[11,3,1,1,512]{4,3,2,1,0:T(1,128)S(1)} %pad_maximum_fusion.18), channel_id=1, source_target_pairs={{4,0},{0,4},{5,1},{1,5},{6,2},{2,6},{7,3},{3,7},{12,8},{8,12},{13,... | collective-permute-start | bytes 202760 | tf_op jit(solution)/shard_map/ppermute | solution.py:23
  41.6 5.6 collective-permute-start.4
  41.7 6.4 collective-permute-start.5
  128.1 11.1 %collective-permute-start.6 = (f32[6,1,1,1,512]{0,4,3,2,1:T(8,128)S(1)}, f32[6,1,1,1,512]{0,4,3,2,1:T(8,128)S(1)}, u32[]{:S(2)}, u32[]{:S(2)}) collective-permute-start(f32[6,1,1,1,512]{0,4,3,2,1:T(8,128)S(1)} %bitcast.474), channel_id=1, source_target_pairs={{0,8},{8,16},{16,24},{24,0},{1,9},{9,17},{17,25},{25,1},{2,10},{10... | collective-permute-start | bytes 36872 | tf_op jit(solution)/shard_map/ppermute | solution.py:21
  129.3 14.3 %collective-permute-start.7 = (f32[6,1,1,1,512]{0,4,3,2,1:T(8,128)S(1)}, f32[6,1,1,1,512]{0,4,3,2,1:T(8,128)S(1)}, u32[]{:S(2)}, u32[]{:S(2)}) collective-permute-start(f32[6,1,1,1,512]{0,4,3,2,1:T(8,128)S(1)} %bitcast.475), channel_id=1, source_target_pairs={{8,0},{16,8},{24,16},{0,24},{9,1},{17,9},{25,17},{1,25},{10,2},{18... | collective-permute-start | bytes 36872 | tf_op jit(solution)/shard_map/ppermute | solution.py:23
  143.7 4.3 collective-permute-start.8
  145.3 4.0 collective-permute-start.9
  149.4 4.2 collective-permute-start.10
  149.4 4.4 collective-permute-start.11
  230.3 10.7 %collective-permute-start.12 = (f32[6,1,1,1,512]{0,4,3,2,1:T(8,128)S(1)}, f32[6,1,1,1,512]{0,4,3,2,1:T(8,128)S(1)}, u32[]{:S(2)}, u32[]{:S(2)}) collective-permute-start(f32[6,1,1,1,512]{0,4,3,2,1:T(8,128)S(1)} %bitcast.477), channel_id=1, source_target_pairs={{0,8},{8,16},{16,24},{24,0},{1,9},{9,17},{17,25},{25,1},{2,10},{10... | collective-permute-start | bytes 36872 | tf_op jit(solution)/shard_map/ppermute | solution.py:21
  231.2 14.6 %collective-permute-start.13 = (f32[6,1,1,1,512]{0,4,3,2,1:T(8,128)S(1)}, f32[6,1,1,1,512]{0,4,3,2,1:T(8,128)S(1)}, u32[]{:S(2)}, u32[]{:S(2)}) collective-permute-start(f32[6,1,1,1,512]{0,4,3,2,1:T(8,128)S(1)} %bitcast.478), channel_id=1, source_target_pairs={{8,0},{16,8},{24,16},{0,24},{9,1},{17,9},{25,17},{1,25},{10,2},{18... | collective-permute-start | bytes 36872 | tf_op jit(solution)/shard_map/ppermute | solution.py:23
  246.0 4.0 collective-permute-start.14
  246.6 4.0 collective-permute-start.15
  250.7 4.2 collective-permute-start.16
  250.8 4.2 collective-permute-start.17
  372.2 11.0 %collective-permute-start.18 = (f32[6,1,1,1,512]{0,4,3,2,1:T(8,128)S(1)}, f32[6,1,1,1,512]{0,4,3,2,1:T(8,128)S(1)}, u32[]{:S(2)}, u32[]{:S(2)}) collective-permute-start(f32[6,1,1,1,512]{0,4,3,2,1:T(8,128)S(1)} %bitcast.480), channel_id=1, source_target_pairs={{0,8},{8,16},{16,24},{24,0},{1,9},{9,17},{17,25},{25,1},{2,10},{10... | collective-permute-start | bytes 36872 | tf_op jit(solution)/shard_map/ppermute | solution.py:21
  373.1 12.6 %collective-permute-start.19 = (f32[6,1,1,1,512]{0,4,3,2,1:T(8,128)S(1)}, f32[6,1,1,1,512]{0,4,3,2,1:T(8,128)S(1)}, u32[]{:S(2)}, u32[]{:S(2)}) collective-permute-start(f32[6,1,1,1,512]{0,4,3,2,1:T(8,128)S(1)} %bitcast.481), channel_id=1, source_target_pairs={{8,0},{16,8},{24,16},{0,24},{9,1},{17,9},{25,17},{1,25},{10,2},{18... | collective-permute-start | bytes 36872 | tf_op jit(solution)/shard_map/ppermute | solution.py:23
  385.8 4.0 collective-permute-start.20
  387.2 4.0 collective-permute-start.21
  391.3 4.2 collective-permute-start.22
  391.3 4.4 collective-permute-start.23
  512.9 11.0 %collective-permute-start.24 = (f32[6,1,1,1,512]{0,4,3,2,1:T(8,128)S(1)}, f32[6,1,1,1,512]{0,4,3,2,1:T(8,128)S(1)}, u32[]{:S(2)}, u32[]{:S(2)}) collective-permute-start(f32[6,1,1,1,512]{0,4,3,2,1:T(8,128)S(1)} %bitcast.471), channel_id=1, source_target_pairs={{0,8},{8,16},{16,24},{24,0},{1,9},{9,17},{17,25},{25,1},{2,10},{10... | collective-permute-start | bytes 36872 | tf_op jit(solution)/shard_map/ppermute | solution.py:21
  513.6 12.6 %collective-permute-start.25 = (f32[6,1,1,1,512]{0,4,3,2,1:T(8,128)S(1)}, f32[6,1,1,1,512]{0,4,3,2,1:T(8,128)S(1)}, u32[]{:S(2)}, u32[]{:S(2)}) collective-permute-start(f32[6,1,1,1,512]{0,4,3,2,1:T(8,128)S(1)} %bitcast.472), channel_id=1, source_target_pairs={{8,0},{16,8},{24,16},{0,24},{9,1},{17,9},{25,17},{1,25},{10,2},{18... | collective-permute-start | bytes 36872 | tf_op jit(solution)/shard_map/ppermute | solution.py:23
  526.3 4.2 collective-permute-start.26
  528.6 4.0 collective-permute-start.27
  532.7 4.5 collective-permute-start.28
  532.8 4.5 collective-permute-start.29
where the time goes:
time: 661 us; the launch traced here: 660 us
  other arithmetic  222 us (34%)
  local copies, waits for them, and re-layouts  187 us (28%)
  blocking collectives  119 us (18%)
  waiting for transfers between devices  77.9 us (12%)
  starting transfers between devices  40.4 us (6%)
  loops' own time  11.6 us (2%)
    reduce_sum x80, other arithmetic, one_block(): jnp.sum(radial[None] * separation - moment * third_power[None], axis=3)  127 us
    psum x3, blocking collectives, joint_sums(): lax.psum((state_sums(first_vec), state_sums(second_vec), state_sums(third...  119 us
    ppermute x15, waiting for transfers between devices, padded(): lax.ppermute(tail, axis, [(i, (i + 1) % count) for i in range(count)])  54 us
    gather x80, local copies, waits for them, and re-layouts, one_block(): jnp.take(source_places, block_row, axis=1) + block_shift.T[:, :, None]  46 us
    gather x80, local copies, waits for them, and re-layouts, one_block(): recv_xyz = jnp.take(recv_places, block_recv, axis=1)  46 us
    gather x80, local copies, waits for them, and re-layouts, one_block(): values = jnp.take(source_data, block_row, axis=1)  44.4 us
    reduce_sum x80, other arithmetic, one_block(): projection = jnp.sum(moment * separation, axis=0)  41.1 us
    ppermute x15, starting transfers between devices, padded(): lax.ppermute(head, axis, [((i + 1) % count, i) for i in range(count)])  25.9 us
  transfers between devices with their start and end apart: 30, of which 26 were waited for; matrix products, arithmetic and copies ran while one was open for 1% of the time, Pallas kernels for 0%

commit v1 on v0

v1 whole, which is shorter than its diff:
```python
import jax
import jax.numpy as jnp
from jax import lax
from jax.experimental import pallas as pl
from jax.experimental.pallas import tpu as pltpu
from jax.sharding import PartitionSpec as P

ITERS = 3
LANES = 128
BRICK = 6.0
STATES = 2
COLS = 16
QCOLS = 4
F32 = jnp.float32
BF16 = jnp.bfloat16
AXES = ("gx", "gy", "gz")
GRAM = tuple((a, b) for a in range(ITERS) for b in range(a, ITERS + 1))

VMEM = pl.BlockSpec(memory_space=pltpu.VMEM)
SMEM = pl.BlockSpec(memory_space=pltpu.SMEM)


def thirds(value):
    high = value.astype(BF16).astype(F32)
    rest = value - high
    middle = rest.astype(BF16).astype(F32)
    return high, middle, rest - middle


def call(kernel, shapes, spaces, scratch=(), limit=None):
    return pl.pallas_call(
        kernel,
        out_shape=[jax.ShapeDtypeStruct(shape, dtype) for shape, dtype in shapes],
        in_specs=spaces,
        out_specs=[VMEM] * len(shapes),
        scratch_shapes=list(scratch),
        compiler_params=pltpu.CompilerParams(vmem_limit_bytes=limit),
    )


def lane_take(rows, lane):
    return jnp.take_along_axis(rows, lane, axis=1, mode="promise_in_bounds")


def permuted(order, rows):
    chunks = order.shape[0]
    lane, chunk = order & (LANES - 1), order >> 7
    picked = [jnp.zeros(order.shape, F32) for _ in rows]
    for c in range(chunks):
        here = chunk == c
        for k, row in enumerate(rows):
            taken = lane_take(jnp.broadcast_to(row[c : c + 1, :], order.shape), lane)
            picked[k] = jnp.where(here, taken, picked[k])
    return picked


def prepare_kernel(coords, charges, dipoles, polar, perturbed, order, border,
                   place, multi, response, outgoing):
    changed = perturbed[...] == 1
    rows = [coords[k] - 0.5 * BRICK for k in range(3)]
    rows += [charges[0], jnp.where(changed, charges[1], charges[0])]
    rows += [dipoles[k] for k in range(3)]
    rows += [jnp.where(changed, dipoles[3 + k], dipoles[k]) for k in range(3)]
    rows += [polar[0], jnp.where(changed, polar[1], polar[0])]
    done = permuted(order[...], rows)
    for k in range(3):
        place[k] = done[k]
    for k in range(8):
        multi[k] = done[3 + k]
    for k in range(2):
        response[k] = done[11 + k]
    for b in range(outgoing.shape[1]):
        row = pl.ds(border[b], 1)
        for k in range(3):
            outgoing[k, pl.ds(b, 1), :] = place[k, row, :]
        for k in range(8):
            outgoing[3 + k, pl.ds(b, 1), :] = multi[k, row, :]


def inverse_kernel(order, inverse):
    clusters = order.shape[0]
    column = jnp.transpose(order[...].astype(F32))
    lanes = lax.broadcasted_iota(jnp.int32, (8, LANES), 1).astype(F32)
    subs = lax.broadcasted_iota(jnp.int32, (8, LANES), 0).astype(F32)
    total = [jnp.zeros((8, LANES), F32) for _ in range(clusters)]
    for c in range(clusters):
        for g in range(LANES // 8):
            value = jnp.broadcast_to(column[8 * g : 8 * g + 8, c : c + 1], (8, LANES))
            slot = subs + float(c * LANES + 8 * g)
            for a in range(clusters):
                total[a] = jnp.where(value == lanes + float(a * LANES), slot, total[a])
    for a in range(clusters):
        inverse[a : a + 1, :] = jnp.sum(total[a], axis=0, keepdims=True).astype(jnp.int32)


def tile_row(tiles, count, clusters, border, t):
    slot = tiles[1, t]
    source = tiles[2, t]
    row = jnp.where(slot == 13, source, clusters + slot * border + source)
    return jnp.where(t < count[0], row, clusters + 13 * border)


def gather_rows(target, own, halo, where, border, shift=False):
    clusters = own.shape[1]
    kinds = own.shape[0]
    for k in range(kinds):
        target[k, 0:clusters, :] = own[k]
    for slot in range(27):
        base = clusters + slot * border
        for k in range(kinds):
            if slot == 13:
                piece = jnp.zeros((border, LANES), F32)
            else:
                ref, index = where[slot]
                piece = halo[ref][index + (k + (0 if shift else 0),)]
            target[k, base : base + border, :] = piece
    used = clusters + 27 * border
    for k in range(kinds):
        if target.shape[1] > used:
            target[k, used:, :] = jnp.zeros((target.shape[1] - used, LANES), F32)


def write_columns(flat, y, v, rows):
    width = STATES * COLS
    for g in range(rows // 8):
        at = slice(8 * g, 8 * g + 8)
        ys = [y[k, at, :] for k in range(3)]
        far = ys[0] * ys[0] + ys[1] * ys[1] + ys[2] * ys[2]
        for s in range(STATES):
            vs = [v[3 * s + k, at, :] for k in range(3)]
            out = list(vs)
            prods = [[vs[b] * ys[k] for k in range(3)] for b in range(3)]
            for b in range(3):
                out += prods[b]
            trace = 3.0 * (prods[0][0] + prods[1][1] + prods[2][2])
            out += [trace * ys[b] - far * vs[b] for b in range(3)]
            out.append(jnp.zeros((8, LANES), F32))
            for c in range(COLS):
                flat[pl.ds(8 * g * width + s * COLS + c, 8, stride=width), :] = out[c]


def split_columns(flat, parts, rows):
    width = STATES * COLS

    def one(r, carry):
        block = flat[pl.ds(pl.multiple_of(r * width, 8), width), :]
        parts[r] = jnp.concatenate(thirds(block), axis=0).astype(BF16)
        return carry

    lax.fori_loop(0, rows, one, None, unroll=4)


def fold(product):
    width = STATES * COLS
    return product[0:width] + product[width : 2 * width] + product[2 * width : 3 * width]


def combine(sums, x, v, selves):
    clusters = x[0].shape[0]
    width = STATES * COLS
    reach = x[0] * x[0] + x[1] * x[1] + x[2] * x[2] + 1.0
    fields = []
    for s in range(STATES):
        def col(c):
            return sums[pl.ds(s * COLS + c, clusters, stride=width), :]

        plain = [col(b) for b in range(3)]
        cross = [[col(3 + 3 * b + k) for k in range(3)] for b in range(3)]
        outer = [col(12 + b) for b in range(3)]
        inner = x[0] * plain[0] + x[1] * plain[1] + x[2] * plain[2]
        inner = 3.0 * (inner - (cross[0][0] + cross[1][1] + cross[2][2]))
        for b in range(3):
            value = x[b] * inner - reach * plain[b] + outer[b]
            for k in range(3):
                value = value + x[k] * (2.0 * cross[b][k] - 3.0 * cross[k][b])
            fields.append(value + selves * v[3 * s + b])
    return fields


def build_kernel(where, parts_of, *refs):
    tiles, count, border_ids, place, multi, response = refs[:6]
    halo = refs[6 : 6 + parts_of]
    induced, outgoing, matrix, y, selves = refs[6 + parts_of : 11 + parts_of]
    sources, flat, flat_q, parts, parts_q, turned, sums, sums_q = refs[11 + parts_of :]
    clusters = place.shape[1]
    border = outgoing.shape[1]
    padded = y.shape[1]
    tile_num = tiles.shape[1]
    qwidth = STATES * QCOLS

    for k in range(3):
        y[k, 0:clusters, :] = place[k]
        y[k, clusters:, :] = jnp.zeros((padded - clusters, LANES), F32)
    for k in range(8):
        sources[k, 0:clusters, :] = multi[k]
        sources[k, clusters:, :] = jnp.zeros((padded - clusters, LANES), F32)
    for slot in range(27):
        if slot == 13:
            continue
        ref, index = where[slot]
        base = clusters + slot * border
        offset = (slot // 9 - 1, slot // 3 % 3 - 1, slot % 3 - 1)
        for k in range(3):
            y[k, base : base + border, :] = halo[ref][index + (k,)] + BRICK * offset[k]
        for k in range(8):
            sources[k, base : base + border, :] = halo[ref][index + (3 + k,)]
    for k in range(3):
        turned[k] = jnp.transpose(y[k])

    write_columns(flat, y, sources.at[pl.ds(2, 6)], padded)
    for g in range(padded // 8):
        at = slice(8 * g, 8 * g + 8)
        for s in range(STATES):
            charge = sources[s, at, :]
            out = [charge] + [charge * y[k, at, :] for k in range(3)]
            for c in range(QCOLS):
                flat_q[pl.ds(8 * g * qwidth + s * QCOLS + c, 8, stride=qwidth), :] = out[c]
    split_columns(flat, parts, padded)

    def one_q(r, carry):
        block = flat_q[pl.ds(pl.multiple_of(r * qwidth, 8), qwidth), :]
        pieces = thirds(block) + (jnp.zeros_like(block),)
        parts_q[r] = jnp.concatenate(pieces, axis=0).astype(BF16)
        return carry

    lax.fori_loop(0, padded, one_q, None, unroll=4)

    sums[...] = jnp.zeros_like(sums)
    sums_q[...] = jnp.zeros_like(sums_q)
    selves[...] = jnp.zeros_like(selves)
    width = STATES * COLS

    def one(t, carry):
        recv = tiles[0, t]
        row = tile_row(tiles, count, clusters, border, t)
        same = jnp.logical_and(row == recv, row < clusters)
        pick = jnp.full((LANES, LANES), row, jnp.int32)
        d = [
            place[k, pl.ds(recv, 1), :] - lane_take(turned[k], pick)
            for k in range(3)
        ]
        squared = d[0] * d[0] + (d[1] * d[1] + (d[2] * d[2] + 1.0))
        inverse = lax.rsqrt(squared)
        second = inverse * inverse
        g3 = second * inverse
        g5 = g3 * second
        high = g5.astype(BF16)
        low = (g5 - high.astype(F32)).astype(BF16)
        matrix[t, 0:LANES, :] = high
        matrix[t, LANES:, :] = low
        left = parts[row]
        both = jnp.concatenate([high, low], axis=0)
        product = jnp.dot(jnp.concatenate([left, left], axis=1), both, preferred_element_type=F32)
        at = pl.ds(pl.multiple_of(recv * width, 8), width)
        sums[at, :] += fold(product)
        high = g3.astype(BF16)
        low = (g3 - high.astype(F32)).astype(BF16)
        left = parts_q[row]
        both = jnp.concatenate([high, low], axis=0)
        product = jnp.dot(jnp.concatenate([left, left], axis=1), both, preferred_element_type=F32)
        at = pl.ds(pl.multiple_of(recv * qwidth, 8), qwidth)
        sums_q[at, :] += product[0:qwidth] + product[qwidth : 2 * qwidth] + product[2 * qwidth : 3 * qwidth]
        at = pl.ds(recv, 1)
        selves[at, :] += jnp.where(same, 1.0, 0.0).astype(F32)
        return carry

    lax.fori_loop(0, tile_num, one, None, unroll=2)

    x = [place[k] for k in range(3)]
    fields = combine(sums, x, [multi[2 + k] for k in range(6)], selves[...])
    for s in range(STATES):
        def col(c):
            return sums_q[pl.ds(s * QCOLS + c, clusters, stride=qwidth), :]

        whole = col(0)
        for b in range(3):
            value = fields[3 * s + b] + (x[b] * whole - col(1 + b))
            induced[3 * s + b] = response[s] * value
    send_border(induced, outgoing, border_ids)


def send_border(vector, outgoing, border_ids):
    for b in range(outgoing.shape[1]):
        row = pl.ds(border_ids[b], 1)
        for k in range(vector.shape[0]):
            outgoing[k, pl.ds(b, 1), :] = vector[k, row, :]


def field_of(where, tiles, count, y, selves, matrix, own, halo, scratch, border):
    sources, flat, parts, sums = scratch
    clusters = own.shape[1]
    padded = y.shape[1]
    width = STATES * COLS
    for k in range(6):
        sources[k, 0:clusters, :] = own[k]
        sources[k, clusters:, :] = jnp.zeros((padded - clusters, LANES), F32)
    for slot in range(27):
        if slot == 13:
            continue
        ref, index = where[slot]
        base = clusters + slot * border
        for k in range(6):
            sources[k, base : base + border, :] = halo[ref][index + (k,)]
    write_columns(flat, y, sources, padded)
    split_columns(flat, parts, padded)
    sums[...] = jnp.zeros_like(sums)

    def one(t, carry):
        recv = tiles[0, t]
        row = tile_row(tiles, count, clusters, border, t)
        left = parts[row]
        product = jnp.dot(
            jnp.concatenate([left, left], axis=1), matrix[t], preferred_element_type=F32
        )
        at = pl.ds(pl.multiple_of(recv * width, 8), width)
        sums[at, :] += fold(product)
        return carry

    lax.fori_loop(0, tiles.shape[1], one, None, unroll=4)
    x = [y[k, 0:clusters, :] for k in range(3)]
    return combine(sums, x, [own[k] for k in range(6)], selves[...])


def step_kernel(where, parts_of, *refs):
    tiles, count, border_ids, response, y, selves, matrix, own = refs[:8]
    halo = refs[8 : 8 + parts_of]
    plain, scaled, outgoing = refs[8 + parts_of : 11 + parts_of]
    scratch = refs[11 + parts_of :]
    border = outgoing.shape[1]
    fields = field_of(where, tiles, count, y, selves, matrix, own, halo, scratch, border)
    for k in range(6):
        plain[k] = fields[k]
        scaled[k] = response[k // 3] * fields[k]
    send_border(scaled, outgoing, border_ids)


def last_kernel(where, parts_of, border, *refs):
    tiles, count, response, y, selves, matrix = refs[:6]
    plains = refs[6 : 6 + ITERS]
    scaleds = refs[6 + ITERS : 6 + 2 * ITERS]
    base = 6 + 2 * ITERS
    halo = refs[base : base + parts_of]
    gram = refs[base + parts_of]
    scratch = refs[base + parts_of + 1 :]
    own = scaleds[-1]
    fields = field_of(where, tiles, count, y, selves, matrix, own, halo, scratch, border)
    lane = lax.broadcasted_iota(jnp.int32, (1, LANES), 1)
    total = jnp.zeros((1, LANES), F32)
    for s in range(STATES):
        for e, (a, b) in enumerate(GRAM):
            sum_of = None
            for k in range(3 * s, 3 * s + 3):
                right = scaleds[b][k] if b < ITERS else response[s] * fields[k]
                term = plains[a][k] * right
                sum_of = term if sum_of is None else sum_of + term
            value = jnp.sum(jnp.sum(sum_of, axis=0, keepdims=True), axis=1, keepdims=True)
            total = jnp.where(lane == s * len(GRAM) + e, value, total)
    gram[...] = jnp.broadcast_to(total, gram.shape)


def coefficients(numbers):
    def entry(a, b):
        return numbers[(a, b) if a <= b else (b, a)]

    def form(left, right, moved):
        out = None
        for a, u in enumerate(left):
            for b, w in enumerate(right):
                term = u * w * entry(a, b + moved)
                out = term if out is None else out + term
        return out

    one = jnp.ones_like(numbers[(0, 0)])
    residual, direction = [one], [one]
    weights = [jnp.zeros_like(one)] * ITERS
    norm = form(residual, residual, 0)
    for sweep in range(ITERS):
        curve = form(direction, direction, 0) - form(direction, direction, 1)
        step = norm / curve
        weights = [
            w + step * direction[k] if k < len(direction) else w for k, w in enumerate(weights)
        ]
        if sweep + 1 == ITERS:
            break
        image = direction + [jnp.zeros_like(one)]
        image = [image[0]] + [image[k] - direction[k - 1] for k in range(1, len(image))]
        residual = [
            (residual[k] if k < len(residual) else 0.0) - step * image[k] for k in range(len(image))
        ]
        after = form(residual, residual, 0)
        ratio = after / norm
        direction = [
            residual[k] + ratio * direction[k] if k < len(direction) else residual[k]
            for k in range(len(residual))
        ]
        norm = after
    return weights


def finish_kernel(grams, induced, *refs):
    scaleds = refs[:ITERS]
    inverse, result = refs[ITERS : ITERS + 2]
    total = jnp.sum(grams[...], axis=0, keepdims=True)
    rows = []
    for s in range(STATES):
        numbers = {
            pair: total[:, s * len(GRAM) + e : s * len(GRAM) + e + 1]
            for e, pair in enumerate(GRAM)
        }
        weights = coefficients(numbers)
        for k in range(3 * s, 3 * s + 3):
            value = induced[k]
            for w, scaled in zip(weights, scaleds):
                value = value + w * scaled[k]
            rows.append(value)
    done = permuted(inverse[...], rows)
    for k in range(6):
        result[k] = done[k]


def ring(cells, axis):
    count = lax.axis_size(axis)
    if count == 1:
        return [cells], (0, 0, 0)
    below = lax.ppermute(cells, axis, [(i, (i + 1) % count) for i in range(count)])
    if count == 2:
        return [cells, below], (1, 0, 1)
    above = lax.ppermute(cells, axis, [((i + 1) % count, i) for i in range(count)])
    return [below, cells, above], (0, 1, 2)


def neighbours(cells):
    first, place_x = ring(cells, "gx")
    stacked = jnp.stack(first)
    second, place_y = ring(stacked, "gy")
    stacked = jnp.stack(second)
    third, place_z = ring(stacked, "gz")
    where = tuple(
        (place_z[n % 3], (place_y[n // 3 % 3], place_x[n // 9])) for n in range(27)
    )
    return third, where


def shards(coords, charges, dipoles, polar, perturbed, cluster_order, border_clusters,
           tile_list, tile_count):
    atoms = coords.shape[-1]
    clusters = atoms // LANES
    border = border_clusters.shape[-1]
    tile_num = tile_list.shape[-1]
    padded = -(-(clusters + 27 * border) // 8) * 8
    width = STATES * COLS
    qwidth = STATES * QCOLS

    def rows(array, kinds):
        return array.reshape(kinds, clusters, LANES)

    order = cluster_order.reshape(clusters, LANES)
    border_ids = border_clusters.reshape(border)
    tiles = tile_list.reshape(3, tile_num)
    count = tile_count.reshape(1)

    cell = (clusters, LANES)
    place, multi, response, outgoing = call(
        prepare_kernel,
        [((3,) + cell, F32), ((8,) + cell, F32), ((2,) + cell, F32), ((11, border, LANES), F32)],
        [VMEM] * 6 + [SMEM],
    )(rows(coords, 3), rows(charges, 2), rows(dipoles, 6), rows(polar, 2),
      perturbed.reshape(cell), order, border_ids)
    (inverse,) = call(inverse_kernel, [(cell, jnp.int32)], [VMEM])(order)

    halo, where = neighbours(outgoing)
    matrix_shape = (tile_num, 2 * LANES, LANES)
    flat = pltpu.VMEM((padded * width, LANES), F32)
    parts = pltpu.VMEM((padded, 3 * width, LANES), BF16)
    sums = pltpu.VMEM((clusters * width, LANES), F32)
    sources = pltpu.VMEM((6, padded, LANES), F32)
    induced, leaving, matrix, y, selves = call(
        lambda *refs: build_kernel(where, len(halo), *refs),
        [((6,) + cell, F32), ((6, border, LANES), F32), (matrix_shape, BF16),
         ((3, padded, LANES), F32), (cell, F32)],
        [SMEM] * 3 + [VMEM] * (3 + len(halo)),
        [pltpu.VMEM((8, padded, LANES), F32), flat, pltpu.VMEM((padded * qwidth, LANES), F32),
         parts, pltpu.VMEM((padded, 4 * qwidth, LANES), BF16),
         pltpu.VMEM((3, LANES, padded), F32), sums, pltpu.VMEM((clusters * qwidth, LANES), F32)],
    )(tiles, count, border_ids, place, multi, response, *halo)

    own = induced
    plains, scaleds = [], []
    for _ in range(ITERS):
        halo, where = neighbours(leaving)
        plain, own, leaving = call(
            lambda *refs, where=where: step_kernel(where, len(halo), *refs),
            [((6,) + cell, F32), ((6,) + cell, F32), ((6, border, LANES), F32)],
            [SMEM] * 3 + [VMEM] * (5 + len(halo)),
            [sources, flat, parts, sums],
        )(tiles, count, border_ids, response, y, selves, matrix, own, *halo)
        plains.append(plain)
        scaleds.append(own)
    halo, where = neighbours(leaving)
    (gram,) = call(
        lambda *refs: last_kernel(where, len(halo), border, *refs),
        [((8, LANES), F32)],
        [SMEM] * 2 + [VMEM] * (4 + 2 * ITERS + len(halo)),
        [sources, flat, parts, sums],
    )(tiles, count, response, y, selves, matrix, *plains, *scaleds, *halo)

    devices = 1
    for axis in AXES:
        devices *= lax.axis_size(axis)
    sent = jnp.broadcast_to(gram[:1], (devices, LANES))
    grams = lax.all_to_all(sent, AXES, 0, 0, tiled=True)
    (result,) = call(
        finish_kernel, [((6,) + cell, F32)], [VMEM] * (3 + ITERS)
    )(grams, induced, *scaleds, inverse)
    return result.reshape(6, 1, 1, 1, atoms)


def solution(mesh):
    wide = P(None, "gx", "gy", "gz", None)
    brick = P("gx", "gy", "gz", None)
    placed = (wide, wide, wide, wide, brick, brick, brick, wide, P("gx", "gy", "gz"))
    return jax.shard_map(
        shards, mesh=mesh, in_specs=placed, out_specs=wide, check_vma=False
    )
```

time: 661 us -> 182 us (0.28)
  other arithmetic: 222 us -> 3.73 us
  local copies, waits for them, and re-layouts: 187 us -> 6.33 us
  blocking collectives: 119 us -> 0 us
  Pallas kernels: 0 us -> 89.5 us
  waiting for transfers between devices: 77.9 us -> 47.2 us
  loops' own time: 11.6 us -> 0 us
  starting transfers between devices: 40.4 us -> 33.5 us
    reduce_sum x170 -> x0, other arithmetic: 169 us -> none  [the longest x80 127 us: one_block(): jnp.sum(radial[None] * separation - moment * third_power[None], axis=3)]
    gather x249 -> x0, local copies, waits for them, and re-layouts: 158 us -> none  [the longest x80 46 us: one_block(): jnp.take(source_places, block_row, axis=1) + block_shift.T[:, :, None]]
    psum x3 -> x0, blocking collectives: 119 us -> none  [joint_sums(): lax.psum((state_sums(first_vec), state_sums(second_vec), state_sums(third...]
    pallas_call x0 -> x8, Pallas kernels: none -> 89.5 us  [the longest x3 38.5 us: shards(): call(lambda *refs, where=where: step_kernel(where, len(halo), *refs), [((...]
    ppermute x30 -> x25, waiting for transfers between devices: 77.9 us -> 44 us  [the longest x15 33.3 us: ring(): lax.ppermute(cells, axis, [(i, (i + 1) % count) for i in range(count)])]
    mul x72 -> x0, other arithmetic: 19.7 us -> none  [the longest x64 19.3 us: one_block(): radial = 3.0 * projection * fifth_power]
    select_n x181 -> x0, other arithmetic: 13 us -> none  [the longest x96 6.16 us: one_block(): values = jnp.take(source_data, block_row, axis=1)]
    add x100 -> x0, other arithmetic: 12.7 us -> none  [the longest x80 6.57 us: one_block(): jnp.take(source_places, block_row, axis=1) + block_shift.T[:, :, None]]
  transfers between devices with their start and end apart: 30 -> 26, of which waited for: 26 -> 26; matrix products, arithmetic and copies ran while one was open for 1% -> 1% of each run, Pallas kernels for 0% -> 2%
where the time goes in v1:
time: 182 us; the launch traced here: 181 us
  Pallas kernels  89.5 us (49%)
  waiting for transfers between devices  47.2 us (26%)
  starting transfers between devices  33.5 us (18%)
  local copies, waits for them, and re-layouts  6.33 us (3%)
  other arithmetic  3.73 us (2%)
    pallas_call x3, Pallas kernels, shards(): call(lambda *refs, where=where: step_kernel(where, len(halo), *refs), [((...  38.5 us
    ppermute x15, waiting for transfers between devices, ring(): lax.ppermute(cells, axis, [(i, (i + 1) % count) for i in range(count)])  33.3 us
    pallas_call x1, Pallas kernels, shards(): call(lambda *refs: build_kernel(where, len(halo), *refs), [((6,) + cell,...  30.2 us
    ppermute x15, starting transfers between devices, ring(): lax.ppermute(cells, axis, [(i, (i + 1) % count) for i in range(count)])  16 us
    ppermute x10, starting transfers between devices, ring(): lax.ppermute(cells, axis, [((i + 1) % count, i) for i in range(count)])  13.9 us
    pallas_call x1, Pallas kernels, shards(): call(lambda *refs: last_kernel(where, len(halo), border, *refs), [((8, LA...  12.9 us
    ppermute x10, waiting for transfers between devices, ring(): lax.ppermute(cells, axis, [((i + 1) % count, i) for i in range(count)])  10.7 us
    unnamed x33, local copies, waits for them, and re-layouts  5.03 us
  transfers between devices with their start and end apart: 26, of which 26 were waited for; matrix products, arithmetic and copies ran while one was open for 1% of the time, Pallas kernels for 2%

profile of v1, /device:TPU:0, one launch (start us, length us, event | category | flops | bytes accessed | tf_op | source)
XLA Modules:
  0.0 181.1 jit_solution(18201921279322670075)
XLA Ops:
  0.0 2.0 %shard_map.91 = (f32[3,16,128]{2,1,0:T(8,128)}, f32[8,16,128]{2,1,0:T(8,128)}, f32[2,16,128]{2,1,0:T(8,128)}, f32[11,4,128]{2,1,0:T(4,128)}) custom-call(f32[3,16,128]{2,1,0:T(8,128)} %bitcast.64, f32[2,16,128]{2,1,0:T(8,128)} %bitcast.68, f32[6,16,128]{2,1,0:T(8,128)} %bitcast.57, f32[2,16,128]{2,1,0:T(8,128)} %bitcast.69, s32[16,128]{1,0:T(8,128)} %bitcast.87, ...), custom_call_target="tpu_custom_call" | custom-call | tf_op jit(solution)/shard_map/pallas_call | solution.py:463
  2.0 5.1 %collective-permute-start.1 = (f32[11,4,128]{2,1,0:T(4,128)}, f32[11,4,128]{2,1,0:T(4,128)S(1)}, u32[]{:S(2)}, u32[]{:S(2)}) collective-permute-start(f32[11,4,128]{2,1,0:T(4,128)} %get-tuple-element.26), channel_id=1, source_target_pairs={{8,0},{16,8},{24,16},{0,24},{9,1},{17,9},{25,17},{1,25},{10,2},{18... | collective-permute-start | bytes 67592 | tf_op jit(solution)/shard_map/ppermute | solution.py:428
  7.1 1.7 collective-permute-done.1
  8.8 4.1 %collective-permute-done = f32[11,4,128]{2,1,0:T(4,128)S(1)} collective-permute-done((f32[11,4,128]{2,1,0:T(4,128)}, f32[11,4,128]{2,1,0:T(4,128)S(1)}, u32[]{:S(2)}, u32[]{:S(2)}) %collective-permute-start) | collective-permute-done | bytes 22560 | tf_op jit(solution)/shard_map/ppermute | solution.py:425
  12.9 0.8 fusion.4
  13.7 1.6 collective-permute-start.2
  15.2 2.8 %collective-permute-done.2 = f32[3,11,4,128]{3,2,1,0:T(4,128)S(1)} collective-permute-done((f32[3,11,4,128]{3,2,1,0:T(4,128)S(1)}, f32[3,11,4,128]{3,2,1,0:T(4,128)S(1)}, u32[]{:S(2)}, u32[]{:S(2)}) %collective-permute-start.2) | collective-permute-done | bytes 67616 | tf_op jit(solution)/shard_map/ppermute | solution.py:425
  18.1 1.7 collective-permute-start.4
  19.9 1.3 copy.15
  21.8 0.8 collective-permute-done.3.refs_6_
  22.6 0.5 collective-permute-done.4.refs_8_
  23.2 0.5 copy-done.6
  23.7 30.2 %shard_map.92 = (f32[6,16,128]{2,1,0:T(8,128)}, f32[6,4,128]{2,1,0:T(4,128)}, bf16[128,256,128]{2,1,0:T(8,128)(2,1)}, f32[3,128,128]{2,1,0:T(8,128)}, f32[16,128]{1,0:T(8,128)}) custom-call(s32[3,128]{1,0:T(4,128)} %bitcast.50, s32[1]{0:T(128)} %bitcast.45.refs_1_, s32[4]{0:T(128)} %bitcast.71, f32[3,16,128]{2,1,0:T(8,128)} %get-tuple-element.24.refs_3_, ...), custom_call_target="tpu_custom_call" | custom-call | tf_op jit(solution)/shard_map/pallas_call | solution.py:477
  53.9 2.0 %collective-permute-start.5 = (f32[6,4,128]{2,1,0:T(4,128)}, f32[6,4,128]{2,1,0:T(4,128)S(1)}, u32[]{:S(2)}, u32[]{:S(2)}) collective-permute-start(f32[6,4,128]{2,1,0:T(4,128)} %get-tuple-element.31), channel_id=1, source_target_pairs={{0,8},{8,16},{16,24},{24,0},{1,9},{9,17},{17,25},{25,1},{2,10},{10... | collective-permute-start | bytes 36872 | tf_op jit(solution)/shard_map/ppermute | solution.py:425
  55.9 1.9 %collective-permute-done.6 = f32[6,4,128]{2,1,0:T(4,128)S(1)} collective-permute-done((f32[6,4,128]{2,1,0:T(4,128)}, f32[6,4,128]{2,1,0:T(4,128)S(1)}, u32[]{:S(2)}, u32[]{:S(2)}) %collective-permute-start.6) | collective-permute-done | bytes 12320 | tf_op jit(solution)/shard_map/ppermute | solution.py:428
  57.8 1.9 %collective-permute-done.5 = f32[6,4,128]{2,1,0:T(4,128)S(1)} collective-permute-done((f32[6,4,128]{2,1,0:T(4,128)}, f32[6,4,128]{2,1,0:T(4,128)S(1)}, u32[]{:S(2)}, u32[]{:S(2)}) %collective-permute-start.5) | collective-permute-done | bytes 12320 | tf_op jit(solution)/shard_map/ppermute | solution.py:425
  59.6 0.7 fusion.3
  60.4 1.6 collective-permute-start.7
  61.9 2.4 %collective-permute-done.7 = f32[3,6,4,128]{3,2,1,0:T(4,128)S(1)} collective-permute-done((f32[3,6,4,128]{3,2,1,0:T(4,128)S(1)}, f32[3,6,4,128]{3,2,1,0:T(4,128)S(1)}, u32[]{:S(2)}, u32[]{:S(2)}) %collective-permute-start.7) | collective-permute-done | bytes 36896 | tf_op jit(solution)/shard_map/ppermute | solution.py:425
  64.5 1.7 collective-permute-start.9
  66.2 2.0 %collective-permute-done.8.refs_8_ = f32[2,3,6,4,128]{4,3,2,1,0:T(4,128)S(1)} collective-permute-done((f32[2,3,6,4,128]{4,3,2,1,0:T(4,128)S(1)}, f32[2,3,6,4,128]{4,3,2,1,0:T(4,128)S(1)}, u32[]{:S(2)}, u32[]{:S(2)}) %collective-permute-start.8) | collective-permute-done | bytes 73760 | tf_op jit(solution)/shard_map/ppermute | solution.py:425
  68.3 0.6 copy-done.9
  68.9 12.8 %shard_map.93 = (f32[6,16,128]{2,1,0:T(8,128)}, f32[6,16,128]{2,1,0:T(8,128)}, f32[6,4,128]{2,1,0:T(4,128)}) custom-call(s32[3,128]{1,0:T(4,128)} %bitcast.51, s32[1]{0:T(128)} %bitcast.46.refs_1_, s32[4]{0:T(128)} %bitcast.72, f32[2,16,128]{2,1,0:T(8,128)} %get-tuple-element.23.refs_5_.refs_3_.refs_2_, f32[3,128,128]{2,1,0:T(8,128)} %get-tuple-element.27.refs_4_.refs_3_, ...), custom_call_target="tpu_custom_call" | custom-call | tf_op jit(solution)/shard_map/pallas_call | solution.py:491
  81.7 2.0 %collective-permute-start.10 = (f32[6,4,128]{2,1,0:T(4,128)}, f32[6,4,128]{2,1,0:T(4,128)S(1)}, u32[]{:S(2)}, u32[]{:S(2)}) collective-permute-start(f32[6,4,128]{2,1,0:T(4,128)} %get-tuple-element.34), channel_id=1, source_target_pairs={{0,8},{8,16},{16,24},{24,0},{1,9},{9,17},{17,25},{25,1},{2,10},{10... | collective-permute-start | bytes 36872 | tf_op jit(solution)/shard_map/ppermute | solution.py:425
  83.8 1.9 %collective-permute-done.11 = f32[6,4,128]{2,1,0:T(4,128)S(1)} collective-permute-done((f32[6,4,128]{2,1,0:T(4,128)}, f32[6,4,128]{2,1,0:T(4,128)S(1)}, u32[]{:S(2)}, u32[]{:S(2)}) %collective-permute-start.11) | collective-permute-done | bytes 12320 | tf_op jit(solution)/shard_map/ppermute | solution.py:428
  85.7 1.8 %collective-permute-done.10 = f32[6,4,128]{2,1,0:T(4,128)S(1)} collective-permute-done((f32[6,4,128]{2,1,0:T(4,128)}, f32[6,4,128]{2,1,0:T(4,128)S(1)}, u32[]{:S(2)}, u32[]{:S(2)}) %collective-permute-start.10) | collective-permute-done | bytes 12320 | tf_op jit(solution)/shard_map/ppermute | solution.py:425
  87.5 0.7 fusion.2
  88.2 1.6 collective-permute-start.12
  89.8 2.5 %collective-permute-done.12 = f32[3,6,4,128]{3,2,1,0:T(4,128)S(1)} collective-permute-done((f32[3,6,4,128]{3,2,1,0:T(4,128)S(1)}, f32[3,6,4,128]{3,2,1,0:T(4,128)S(1)}, u32[]{:S(2)}, u32[]{:S(2)}) %collective-permute-start.12) | collective-permute-done | bytes 36896 | tf_op jit(solution)/shard_map/ppermute | solution.py:425
  92.4 1.7 collective-permute-start.14
  94.2 2.0 %collective-permute-done.13.refs_8_ = f32[2,3,6,4,128]{4,3,2,1,0:T(4,128)S(1)} collective-permute-done((f32[2,3,6,4,128]{4,3,2,1,0:T(4,128)S(1)}, f32[2,3,6,4,128]{4,3,2,1,0:T(4,128)S(1)}, u32[]{:S(2)}, u32[]{:S(2)}) %collective-permute-start.13) | collective-permute-done | bytes 73760 | tf_op jit(solution)/shard_map/ppermute | solution.py:425
  96.4 0.4 copy-done.10
  96.8 0.2 copy-done.13
  97.0 12.8 %shard_map.94 = (f32[6,16,128]{2,1,0:T(8,128)}, f32[6,16,128]{2,1,0:T(8,128)}, f32[6,4,128]{2,1,0:T(4,128)}) custom-call(s32[3,128]{1,0:T(4,128)} %bitcast.52, s32[1]{0:T(128)} %bitcast.47.refs_1_, s32[4]{0:T(128)} %bitcast.73, f32[2,16,128]{2,1,0:T(8,128)} %get-tuple-element.23.refs_5_.refs_3_.refs_2_, f32[3,128,128]{2,1,0:T(8,128)} %get-tuple-element.27.refs_4_.refs_3_, ...), custom_call_target="tpu_custom_call" | custom-call | tf_op jit(solution)/shard_map/pallas_call | solution.py:491
  109.9 1.9 %collective-permute-start.15 = (f32[6,4,128]{2,1,0:T(4,128)}, f32[6,4,128]{2,1,0:T(4,128)S(1)}, u32[]{:S(2)}, u32[]{:S(2)}) collective-permute-start(f32[6,4,128]{2,1,0:T(4,128)} %get-tuple-element.37), channel_id=1, source_target_pairs={{0,8},{8,16},{16,24},{24,0},{1,9},{9,17},{17,25},{25,1},{2,10},{10... | collective-permute-start | bytes 36872 | tf_op jit(solution)/shard_map/ppermute | solution.py:425
  111.9 1.9 %collective-permute-done.16 = f32[6,4,128]{2,1,0:T(4,128)S(1)} collective-permute-done((f32[6,4,128]{2,1,0:T(4,128)}, f32[6,4,128]{2,1,0:T(4,128)S(1)}, u32[]{:S(2)}, u32[]{:S(2)}) %collective-permute-start.16) | collective-permute-done | bytes 12320 | tf_op jit(solution)/shard_map/ppermute | solution.py:428
  113.7 1.9 %collective-permute-done.15 = f32[6,4,128]{2,1,0:T(4,128)S(1)} collective-permute-done((f32[6,4,128]{2,1,0:T(4,128)}, f32[6,4,128]{2,1,0:T(4,128)S(1)}, u32[]{:S(2)}, u32[]{:S(2)}) %collective-permute-start.15) | collective-permute-done | bytes 12320 | tf_op jit(solution)/shard_map/ppermute | solution.py:425
  115.7 0.7 fusion.1
  116.4 1.5 collective-permute-start.17
  117.9 2.5 %collective-permute-done.17 = f32[3,6,4,128]{3,2,1,0:T(4,128)S(1)} collective-permute-done((f32[3,6,4,128]{3,2,1,0:T(4,128)S(1)}, f32[3,6,4,128]{3,2,1,0:T(4,128)S(1)}, u32[]{:S(2)}, u32[]{:S(2)}) %collective-permute-start.17) | collective-permute-done | bytes 36896 | tf_op jit(solution)/shard_map/ppermute | solution.py:425
  120.5 1.7 collective-permute-start.19
  122.2 2.0 %collective-permute-done.18.refs_8_ = f32[2,3,6,4,128]{4,3,2,1,0:T(4,128)S(1)} collective-permute-done((f32[2,3,6,4,128]{4,3,2,1,0:T(4,128)S(1)}, f32[2,3,6,4,128]{4,3,2,1,0:T(4,128)S(1)}, u32[]{:S(2)}, u32[]{:S(2)}) %collective-permute-start.18) | collective-permute-done | bytes 73760 | tf_op jit(solution)/shard_map/ppermute | solution.py:425
  124.3 0.3 collective-permute-done.19.refs_10_
  124.6 0.3 copy-done.11
  124.9 0.3 copy-done.14
  125.2 12.8 %shard_map.95 = (f32[6,16,128]{2,1,0:T(8,128)}, f32[6,16,128]{2,1,0:T(8,128)}, f32[6,4,128]{2,1,0:T(4,128)}) custom-call(s32[3,128]{1,0:T(4,128)} %bitcast.53, s32[1]{0:T(128)} %bitcast.48.refs_1_, s32[4]{0:T(128)} %bitcast.74, f32[2,16,128]{2,1,0:T(8,128)} %get-tuple-element.23.refs_5_.refs_3_.refs_2_, f32[3,128,128]{2,1,0:T(8,128)} %get-tuple-element.27.refs_4_.refs_3_, ...), custom_call_target="tpu_custom_call" | custom-call | tf_op jit(solution)/shard_map/pallas_call | solution.py:491
  138.0 2.0 %collective-permute-start.20 = (f32[6,4,128]{2,1,0:T(4,128)}, f32[6,4,128]{2,1,0:T(4,128)S(1)}, u32[]{:S(2)}, u32[]{:S(2)}) collective-permute-start(f32[6,4,128]{2,1,0:T(4,128)} %get-tuple-element.40), channel_id=1, source_target_pairs={{0,8},{8,16},{16,24},{24,0},{1,9},{9,17},{17,25},{25,1},{2,10},{10... | collective-permute-start | bytes 36872 | tf_op jit(solution)/shard_map/ppermute | solution.py:425
  140.0 1.9 %collective-permute-done.21 = f32[6,4,128]{2,1,0:T(4,128)S(1)} collective-permute-done((f32[6,4,128]{2,1,0:T(4,128)}, f32[6,4,128]{2,1,0:T(4,128)S(1)}, u32[]{:S(2)}, u32[]{:S(2)}) %collective-permute-start.21) | collective-permute-done | bytes 12320 | tf_op jit(solution)/shard_map/ppermute | solution.py:428
  141.9 1.8 %collective-permute-done.20 = f32[6,4,128]{2,1,0:T(4,128)S(1)} collective-permute-done((f32[6,4,128]{2,1,0:T(4,128)}, f32[6,4,128]{2,1,0:T(4,128)S(1)}, u32[]{:S(2)}, u32[]{:S(2)}) %collective-permute-start.20) | collective-permute-done | bytes 12320 | tf_op jit(solution)/shard_map/ppermute | solution.py:425
  143.8 0.7 fusion
  144.5 1.5 collective-permute-start.22
  146.0 2.6 %collective-permute-done.22 = f32[3,6,4,128]{3,2,1,0:T(4,128)S(1)} collective-permute-done((f32[3,6,4,128]{3,2,1,0:T(4,128)S(1)}, f32[3,6,4,128]{3,2,1,0:T(4,128)S(1)}, u32[]{:S(2)}, u32[]{:S(2)}) %collective-permute-start.22) | collective-permute-done | bytes 36896 | tf_op jit(solution)/shard_map/ppermute | solution.py:425
  148.7 1.7 collective-permute-start.24
  150.4 2.0 %collective-permute-done.23.refs_12_ = f32[2,3,6,4,128]{4,3,2,1,0:T(4,128)S(1)} collective-permute-done((f32[2,3,6,4,128]{4,3,2,1,0:T(4,128)S(1)}, f32[2,3,6,4,128]{4,3,2,1,0:T(4,128)S(1)}, u32[]{:S(2)}, u32[]{:S(2)}) %collective-permute-start.23) | collective-permute-done | bytes 73760 | tf_op jit(solution)/shard_map/ppermute | solution.py:425
  152.5 0.4 collective-permute-done.24.refs_14_
  153.1 0.4 copy-done.8
  153.5 12.9 %shard_map.96 = f32[8,128]{1,0:T(8,128)} custom-call(s32[3,128]{1,0:T(4,128)} %bitcast.54, s32[1]{0:T(128)} %bitcast.49.refs_1_, f32[2,16,128]{2,1,0:T(8,128)} %get-tuple-element.23.refs_5_.refs_3_.refs_2_, f32[3,128,128]{2,1,0:T(8,128)} %get-tuple-element.27.refs_4_.refs_3_, f32[16,128]{1,0:T(8,128)} %get-tuple-element.28.refs_5_.refs_4_, ...), custom_call_target="tpu_custom_call" | custom-call | tf_op jit(solution)/shard_map/pallas_call | solution.py:500
  166.4 0.7 slice_bitcast_fusion
  167.1 0.6 broadcast_in_dim.2
  167.7 3.7 %all-to-all-start = ((f32[32,1,128]{2,1,0:T(1,128)}), f32[32,1,128]{2,1,0:T(1,128)S(1)}, u32[]{:S(2)}, u32[]{:S(2)}) async-start(f32[32,1,128]{2,1,0:T(1,128)} %broadcast_in_dim.2), calls=%async_computation | async-start | bytes 32768 | tf_op jit(solution)/shard_map/all_to_all | solution.py:511
  171.4 3.8 %shard_map.97.refs_3_ = s32[16,128]{1,0:T(8,128)} custom-call(s32[16,128]{1,0:T(8,128)} %bitcast.63), custom_call_target="tpu_custom_call" | custom-call | tf_op jit(solution)/shard_map/pallas_call | solution.py:469
  175.2 3.2 %all-to-all-done = f32[32,1,128]{2,1,0:T(1,128)S(1)} async-done(((f32[32,1,128]{2,1,0:T(1,128)}), f32[32,1,128]{2,1,0:T(1,128)S(1)}, u32[]{:S(2)}, u32[]{:S(2)}) %all-to-all-start) | async-done | bytes 16416 | tf_op jit(solution)/shard_map/all_to_all | solution.py:511
  178.3 0.6 copy-done.15
  178.9 2.2 %shard_map.98 = f32[6,16,128]{2,1,0:T(8,128)} custom-call(f32[32,128]{1,0:T(8,128)} %bitcast.56, f32[6,16,128]{2,1,0:T(8,128)} %get-tuple-element.30.refs_7_.induced, f32[6,16,128]{2,1,0:T(8,128)} %get-tuple-element.33.refs_7_.refs_9_.refs_0_, f32[6,16,128]{2,1,0:T(8,128)} %get-tuple-element.36.refs_7_.refs_10_.refs_1_, ...), custom_call_target="tpu_custom_call" | custom-call | tf_op jit(solution)/shard_map/pallas_call | solution.py:512
  (41 shorter events, 1.2 us)
Async XLA Ops:
  2.0 6.8 %collective-permute-start.1 = (f32[11,4,128]{2,1,0:T(4,128)}, f32[11,4,128]{2,1,0:T(4,128)S(1)}, u32[]{:S(2)}, u32[]{:S(2)}) collective-permute-start(f32[11,4,128]{2,1,0:T(4,128)} %get-tuple-element.26), channel_id=1, source_target_pairs={{8,0},{16,8},{24,16},{0,24},{9,1},{17,9},{25,17},{1,25},{10,2},{18... | collective-permute-start | bytes 67592 | tf_op jit(solution)/shard_map/ppermute | solution.py:428
  7.1 5.8 %collective-permute-start = (f32[11,4,128]{2,1,0:T(4,128)}, f32[11,4,128]{2,1,0:T(4,128)S(1)}, u32[]{:S(2)}, u32[]{:S(2)}) collective-permute-start(f32[11,4,128]{2,1,0:T(4,128)} %get-tuple-element.26), channel_id=1, source_target_pairs={{0,8},{8,16},{16,24},{24,0},{1,9},{9,17},{17,25},{25,1},{2,10},{10... | collective-permute-start | bytes 67592 | tf_op jit(solution)/shard_map/ppermute | solution.py:425
  13.7 4.4 %collective-permute-start.2 = (f32[3,11,4,128]{3,2,1,0:T(4,128)S(1)}, f32[3,11,4,128]{3,2,1,0:T(4,128)S(1)}, u32[]{:S(2)}, u32[]{:S(2)}) collective-permute-start(f32[3,11,4,128]{3,2,1,0:T(4,128)S(1)} %get-tuple-element.42), channel_id=1, source_target_pairs={{0,4},{4,0},{1,5},{5,1},{2,6},{6,2},{3,7},{7,3},{8,12},{12,8},{9,1... | collective-permute-start | bytes 202760 | tf_op jit(solution)/shard_map/ppermute | solution.py:425
  18.1 5.0 %copy-start = (f32[2,3,11,4,128]{4,3,2,1,0:T(4,128)}, f32[2,3,11,4,128]{4,3,2,1,0:T(4,128)S(1)}, u32[]{:S(2)}) copy-start(f32[2,3,11,4,128]{4,3,2,1,0:T(4,128)S(1)} %pad_maximum_fusion.refs_7_) | copy-start | bytes 405508
  18.1 4.5 %collective-permute-start.3 = (f32[2,3,11,4,128]{4,3,2,1,0:T(4,128)S(1)}, f32[2,3,11,4,128]{4,3,2,1,0:T(4,128)S(1)}, u32[]{:S(2)}, u32[]{:S(2)}) collective-permute-start(f32[2,3,11,4,128]{4,3,2,1,0:T(4,128)S(1)} %pad_maximum_fusion.refs_7_), channel_id=1, source_target_pairs={{0,1},{1,2},{2,3},{3,0},{4,5},{5,6},{6,7},{7,4},{8,9},{9,10},{10,1... | collective-permute-start | bytes 405512 | tf_op jit(solution)/shard_map/ppermute | solution.py:425
  18.1 4.9 %collective-permute-start.4 = (f32[2,3,11,4,128]{4,3,2,1,0:T(4,128)S(1)}, f32[2,3,11,4,128]{4,3,2,1,0:T(4,128)S(1)}, u32[]{:S(2)}, u32[]{:S(2)}) collective-permute-start(f32[2,3,11,4,128]{4,3,2,1,0:T(4,128)S(1)} %pad_maximum_fusion.refs_7_), channel_id=1, source_target_pairs={{1,0},{2,1},{3,2},{0,3},{5,4},{6,5},{7,6},{4,7},{9,8},{10,9},{11,1... | collective-permute-start | bytes 405512 | tf_op jit(solution)/shard_map/ppermute | solution.py:428
  22.6 0.7 copy-start.5
  23.0 0.6 copy-start.6
  53.9 3.9 %collective-permute-start.6 = (f32[6,4,128]{2,1,0:T(4,128)}, f32[6,4,128]{2,1,0:T(4,128)S(1)}, u32[]{:S(2)}, u32[]{:S(2)}) collective-permute-start(f32[6,4,128]{2,1,0:T(4,128)} %get-tuple-element.31), channel_id=1, source_target_pairs={{8,0},{16,8},{24,16},{0,24},{9,1},{17,9},{25,17},{1,25},{10,2},{18... | collective-permute-start | bytes 36872 | tf_op jit(solution)/shard_map/ppermute | solution.py:428
  53.9 5.7 %collective-permute-start.5 = (f32[6,4,128]{2,1,0:T(4,128)}, f32[6,4,128]{2,1,0:T(4,128)S(1)}, u32[]{:S(2)}, u32[]{:S(2)}) collective-permute-start(f32[6,4,128]{2,1,0:T(4,128)} %get-tuple-element.31), channel_id=1, source_target_pairs={{0,8},{8,16},{16,24},{24,0},{1,9},{9,17},{17,25},{25,1},{2,10},{10... | collective-permute-start | bytes 36872 | tf_op jit(solution)/shard_map/ppermute | solution.py:425
  60.4 4.0 %collective-permute-start.7 = (f32[3,6,4,128]{3,2,1,0:T(4,128)S(1)}, f32[3,6,4,128]{3,2,1,0:T(4,128)S(1)}, u32[]{:S(2)}, u32[]{:S(2)}) collective-permute-start(f32[3,6,4,128]{3,2,1,0:T(4,128)S(1)} %get-tuple-element.50), channel_id=1, source_target_pairs={{0,4},{4,0},{1,5},{5,1},{2,6},{6,2},{3,7},{7,3},{8,12},{12,8},{9,1... | collective-permute-start | bytes 110600 | tf_op jit(solution)/shard_map/ppermute | solution.py:425
  64.4 3.9 %copy-start.2 = (f32[2,3,6,4,128]{4,3,2,1,0:T(4,128)}, f32[2,3,6,4,128]{4,3,2,1,0:T(4,128)S(1)}, u32[]{:S(2)}) copy-start(f32[2,3,6,4,128]{4,3,2,1,0:T(4,128)S(1)} %pad_maximum_fusion.1.refs_9_) | copy-start | bytes 221188
  64.4 3.8 %collective-permute-start.8 = (f32[2,3,6,4,128]{4,3,2,1,0:T(4,128)S(1)}, f32[2,3,6,4,128]{4,3,2,1,0:T(4,128)S(1)}, u32[]{:S(2)}, u32[]{:S(2)}) collective-permute-start(f32[2,3,6,4,128]{4,3,2,1,0:T(4,128)S(1)} %pad_maximum_fusion.1.refs_9_), channel_id=1, source_target_pairs={{0,1},{1,2},{2,3},{3,0},{4,5},{5,6},{6,7},{7,4},{8,9},{9,10},{10,1... | collective-permute-start | bytes 221192 | tf_op jit(solution)/shard_map/ppermute | solution.py:425
  64.5 3.8 %collective-permute-start.9 = (f32[2,3,6,4,128]{4,3,2,1,0:T(4,128)S(1)}, f32[2,3,6,4,128]{4,3,2,1,0:T(4,128)S(1)}, u32[]{:S(2)}, u32[]{:S(2)}) collective-permute-start(f32[2,3,6,4,128]{4,3,2,1,0:T(4,128)S(1)} %pad_maximum_fusion.1.refs_9_), channel_id=1, source_target_pairs={{1,0},{2,1},{3,2},{0,3},{5,4},{6,5},{7,6},{4,7},{9,8},{10,9},{11,1... | collective-permute-start | bytes 221192 | tf_op jit(solution)/shard_map/ppermute | solution.py:428
  68.2 0.6 copy-start.9
  68.3 0.6 copy-start.12
  81.7 3.9 %collective-permute-start.11 = (f32[6,4,128]{2,1,0:T(4,128)}, f32[6,4,128]{2,1,0:T(4,128)S(1)}, u32[]{:S(2)}, u32[]{:S(2)}) collective-permute-start(f32[6,4,128]{2,1,0:T(4,128)} %get-tuple-element.34), channel_id=1, source_target_pairs={{8,0},{16,8},{24,16},{0,24},{9,1},{17,9},{25,17},{1,25},{10,2},{18... | collective-permute-start | bytes 36872 | tf_op jit(solution)/shard_map/ppermute | solution.py:428
  81.7 5.7 %collective-permute-start.10 = (f32[6,4,128]{2,1,0:T(4,128)}, f32[6,4,128]{2,1,0:T(4,128)S(1)}, u32[]{:S(2)}, u32[]{:S(2)}) collective-permute-start(f32[6,4,128]{2,1,0:T(4,128)} %get-tuple-element.34), channel_id=1, source_target_pairs={{0,8},{8,16},{16,24},{24,0},{1,9},{9,17},{17,25},{25,1},{2,10},{10... | collective-permute-start | bytes 36872 | tf_op jit(solution)/shard_map/ppermute | solution.py:425
  88.2 4.1 %collective-permute-start.12 = (f32[3,6,4,128]{3,2,1,0:T(4,128)S(1)}, f32[3,6,4,128]{3,2,1,0:T(4,128)S(1)}, u32[]{:S(2)}, u32[]{:S(2)}) collective-permute-start(f32[3,6,4,128]{3,2,1,0:T(4,128)S(1)} %get-tuple-element.48), channel_id=1, source_target_pairs={{0,4},{4,0},{1,5},{5,1},{2,6},{6,2},{3,7},{7,3},{8,12},{12,8},{9,1... | collective-permute-start | bytes 110600 | tf_op jit(solution)/shard_map/ppermute | solution.py:425
  92.3 4.0 %copy-start.3 = (f32[2,3,6,4,128]{4,3,2,1,0:T(4,128)}, f32[2,3,6,4,128]{4,3,2,1,0:T(4,128)S(1)}, u32[]{:S(2)}) copy-start(f32[2,3,6,4,128]{4,3,2,1,0:T(4,128)S(1)} %pad_maximum_fusion.2.refs_9_) | copy-start | bytes 221188
  92.4 3.8 %collective-permute-start.13 = (f32[2,3,6,4,128]{4,3,2,1,0:T(4,128)S(1)}, f32[2,3,6,4,128]{4,3,2,1,0:T(4,128)S(1)}, u32[]{:S(2)}, u32[]{:S(2)}) collective-permute-start(f32[2,3,6,4,128]{4,3,2,1,0:T(4,128)S(1)} %pad_maximum_fusion.2.refs_9_), channel_id=1, source_target_pairs={{0,1},{1,2},{2,3},{3,0},{4,5},{5,6},{6,7},{7,4},{8,9},{9,10},{10,1... | collective-permute-start | bytes 221192 | tf_op jit(solution)/shard_map/ppermute | solution.py:425
  92.4 3.9 %collective-permute-start.14 = (f32[2,3,6,4,128]{4,3,2,1,0:T(4,128)S(1)}, f32[2,3,6,4,128]{4,3,2,1,0:T(4,128)S(1)}, u32[]{:S(2)}, u32[]{:S(2)}) collective-permute-start(f32[2,3,6,4,128]{4,3,2,1,0:T(4,128)S(1)} %pad_maximum_fusion.2.refs_9_), channel_id=1, source_target_pairs={{1,0},{2,1},{3,2},{0,3},{5,4},{6,5},{7,6},{4,7},{9,8},{10,9},{11,1... | collective-permute-start | bytes 221192 | tf_op jit(solution)/shard_map/ppermute | solution.py:428
  96.2 0.6 copy-start.10
  96.4 0.6 copy-start.13
  109.8 3.9 %collective-permute-start.16 = (f32[6,4,128]{2,1,0:T(4,128)}, f32[6,4,128]{2,1,0:T(4,128)S(1)}, u32[]{:S(2)}, u32[]{:S(2)}) collective-permute-start(f32[6,4,128]{2,1,0:T(4,128)} %get-tuple-element.37), channel_id=1, source_target_pairs={{8,0},{16,8},{24,16},{0,24},{9,1},{17,9},{25,17},{1,25},{10,2},{18... | collective-permute-start | bytes 36872 | tf_op jit(solution)/shard_map/ppermute | solution.py:428
  109.9 5.7 %collective-permute-start.15 = (f32[6,4,128]{2,1,0:T(4,128)}, f32[6,4,128]{2,1,0:T(4,128)S(1)}, u32[]{:S(2)}, u32[]{:S(2)}) collective-permute-start(f32[6,4,128]{2,1,0:T(4,128)} %get-tuple-element.37), channel_id=1, source_target_pairs={{0,8},{8,16},{16,24},{24,0},{1,9},{9,17},{17,25},{25,1},{2,10},{10... | collective-permute-start | bytes 36872 | tf_op jit(solution)/shard_map/ppermute | solution.py:425
  116.4 4.0 %collective-permute-start.17 = (f32[3,6,4,128]{3,2,1,0:T(4,128)S(1)}, f32[3,6,4,128]{3,2,1,0:T(4,128)S(1)}, u32[]{:S(2)}, u32[]{:S(2)}) collective-permute-start(f32[3,6,4,128]{3,2,1,0:T(4,128)S(1)} %get-tuple-element.46), channel_id=1, source_target_pairs={{0,4},{4,0},{1,5},{5,1},{2,6},{6,2},{3,7},{7,3},{8,12},{12,8},{9,1... | collective-permute-start | bytes 110600 | tf_op jit(solution)/shard_map/ppermute | solution.py:425
  120.4 4.2 %copy-start.4 = (f32[2,3,6,4,128]{4,3,2,1,0:T(4,128)}, f32[2,3,6,4,128]{4,3,2,1,0:T(4,128)S(1)}, u32[]{:S(2)}) copy-start(f32[2,3,6,4,128]{4,3,2,1,0:T(4,128)S(1)} %pad_maximum_fusion.3.refs_9_) | copy-start | bytes 221188
  120.4 3.8 %collective-permute-start.18 = (f32[2,3,6,4,128]{4,3,2,1,0:T(4,128)S(1)}, f32[2,3,6,4,128]{4,3,2,1,0:T(4,128)S(1)}, u32[]{:S(2)}, u32[]{:S(2)}) collective-permute-start(f32[2,3,6,4,128]{4,3,2,1,0:T(4,128)S(1)} %pad_maximum_fusion.3.refs_9_), channel_id=1, source_target_pairs={{0,1},{1,2},{2,3},{3,0},{4,5},{5,6},{6,7},{7,4},{8,9},{9,10},{10,1... | collective-permute-start | bytes 221192 | tf_op jit(solution)/shard_map/ppermute | solution.py:425
  120.5 4.1 %collective-permute-start.19 = (f32[2,3,6,4,128]{4,3,2,1,0:T(4,128)S(1)}, f32[2,3,6,4,128]{4,3,2,1,0:T(4,128)S(1)}, u32[]{:S(2)}, u32[]{:S(2)}) collective-permute-start(f32[2,3,6,4,128]{4,3,2,1,0:T(4,128)S(1)} %pad_maximum_fusion.3.refs_9_), channel_id=1, source_target_pairs={{1,0},{2,1},{3,2},{0,3},{5,4},{6,5},{7,6},{4,7},{9,8},{10,9},{11,1... | collective-permute-start | bytes 221192 | tf_op jit(solution)/shard_map/ppermute | solution.py:428
  124.3 0.6 copy-start.11
  124.6 0.6 copy-start.14
  138.0 3.9 %collective-permute-start.21 = (f32[6,4,128]{2,1,0:T(4,128)}, f32[6,4,128]{2,1,0:T(4,128)S(1)}, u32[]{:S(2)}, u32[]{:S(2)}) collective-permute-start(f32[6,4,128]{2,1,0:T(4,128)} %get-tuple-element.40), channel_id=1, source_target_pairs={{8,0},{16,8},{24,16},{0,24},{9,1},{17,9},{25,17},{1,25},{10,2},{18... | collective-permute-start | bytes 36872 | tf_op jit(solution)/shard_map/ppermute | solution.py:428
  138.0 5.7 %collective-permute-start.20 = (f32[6,4,128]{2,1,0:T(4,128)}, f32[6,4,128]{2,1,0:T(4,128)S(1)}, u32[]{:S(2)}, u32[]{:S(2)}) collective-permute-start(f32[6,4,128]{2,1,0:T(4,128)} %get-tuple-element.40), channel_id=1, source_target_pairs={{0,8},{8,16},{16,24},{24,0},{1,9},{9,17},{17,25},{25,1},{2,10},{10... | collective-permute-start | bytes 36872 | tf_op jit(solution)/shard_map/ppermute | solution.py:425
  144.5 4.1 %collective-permute-start.22 = (f32[3,6,4,128]{3,2,1,0:T(4,128)S(1)}, f32[3,6,4,128]{3,2,1,0:T(4,128)S(1)}, u32[]{:S(2)}, u32[]{:S(2)}) collective-permute-start(f32[3,6,4,128]{3,2,1,0:T(4,128)S(1)} %get-tuple-element.44), channel_id=1, source_target_pairs={{0,4},{4,0},{1,5},{5,1},{2,6},{6,2},{3,7},{7,3},{8,12},{12,8},{9,1... | collective-permute-start | bytes 110600 | tf_op jit(solution)/shard_map/ppermute | solution.py:425
  148.6 4.3 %copy-start.1 = (f32[2,3,6,4,128]{4,3,2,1,0:T(4,128)}, f32[2,3,6,4,128]{4,3,2,1,0:T(4,128)S(1)}, u32[]{:S(2)}) copy-start(f32[2,3,6,4,128]{4,3,2,1,0:T(4,128)S(1)} %pad_maximum_fusion.4.refs_13_) | copy-start | bytes 221188
  148.6 3.8 %collective-permute-start.23 = (f32[2,3,6,4,128]{4,3,2,1,0:T(4,128)S(1)}, f32[2,3,6,4,128]{4,3,2,1,0:T(4,128)S(1)}, u32[]{:S(2)}, u32[]{:S(2)}) collective-permute-start(f32[2,3,6,4,128]{4,3,2,1,0:T(4,128)S(1)} %pad_maximum_fusion.4.refs_13_), channel_id=1, source_target_pairs={{0,1},{1,2},{2,3},{3,0},{4,5},{5,6},{6,7},{7,4},{8,9},{9,10},{10,1... | collective-permute-start | bytes 221192 | tf_op jit(solution)/shard_map/ppermute | solution.py:425
  148.7 4.2 %collective-permute-start.24 = (f32[2,3,6,4,128]{4,3,2,1,0:T(4,128)S(1)}, f32[2,3,6,4,128]{4,3,2,1,0:T(4,128)S(1)}, u32[]{:S(2)}, u32[]{:S(2)}) collective-permute-start(f32[2,3,6,4,128]{4,3,2,1,0:T(4,128)S(1)} %pad_maximum_fusion.4.refs_13_), channel_id=1, source_target_pairs={{1,0},{2,1},{3,2},{0,3},{5,4},{6,5},{7,6},{4,7},{9,8},{10,9},{11,1... | collective-permute-start | bytes 221192 | tf_op jit(solution)/shard_map/ppermute | solution.py:428
  152.5 0.6 copy-start.7
  152.9 0.6 copy-start.8
  167.7 10.6 %all-to-all-start = ((f32[32,1,128]{2,1,0:T(1,128)}), f32[32,1,128]{2,1,0:T(1,128)S(1)}, u32[]{:S(2)}, u32[]{:S(2)}) async-start(f32[32,1,128]{2,1,0:T(1,128)} %broadcast_in_dim.2), calls=%async_computation | async-start | bytes 32768 | tf_op jit(solution)/shard_map/all_to_all | solution.py:511
  178.3 0.6 copy-start.15

commit v2 on v1

v2 whole, which is shorter than its diff:
```python
import jax
import jax.numpy as jnp
from jax import lax
from jax.experimental import pallas as pl
from jax.experimental.pallas import tpu as pltpu
from jax.sharding import PartitionSpec as P

ITERS = 3
LANES = 128
BRICK = 6.0
STATES = 2
WIDTH = STATES * 3 * 8
QWIDTH = STATES * 8
PARTS = 12
UNROLL = 16
WEIGH_UNROLL = 8
HIDDEN = 4_000_000_000
F32 = jnp.float32
BF16 = jnp.bfloat16
AXES = ("gx", "gy", "gz")
GRAM = tuple((a, b) for a in range(ITERS) for b in range(a, ITERS + 1))

VMEM = pl.BlockSpec(memory_space=pltpu.VMEM)
SMEM = pl.BlockSpec(memory_space=pltpu.SMEM)


def thirds(value):
    high = value.astype(BF16).astype(F32)
    rest = value - high
    middle = rest.astype(BF16).astype(F32)
    return high, middle, rest - middle


def call(kernel, shapes, spaces, scratch=(), limit=8, outs=None, flops=None):
    cost = None
    if flops is not None:
        cost = pl.CostEstimate(flops=flops, bytes_accessed=0, transcendentals=0)
    return pl.pallas_call(
        kernel,
        out_shape=[jax.ShapeDtypeStruct(shape, dtype) for shape, dtype in shapes],
        in_specs=spaces,
        out_specs=outs or [VMEM] * len(shapes),
        scratch_shapes=list(scratch),
        cost_estimate=cost,
        compiler_params=pltpu.CompilerParams(vmem_limit_bytes=limit << 20),
    )


def lane_take(rows, lane):
    return jnp.take_along_axis(rows, lane, axis=1, mode="promise_in_bounds")


def permuted(order, rows):
    chunks = order.shape[0]
    lane, chunk = order & (LANES - 1), order >> 7
    picked = [jnp.zeros(order.shape, F32) for _ in rows]
    for c in range(chunks):
        here = chunk == c
        for k, row in enumerate(rows):
            taken = lane_take(jnp.broadcast_to(row[c : c + 1, :], order.shape), lane)
            picked[k] = jnp.where(here, taken, picked[k])
    return picked


def prepare_kernel(packed, place, multi, response, outgoing, order):
    coords, charges, dipoles, polar = (
        [packed[k] for k in range(first, end)]
        for first, end in ((0, 3), (3, 5), (5, 11), (11, 13))
    )
    changed = packed[13] == 1.0
    order[...] = packed[14].astype(jnp.int32)
    lane = lax.broadcasted_iota(jnp.int32, (1, LANES), 1)
    ids = packed[15, 0:1, :]
    rows = [coord - 0.5 * BRICK for coord in coords]
    rows += [charges[0], jnp.where(changed, charges[1], charges[0])]
    rows += dipoles[:3]
    rows += [jnp.where(changed, dipoles[3 + k], dipoles[k]) for k in range(3)]
    rows += [polar[0], jnp.where(changed, polar[1], polar[0])]
    done = permuted(order[...], rows)
    for k in range(3):
        place[k] = done[k]
    for k in range(8):
        multi[k] = done[3 + k]
    for k in range(2):
        response[k] = done[11 + k]
    for b in range(outgoing.shape[1]):
        chosen = jnp.sum(jnp.where(lane == b, ids, 0.0)).astype(jnp.int32)
        row = pl.ds(chosen, 1)
        for k in range(3):
            outgoing[k, pl.ds(b, 1), :] = place[k, row, :]
        for k in range(8):
            outgoing[3 + k, pl.ds(b, 1), :] = multi[k, row, :]


def inverse_kernel(order, inverse):
    clusters = order.shape[0]
    column = jnp.transpose(order[...].astype(F32))
    lanes = lax.broadcasted_iota(jnp.int32, (8, LANES), 1).astype(F32)
    subs = lax.broadcasted_iota(jnp.int32, (8, LANES), 0).astype(F32)
    total = [jnp.zeros((8, LANES), F32) for _ in range(clusters)]
    for c in range(clusters):
        for g in range(LANES // 8):
            value = jnp.broadcast_to(column[8 * g : 8 * g + 8, c : c + 1], (8, LANES))
            slot = subs + float(c * LANES + 8 * g)
            for a in range(clusters):
                total[a] = jnp.where(value == lanes + float(a * LANES), slot, total[a])
    for a in range(clusters):
        inverse[a : a + 1, :] = jnp.sum(total[a], axis=0, keepdims=True).astype(jnp.int32)


def collect(target, first, own, halo, where, border, moves=None):
    kinds, padded = target.shape[0], target.shape[1]
    clusters = own.shape[1]
    base13 = clusters + 13 * border
    used = clusters + 27 * border
    for k in range(kinds):
        target[k, 0:clusters, :] = own[first + k]
        target[k, base13 : base13 + border, :] = jnp.zeros((border, LANES), F32)
        if padded > used:
            target[k, used:padded, :] = jnp.zeros((padded - used, LANES), F32)
    for slot in range(27):
        if slot == 13:
            continue
        ref, index = where[slot]
        base = clusters + slot * border
        for k in range(kinds):
            piece = halo[ref][index + (first + k,)]
            if moves is not None:
                piece = piece + moves[slot][k]
            target[k, base : base + border, :] = piece


def spread_row(ref, k, row):
    return jnp.broadcast_to(ref[k, pl.ds(row, 1), :], (8, LANES))


def write_factors(factors, y):
    sub = lax.broadcasted_iota(jnp.int32, (8, LANES), 0)
    axis_of = [jnp.logical_or(sub == 1 + k, sub == 4 + k) for k in range(3)]
    outer = jnp.logical_and(sub >= 4, sub < 7)
    unit = jnp.where(sub == 0, 1.0, 0.0).astype(F32)

    def one(r, carry):
        ys = [spread_row(y, k, r) for k in range(3)]
        far = ys[0] * ys[0] + ys[1] * ys[1] + ys[2] * ys[2]
        line = unit
        for k in range(3):
            line = jnp.where(axis_of[k], ys[k], line)
        for b in range(3):
            value = line * jnp.where(outer, 3.0 * ys[b], 1.0)
            factors[r, b] = value - jnp.where(sub == 4 + b, far, 0.0)
        return carry

    lax.fori_loop(0, y.shape[1], one, None, unroll=4)


def columns(factors, sources, row):
    block = jnp.concatenate(
        [factors[row, k % 3] * spread_row(sources, k, row) for k in range(3 * STATES)], axis=0
    )
    return jnp.concatenate(thirds(block), axis=0).astype(BF16)


def charge_columns(factors, charges, row):
    line = factors[row, 0]
    block = jnp.concatenate([line * spread_row(charges, s, row) for s in range(STATES)], axis=0)
    return jnp.concatenate(thirds(block), axis=0).astype(BF16)


def apply(left, right, width):
    both = jnp.concatenate([right[0:LANES], right[LANES:]], axis=1)
    product = lax.dot_general(
        jnp.concatenate([left, left], axis=1), both, (((1,), (1,)), ((), ())),
        preferred_element_type=F32,
    )
    return product[0:width] + product[width : 2 * width] + product[2 * width : 3 * width]


def add_tile(sums, recv, width, value):
    at = pl.ds(pl.multiple_of(recv * width, 8), width)
    sums[at, :] += value


def combine(sums, x, v, selves):
    clusters = x[0].shape[0]
    reach = x[0] * x[0] + x[1] * x[1] + x[2] * x[2] + 1.0
    fields = []
    for s in range(STATES):
        def col(b, c):
            return sums[pl.ds((3 * s + b) * 8 + c, clusters, stride=WIDTH), :]

        plain = [col(b, 0) for b in range(3)]
        cross = [[col(b, 1 + k) for k in range(3)] for b in range(3)]
        outer = [col(0, 4 + b) + col(1, 4 + b) + col(2, 4 + b) for b in range(3)]
        inner = x[0] * plain[0] + x[1] * plain[1] + x[2] * plain[2]
        inner = 3.0 * (inner - (cross[0][0] + cross[1][1] + cross[2][2]))
        for b in range(3):
            value = x[b] * inner - reach * plain[b] + outer[b]
            for k in range(3):
                value = value + x[k] * (2.0 * cross[b][k] - 3.0 * cross[k][b])
            fields.append(value + selves * v[3 * s + b])
    return fields


def receiver_features(place, c):
    sub = lax.broadcasted_iota(jnp.int32, (8, LANES), 0)
    zero = jnp.zeros((8, LANES), F32)
    unit = jnp.where(sub == 0, 1.0, 0.0).astype(F32)
    xs = [spread_row(place, k, c) for k in range(3)]
    groups = []
    for x in xs:
        high, middle, low = thirds(-2.0 * x)
        first = jnp.where(sub == 0, high, zero)
        second = jnp.where(sub == 1, middle, first)
        groups += [jnp.where(sub == 2, low, second), second, first]
    groups += [unit, unit, unit]
    high, middle, low = thirds(xs[0] * xs[0] + xs[1] * xs[1] + xs[2] * xs[2])
    groups.append(
        jnp.where(sub == 0, high, jnp.where(sub == 1, middle, jnp.where(sub == 2, low, zero)))
    )
    groups += [zero] * (LANES // 8 - len(groups))
    return jnp.concatenate(groups, axis=0).astype(BF16)


def write_parts(pieces, y):
    for g in range(y.shape[1] // 8):
        at = slice(8 * g, 8 * g + 8)
        ys = [y[k, at, :] for k in range(3)]
        ys.append(ys[0] * ys[0] + ys[1] * ys[1] + ys[2] * ys[2] + 1.0)
        for k in range(4):
            for p, part in enumerate(thirds(ys[k])):
                pieces[3 * k + p, at, :] = part


def source_features(pieces, row):
    groups = [spread_row(pieces, k, row) for k in range(PARTS)]
    groups.append(jnp.ones((8, LANES), F32))
    groups += [jnp.zeros((8, LANES), F32)] * (LANES // 8 - len(groups))
    return jnp.concatenate(groups, axis=0).astype(BF16)


def plan_kernel(tiles, count, border_ids, near, rest, sizes, selves, flags, pairs):
    clusters = selves.shape[0]
    border = border_ids.shape[0]
    tile_num = tiles.shape[1]
    dummy = clusters + 13 * border
    for c in range(clusters):
        flags[c] = 0
        pairs[c] = 0
    for b in range(border):
        flags[border_ids[b]] = 1

    def place_tile(t, ends):
        recv, slot, source = tiles[0, t], tiles[1, t], tiles[2, t]
        row = jnp.where(slot == 13, source, clusters + slot * border + source)
        used = (t < count[0]).astype(jnp.int32)
        seen = flags[recv]
        for which, target in enumerate((near, rest)):
            target[0, ends[which]] = recv
            target[1, ends[which]] = row
        same = jnp.logical_and(slot == 13, source == recv).astype(jnp.int32)
        pairs[recv] = pairs[recv] + used * same
        return ends[0] + used * seen, ends[1] + used * (1 - seen)

    ends = lax.fori_loop(0, tile_num, place_tile, (jnp.int32(0), jnp.int32(0)))
    for which, target in enumerate((near, rest)):
        for u in range(UNROLL):
            target[0, ends[which] + u] = 0
            target[1, ends[which] + u] = dummy
        sizes[which] = (ends[which] + UNROLL - 1) // UNROLL
    sizes[2] = (sizes[1] + 1) // 2
    for c in range(clusters):
        selves[c : c + 1, :] = jnp.full((1, LANES), pairs[c].astype(F32))


def turn_kernel(place, turned):
    eye = lax.broadcasted_iota(jnp.int32, (LANES, LANES), 0) == lax.broadcasted_iota(
        jnp.int32, (LANES, LANES), 1
    )
    eye = jnp.where(eye, 1.0, 0.0).astype(BF16)

    def turn(c, carry):
        turned[c] = lax.dot_general(
            eye, receiver_features(place, c), (((1,), (1,)), ((), ())),
            preferred_element_type=F32,
        ).astype(BF16)
        return carry

    lax.fori_loop(0, place.shape[1], turn, None, unroll=8)


def over_tiles(groups, body, unroll=UNROLL):
    def one(i, carry):
        for u in range(unroll):
            body(i * unroll + u)
        return carry

    first, end = groups if isinstance(groups, tuple) else (0, groups)
    lax.fori_loop(first * (UNROLL // unroll), end * (UNROLL // unroll), one, None)


def weigh_tiles(tiles, groups, turned, pieces, matrix, cubes):
    def one(t):
        recv, row = tiles[0, t], tiles[1, t]
        squared = jnp.dot(
            turned[recv], source_features(pieces, row), preferred_element_type=F32
        )
        inverse = lax.rsqrt(squared)
        second = inverse * inverse
        g3 = second * inverse
        g5 = g3 * second
        for target, value in ((matrix, g5), (cubes, g3)):
            high = value.astype(BF16)
            target[t, 0:LANES, :] = high
            target[t, LANES:, :] = (value - high.astype(F32)).astype(BF16)

    over_tiles(groups, one, WEIGH_UNROLL)


def apply_tiles(tiles, groups, factors, sources, matrix, sums, charges=None, cubes=None, sums_q=None):
    def one(t):
        recv, row = tiles[0, t], tiles[1, t]
        add_tile(sums, recv, WIDTH, apply(columns(factors, sources, row), matrix[t], WIDTH))
        if cubes is not None:
            left = charge_columns(factors, charges, row)
            add_tile(sums_q, recv, QWIDTH, apply(left, cubes[t], QWIDTH))

    over_tiles(groups, one)


def permanent(sums, sums_q, place, multi, selves):
    clusters = place.shape[1]
    x = [place[k] for k in range(3)]
    fields = combine(sums, x, [multi[2 + k] for k in range(6)], selves[...])
    for s in range(STATES):
        def col(c):
            return sums_q[pl.ds(s * 8 + c, clusters, stride=QWIDTH), :]

        whole = col(0)
        for b in range(3):
            fields[3 * s + b] = fields[3 * s + b] + (x[b] * whole - col(1 + b))
    return fields


class Stack:
    def __init__(self, rows):
        self.rows = rows
        self.shape = (len(rows),) + rows[0].shape

    def __getitem__(self, k):
        return self.rows[k]


def send_border(values, held, outgoing, border_ids):
    for k, value in enumerate(values):
        held[k] = value
    for b in range(outgoing.shape[1]):
        row = pl.ds(border_ids[b], 1)
        for k in range(len(values)):
            outgoing[k, pl.ds(b, 1), :] = held[k, row, :]


def first_near_kernel(where, parts_of, *refs):
    tiles, sizes, border_ids, place, multi, response, turned, selves = refs[:8]
    halo = refs[8 : 8 + parts_of]
    (outgoing, matrix, factors, pieces, moments, charges, sums, sums_q,
     y, cubes, held) = refs[8 + parts_of :]
    border = outgoing.shape[1]
    moves = [
        tuple(BRICK * o for o in (slot // 9 - 1, slot // 3 % 3 - 1, slot % 3 - 1))
        for slot in range(27)
    ]
    own = Stack([place[k] for k in range(3)] + [multi[k] for k in range(8)])
    collect(y, 0, own, halo, where, border, moves)
    collect(charges, 3, own, halo, where, border)
    collect(moments, 5, own, halo, where, border)
    write_factors(factors, y)
    write_parts(pieces, y)
    sums[...] = jnp.zeros_like(sums)
    sums_q[...] = jnp.zeros_like(sums_q)
    weigh_tiles(tiles, sizes[0], turned, pieces, matrix, cubes)
    apply_tiles(tiles, sizes[0], factors, moments, matrix, sums, charges, cubes, sums_q)
    fields = permanent(sums, sums_q, place, multi, selves)
    send_border(
        [response[k // 3] * fields[k] for k in range(6)], held, outgoing, border_ids
    )


def first_weigh_kernel(tiles, sizes, turned, pieces, matrix, cubes):
    weigh_tiles(tiles, sizes[1], turned, pieces, matrix, cubes)


def first_rest_kernel(tiles, sizes, place, multi, response, selves, factors,
                      moments, charges, matrix, cubes, sums_in, sums_q_in, induced, sums, sums_q):
    sums[...] = sums_in[...]
    sums_q[...] = sums_q_in[...]
    apply_tiles(tiles, sizes[1], factors, moments, matrix, sums, charges, cubes, sums_q)
    fields = permanent(sums, sums_q, place, multi, selves)
    for k in range(6):
        induced[k] = response[k // 3] * fields[k]


def near_kernel(where, parts_of, *refs):
    tiles, sizes, border_ids, place, response, selves, factors, matrix, own = refs[:9]
    halo = refs[9 : 9 + parts_of]
    outgoing, sources, sums, held = refs[9 + parts_of :]
    collect(sources, 0, own, halo, where, outgoing.shape[1])
    sums[...] = jnp.zeros_like(sums)
    apply_tiles(tiles, sizes[0], factors, sources, matrix, sums)
    x = [place[k] for k in range(3)]
    fields = combine(sums, x, [own[k] for k in range(6)], selves[...])
    send_border(
        [response[k // 3] * fields[k] for k in range(6)], held, outgoing, border_ids
    )


def middle_kernel(tiles, sizes, factors, matrix, sources, sums_in, sums):
    sums[...] = sums_in[...]
    apply_tiles(tiles, sizes[2], factors, sources, matrix, sums)


def rest_kernel(tiles, sizes, place, response, selves, factors, matrix, own, sources, sums_in,
                plain, scaled, sums):
    sums[...] = sums_in[...]
    apply_tiles(tiles, (sizes[2], sizes[1]), factors, sources, matrix, sums)
    x = [place[k] for k in range(3)]
    fields = combine(sums, x, [own[k] for k in range(6)], selves[...])
    for k in range(6):
        plain[k] = fields[k]
        scaled[k] = response[k // 3] * fields[k]


def last_kernel(where, parts_of, border, *refs):
    near, rest, sizes, place, response, selves, factors, matrix_near, matrix_rest = refs[:9]
    plains = refs[9 : 9 + ITERS]
    scaleds = refs[9 + ITERS : 9 + 2 * ITERS]
    base = 9 + 2 * ITERS
    halo = refs[base : base + parts_of]
    gram, sources, sums = refs[base + parts_of :]
    own = scaleds[-1]
    collect(sources, 0, own, halo, where, border)
    sums[...] = jnp.zeros_like(sums)
    apply_tiles(near, sizes[0], factors, sources, matrix_near, sums)
    apply_tiles(rest, sizes[1], factors, sources, matrix_rest, sums)
    x = [place[k] for k in range(3)]
    fields = combine(sums, x, [own[k] for k in range(6)], selves[...])
    lane = lax.broadcasted_iota(jnp.int32, (1, LANES), 1)
    total = jnp.zeros((1, LANES), F32)
    for s in range(STATES):
        for e, (a, b) in enumerate(GRAM):
            sum_of = None
            for k in range(3 * s, 3 * s + 3):
                right = scaleds[b][k] if b < ITERS else response[s] * fields[k]
                term = plains[a][k] * right
                sum_of = term if sum_of is None else sum_of + term
            value = jnp.sum(jnp.sum(sum_of, axis=0, keepdims=True), axis=1, keepdims=True)
            total = jnp.where(lane == s * len(GRAM) + e, value, total)
    gram[...] = jnp.broadcast_to(total, gram.shape)


def coefficients(numbers):
    def entry(a, b):
        return numbers[(a, b) if a <= b else (b, a)]

    def form(left, right, moved):
        out = None
        for a, u in enumerate(left):
            for b, w in enumerate(right):
                term = u * w * entry(a, b + moved)
                out = term if out is None else out + term
        return out

    one = jnp.ones_like(numbers[(0, 0)])
    residual, direction = [one], [one]
    weights = [jnp.zeros_like(one)] * ITERS
    norm = form(residual, residual, 0)
    for sweep in range(ITERS):
        curve = form(direction, direction, 0) - form(direction, direction, 1)
        step = norm / curve
        weights = [
            w + step * direction[k] if k < len(direction) else w for k, w in enumerate(weights)
        ]
        if sweep + 1 == ITERS:
            break
        image = direction + [jnp.zeros_like(one)]
        image = [image[0]] + [image[k] - direction[k - 1] for k in range(1, len(image))]
        residual = [
            (residual[k] if k < len(residual) else 0.0) - step * image[k] for k in range(len(image))
        ]
        after = form(residual, residual, 0)
        ratio = after / norm
        direction = [
            residual[k] + ratio * direction[k] if k < len(direction) else residual[k]
            for k in range(len(residual))
        ]
        norm = after
    return weights


def finish_kernel(grams, induced, *refs):
    scaleds = refs[:ITERS]
    inverse, result = refs[ITERS : ITERS + 2]
    total = jnp.sum(grams[...], axis=0, keepdims=True)
    rows = []
    for s in range(STATES):
        numbers = {
            pair: total[:, s * len(GRAM) + e : s * len(GRAM) + e + 1]
            for e, pair in enumerate(GRAM)
        }
        weights = coefficients(numbers)
        for k in range(3 * s, 3 * s + 3):
            value = induced[k]
            for w, scaled in zip(weights, scaleds):
                value = value + w * scaled[k]
            rows.append(value)
    done = permuted(inverse[...], rows)
    for k in range(6):
        result[k] = done[k]


def ring(cells, axis):
    count = lax.axis_size(axis)
    if count == 1:
        return [cells], (0, 0, 0)
    below = lax.ppermute(cells, axis, [(i, (i + 1) % count) for i in range(count)])
    if count == 2:
        return [cells, below], (1, 0, 1)
    above = lax.ppermute(cells, axis, [((i + 1) % count, i) for i in range(count)])
    return [below, cells, above], (0, 1, 2)


def neighbours(cells, beside):
    first, place_x = ring(cells, "gx")
    stacked, *beside = lax.optimization_barrier((jnp.stack(first), *beside))
    second, place_y = ring(stacked, "gy")
    stacked = jnp.stack(second)
    third, place_z = ring(stacked, "gz")
    where = tuple(
        (place_z[n % 3], (place_y[n // 3 % 3], place_x[n // 9])) for n in range(27)
    )
    return third, where, beside


def shards(coords, charges, dipoles, polar, perturbed, cluster_order, border_clusters,
           tile_list, tile_count):
    atoms = coords.shape[-1]
    clusters = atoms // LANES
    border = border_clusters.shape[-1]
    tile_num = tile_list.shape[-1]
    padded = -(-(clusters + 27 * border) // LANES) * LANES

    border_ids = border_clusters.reshape(border)
    tiles = tile_list.reshape(3, tile_num)
    count = tile_count.reshape(1)
    devices = 1
    for axis in AXES:
        devices *= lax.axis_size(axis)

    cell = (clusters, LANES)
    vector = ((6,) + cell, F32)
    leave = ((6, border, LANES), F32)
    listed = -(-tile_num // UNROLL) * UNROLL
    matrix = ((listed, 2 * LANES, LANES), BF16)
    table = ((6, padded, LANES), F32)
    sums = ((clusters * WIDTH, LANES), F32)
    sums_q = ((clusters * QWIDTH, LANES), F32)
    listing = ((2, listed + UNROLL), jnp.int32)

    whole, at = {}, 0
    for array in (coords, charges, dipoles, polar, perturbed, cluster_order, border_ids):
        array = array.reshape((1, 1, border) if array.ndim == 1 else (-1,) + cell)
        kinds = array.shape[0]
        sides = [(at, 16 - at - kinds)] + [(0, n - k) for n, k in zip(cell, array.shape[1:])]
        array = jnp.pad(array, sides)
        whole[array.dtype] = whole[array.dtype] + array if array.dtype in whole else array
        at += kinds
    whole = sum(part.astype(F32) for part in whole.values())
    place, multi, response, outgoing, order = call(
        prepare_kernel,
        [((3,) + cell, F32), ((8,) + cell, F32), ((2,) + cell, F32), ((11, border, LANES), F32),
         (cell, jnp.int32)],
        [VMEM],
    )(whole)
    near, rest, sizes, selves = call(
        plan_kernel,
        [listing, listing, ((3,), jnp.int32), (cell, F32)],
        [SMEM] * 3,
        [pltpu.SMEM((clusters,), jnp.int32)] * 2,
        outs=[SMEM] * 3 + [VMEM],
        flops=HIDDEN,
    )(tiles, count, border_ids)
    (turned,) = call(
        turn_kernel, [((clusters, LANES, LANES), BF16)], [VMEM], flops=HIDDEN
    )(place)
    (inverse,) = call(inverse_kernel, [(cell, jnp.int32)], [VMEM], flops=HIDDEN)(order)

    halo, where, (turned,) = neighbours(outgoing, (turned,))
    (leaving, matrix_near, factors, pieces, moments, charge_rows, partial, partial_q) = call(
        lambda *refs: first_near_kernel(where, len(halo), *refs),
        [leave, matrix, ((padded, 3, 8, LANES), F32), ((PARTS, padded, LANES), F32), table,
         ((2, padded, LANES), F32), sums, sums_q],
        [SMEM] * 3 + [VMEM] * (5 + len(halo)),
        [pltpu.VMEM((3, padded, LANES), F32), pltpu.VMEM(*matrix), pltpu.VMEM(*vector)],
        16,
    )(near, sizes, border_ids, place, multi, response, turned, selves, *halo)
    matrix_rest, cubes = call(
        first_weigh_kernel, [matrix, matrix], [SMEM] * 2 + [VMEM] * 2, flops=HIDDEN
    )(rest, sizes, turned, pieces)
    halo, where, (matrix_rest, cubes) = neighbours(leaving, (matrix_rest, cubes))
    (induced,) = call(
        first_rest_kernel, [vector], [SMEM] * 2 + [VMEM] * 11,
        [pltpu.VMEM(*sums), pltpu.VMEM(*sums_q)], flops=HIDDEN,
    )(rest, sizes, place, multi, response, selves, factors, moments, charge_rows,
      matrix_rest, cubes, partial, partial_q)

    own = induced
    plains, scaleds = [], []
    for _ in range(ITERS):
        leaving, sources, partial = call(
            lambda *refs, where=where, parts=len(halo): near_kernel(where, parts, *refs),
            [leave, table, sums], [SMEM] * 3 + [VMEM] * (6 + len(halo)),
            [pltpu.VMEM(*vector)],
        )(near, sizes, border_ids, place, response, selves, factors, matrix_near, own, *halo)
        (partial,) = call(
            middle_kernel, [sums], [SMEM] * 2 + [VMEM] * 4, flops=HIDDEN
        )(rest, sizes, factors, matrix_rest, sources, partial)
        halo, where, (partial,) = neighbours(leaving, (partial,))
        plain, own = call(
            rest_kernel, [vector, vector], [SMEM] * 2 + [VMEM] * 8, [pltpu.VMEM(*sums)],
            flops=HIDDEN,
        )(rest, sizes, place, response, selves, factors, matrix_rest, own, sources, partial)
        plains.append(plain)
        scaleds.append(own)
    (gram,) = call(
        lambda *refs: last_kernel(where, len(halo), border, *refs),
        [((devices, LANES), F32)],
        [SMEM] * 3 + [VMEM] * (6 + 2 * ITERS + len(halo)),
        [pltpu.VMEM(*table), pltpu.VMEM(*sums)],
    )(near, rest, sizes, place, response, selves, factors, matrix_near, matrix_rest,
      *plains, *scaleds, *halo)

    grams = lax.all_to_all(gram, AXES, 0, 0, tiled=True)
    (result,) = call(
        finish_kernel, [vector], [VMEM] * (3 + ITERS)
    )(grams, induced, *scaleds, inverse)
    return result.reshape(6, 1, 1, 1, atoms)


def solution(mesh):
    wide = P(None, "gx", "gy", "gz", None)
    brick = P("gx", "gy", "gz", None)
    placed = (wide, wide, wide, wide, brick, brick, brick, wide, P("gx", "gy", "gz"))
    return jax.shard_map(
        shards, mesh=mesh, in_specs=placed, out_specs=wide, check_vma=False
    )
```

time: 182 us -> 117 us (0.64)
  Pallas kernels: 89.5 us -> 47.1 us
  waiting for transfers between devices: 47.2 us -> 19.8 us
  starting transfers between devices: 33.5 us -> 48.3 us
  local copies, waits for them, and re-layouts: 6.33 us -> 0.01 us
  other arithmetic: 3.73 us -> 1.07 us
    pallas_call x7 -> x17, Pallas kernels: 87.5 us -> 46.5 us  [the longest x3 6.6 us: shards(): call(rest_kernel, [vector, vector], [SMEM] * 2 + [VMEM] * 8, [pltpu.VMEM(...]
    ppermute x15, waiting for transfers between devices: 33.3 us -> 14.3 us  [ring(): lax.ppermute(cells, axis, [(i, (i + 1) % count) for i in range(count)])]
    ppermute x10, starting transfers between devices: 13.9 us -> 29 us  [ring(): lax.ppermute(cells, axis, [((i + 1) % count, i) for i in range(count)])]
    ppermute x10, waiting for transfers between devices: 10.7 us -> 0.93 us  [ring(): lax.ppermute(cells, axis, [((i + 1) % count, i) for i in range(count)])]
    unnamed x33 -> x5, local copies, waits for them, and re-layouts: 5.03 us -> 0.01 us
    another operation x10 -> x5, other arithmetic: 3.73 us -> 0.1 us  [neighbours(): stacked = jnp.stack(second)]
    ppermute x15, starting transfers between devices: 16 us -> 13.1 us  [ring(): lax.ppermute(cells, axis, [(i, (i + 1) % count) for i in range(count)])]
    all_to_all x1, starting transfers between devices: 3.67 us -> 6.18 us  [shards(): grams = lax.all_to_all(gram, AXES, 0, 0, tiled=True)]
  transfers between devices with their start and end apart: 26 -> 26, of which waited for: 26 -> 10; matrix products, arithmetic and copies ran while one was open for 1% -> 0% of each run, Pallas kernels for 2% -> 25%
where the time goes in v2:
time: 117 us
  starting transfers between devices  48.3 us (41%)
  Pallas kernels  47.1 us (40%)
  waiting for transfers between devices  19.8 us (17%)
    ppermute x10, starting transfers between devices, ring(): lax.ppermute(cells, axis, [((i + 1) % count, i) for i in range(count)])  29 us
    ppermute x15, waiting for transfers between devices, ring(): lax.ppermute(cells, axis, [(i, (i + 1) % count) for i in range(count)])  14.3 us
    ppermute x15, starting transfers between devices, ring(): lax.ppermute(cells, axis, [(i, (i + 1) % count) for i in range(count)])  13.1 us
    pallas_call x3, Pallas kernels, shards(): call(rest_kernel, [vector, vector], [SMEM] * 2 + [VMEM] * 8, [pltpu.VMEM(...  6.6 us
    pallas_call x3, Pallas kernels, shards(): call(middle_kernel, [sums], [SMEM] * 2 + [VMEM] * 4, flops=HIDDEN)  6.2 us
    all_to_all x1, starting transfers between devices, shards(): grams = lax.all_to_all(gram, AXES, 0, 0, tiled=True)  6.18 us
    pallas_call x1, Pallas kernels, shards(): call(lambda *refs: last_kernel(where, len(halo), border, *refs), [((devic...  5.68 us
    pallas_call x1, Pallas kernels, shards(): call(first_rest_kernel, [vector], [SMEM] * 2 + [VMEM] * 11, [pltpu.VMEM(*...  5.54 us
  transfers between devices with their start and end apart: 26, of which 10 were waited for; matrix products, arithmetic and copies ran while one was open for 0% of the time, Pallas kernels for 25%

profile of v2, /device:TPU:0, one launch (start us, length us, event | category | flops | bytes accessed | tf_op | source)
XLA Modules:
  0.0 117.3 jit_solution(10215375699288372966)
XLA Ops:
  0.0 0.9 convert_add_fusion.packed
  0.9 0.6 shard_map.92
  1.5 5.1 %collective-permute-start.1 = (f32[11,4,128]{2,1,0:T(4,128)S(1)}, f32[11,4,128]{2,1,0:T(4,128)S(1)}, u32[]{:S(2)}, u32[]{:S(2)}) collective-permute-start(f32[11,4,128]{2,1,0:T(4,128)S(1)} %get-tuple-element.57), channel_id=1, source_target_pairs={{8,0},{16,8},{24,16},{0,24},{9,1},{17,9},{25,17},{1,25},{10,2},{18... | collective-permute-start | bytes 67592 | tf_op jit(solution)/shard_map/ppermute | solution.py:528
  6.7 0.0 collective-permute-start
  6.7 0.6 shard_map.93.refs_6_.turned
  7.2 0.9 collective-permute-done.1
  8.2 4.1 %collective-permute-done = f32[11,4,128]{2,1,0:T(4,128)S(1)} collective-permute-done((f32[11,4,128]{2,1,0:T(4,128)S(1)}, f32[11,4,128]{2,1,0:T(4,128)S(1)}, u32[]{:S(2)}, u32[]{:S(2)}) %collective-permute-start) | collective-permute-done | bytes 22560 | tf_op jit(solution)/shard_map/ppermute | solution.py:525
  12.3 1.6 %collective-permute-start.2 = (f32[3,11,4,128]{3,2,1,0:T(4,128)S(1)}, f32[3,11,4,128]{3,2,1,0:T(4,128)S(1)}, u32[]{:S(2)}, u32[]{:S(2)}) collective-permute-start(f32[3,11,4,128]{3,2,1,0:T(4,128)S(1)} %pad_maximum_fusion.5), channel_id=1, source_target_pairs={{0,4},{4,0},{1,5},{5,1},{2,6},{6,2},{3,7},{7,3},{8,12},{12,8},{9,1... | collective-permute-start | bytes 202760 | tf_op jit(solution)/shard_map/ppermute | solution.py:525
  14.5 2.1 %collective-permute-done.2 = f32[3,11,4,128]{3,2,1,0:T(4,128)S(1)} collective-permute-done((f32[3,11,4,128]{3,2,1,0:T(4,128)S(1)}, f32[3,11,4,128]{3,2,1,0:T(4,128)S(1)}, u32[]{:S(2)}, u32[]{:S(2)}) %collective-permute-start.2) | collective-permute-done | bytes 67616 | tf_op jit(solution)/shard_map/ppermute | solution.py:525
  16.7 0.1 collective-permute-start.3
  16.7 1.7 %collective-permute-start.4 = (f32[2,3,11,4,128]{4,3,2,1,0:T(4,128)S(1)}, f32[2,3,11,4,128]{4,3,2,1,0:T(4,128)S(1)}, u32[]{:S(2)}, u32[]{:S(2)}) collective-permute-start(f32[2,3,11,4,128]{4,3,2,1,0:T(4,128)S(1)} %pad_maximum_fusion.refs_9_), channel_id=1, source_target_pairs={{1,0},{2,1},{3,2},{0,3},{5,4},{6,5},{7,6},{4,7},{9,8},{10,9},{11,1... | collective-permute-start | bytes 405512 | tf_op jit(solution)/shard_map/ppermute | solution.py:528
  18.5 3.7 %shard_map.91 = (s32[2,144]{1,0:T(2,128)S(1)}, s32[2,144]{1,0:T(2,128)S(1)}, s32[3]{0:T(128)S(1)}, f32[16,128]{1,0:T(8,128)S(1)}) custom-call(s32[3,128]{1,0:T(4,128)S(1)} %bitcast.55, s32[1]{0:T(128)} %bitcast.42.count, s32[4]{0:T(128)S(1)} %bitcast.46), custom_call_target="tpu_custom_call" | custom-call | flops 4000000000 | tf_op jit(solution)/shard_map/pallas_call | solution.py:584
  22.1 0.0 collective-permute-done.3.refs_8_
  22.1 0.0 collective-permute-done.4.refs_10_
  22.1 4.4 %shard_map.94 = (f32[6,4,128]{2,1,0:T(4,128)S(1)}, bf16[128,256,128]{2,1,0:T(8,128)(2,1)S(1)}, f32[128,3,8,128]{3,2,1,0:T(8,128)S(1)}, f32[12,128,128]{2,1,0:T(8...) custom-call(s32[2,144]{1,0:T(2,128)S(1)} %get-tuple-element.50.refs_, ...), custom_call_target="tpu_custom_call" | custom-call | tf_op jit(solution)/shard_map/pallas_call | solution.py:598
  26.6 0.1 collective-permute-start.5
  26.7 3.8 %collective-permute-start.6 = (f32[6,4,128]{2,1,0:T(4,128)S(1)}, f32[6,4,128]{2,1,0:T(4,128)S(1)}, u32[]{:S(2)}, u32[]{:S(2)}) collective-permute-start(f32[6,4,128]{2,1,0:T(4,128)S(1)} %get-tuple-element.62), channel_id=1, source_target_pairs={{8,0},{16,8},{24,16},{0,24},{9,1},{17,9},{25,17},{1,25},{10,2},{18... | collective-permute-start | bytes 36872 | tf_op jit(solution)/shard_map/ppermute | solution.py:528
  30.5 4.7 %shard_map.95 = (bf16[128,256,128]{2,1,0:T(8,128)(2,1)S(1)}, bf16[128,256,128]{2,1,0:T(8,128)(2,1)S(1)}) custom-call(s32[2,144]{1,0:T(2,128)S(1)} %get-tuple-element.51.tiles.refs_1_, s32[3]{0:T(128)S(1)} %get-tuple-element.52.refs_1_.sizes.refs_2_, bf16[16,128,128]{2,1,0:T(8,128)(2,1)S(1)} %shard_map.93.refs_6_.turned, ...), custom_call_target="tpu_custom_call" | custom-call | flops 4000000000 | tf_op jit(solution)/shard_map/pallas_call | solution.py:606
  35.2 0.0 collective-permute-done.5
  35.2 0.0 collective-permute-done.6
  35.2 2.2 %collective-permute-start.7 = (f32[3,6,4,128]{3,2,1,0:T(4,128)S(1)}, f32[3,6,4,128]{3,2,1,0:T(4,128)S(1)}, u32[]{:S(2)}, u32[]{:S(2)}) collective-permute-start(f32[3,6,4,128]{3,2,1,0:T(4,128)S(1)} %pad_maximum_fusion.6), channel_id=1, source_target_pairs={{0,4},{4,0},{1,5},{5,1},{2,6},{6,2},{3,7},{7,3},{8,12},{12,8},{9,1... | collective-permute-start | bytes 110600 | tf_op jit(solution)/shard_map/ppermute | solution.py:525
  37.5 1.9 %collective-permute-done.7 = f32[3,6,4,128]{3,2,1,0:T(4,128)S(1)} collective-permute-done((f32[3,6,4,128]{3,2,1,0:T(4,128)S(1)}, f32[3,6,4,128]{3,2,1,0:T(4,128)S(1)}, u32[]{:S(2)}, u32[]{:S(2)}) %collective-permute-start.7) | collective-permute-done | bytes 36896 | tf_op jit(solution)/shard_map/ppermute | solution.py:525
  39.4 0.1 collective-permute-start.8
  39.5 1.7 %collective-permute-start.9 = (f32[2,3,6,4,128]{4,3,2,1,0:T(4,128)S(1)}, f32[2,3,6,4,128]{4,3,2,1,0:T(4,128)S(1)}, u32[]{:S(2)}, u32[]{:S(2)}) collective-permute-start(f32[2,3,6,4,128]{4,3,2,1,0:T(4,128)S(1)} %pad_maximum_fusion.1.refs_10_), channel_id=1, source_target_pairs={{1,0},{2,1},{3,2},{0,3},{5,4},{6,5},{7,6},{4,7},{9,8},{10,9},{11,1... | collective-permute-start | bytes 221192 | tf_op jit(solution)/shard_map/ppermute | solution.py:528
  41.2 5.5 %shard_map.96.refs_8_.own.induced = f32[6,16,128]{2,1,0:T(8,128)S(1)} custom-call(s32[2,144]{1,0:T(2,128)S(1)} %get-tuple-element.51.tiles.refs_1_, s32[3]{0:T(128)S(1)} %get-tuple-element.52.refs_1_.sizes.refs_2_, f32[3,16,128]{2,1,0:T(8,128)S(1)} %get-tuple-element.53.place.refs_3_, f32[8,16,128]{2,1,0:T(8,128)S(1)} %get-tuple-element.56.refs_4_.multi, ...), custom_call_target="tpu_custom_call" | custom-call | flops 4000000000 | tf_op jit(solution)/shard_map/pallas_call | solution.py:610
  46.8 0.0 collective-permute-done.8.refs_9_
  46.8 1.8 %shard_map.97 = (f32[6,4,128]{2,1,0:T(4,128)S(1)}, f32[6,128,128]{2,1,0:T(8,128)S(1)}, f32[768,128]{1,0:T(8,128)S(1)}) custom-call(s32[2,144]{1,0:T(2,128)S(1)} %get-tuple-element.50.refs_0_, s32[3]{0:T(128)S(1)} %get-tuple-element.52.refs_1_.sizes.refs_2_, s32[4]{0:T(128)S(1)} %bitcast.48, f32[3,16,128]{2,1,0:T(8,128)S(1)} %get-tuple-element.53.place.refs_3_, ...), custom_call_target="tpu_custom_call" | custom-call | tf_op jit(solution)/shard_map/pallas_call | solution.py:619
  48.6 0.1 collective-permute-start.10
  48.6 3.8 %collective-permute-start.11 = (f32[6,4,128]{2,1,0:T(4,128)S(1)}, f32[6,4,128]{2,1,0:T(4,128)S(1)}, u32[]{:S(2)}, u32[]{:S(2)}) collective-permute-start(f32[6,4,128]{2,1,0:T(4,128)S(1)} %get-tuple-element.74), channel_id=1, source_target_pairs={{8,0},{16,8},{24,16},{0,24},{9,1},{17,9},{25,17},{1,25},{10,2},{18... | collective-permute-start | bytes 36872 | tf_op jit(solution)/shard_map/ppermute | solution.py:528
  52.5 2.1 %shard_map.98.sums_in = f32[768,128]{1,0:T(8,128)S(1)} custom-call(s32[2,144]{1,0:T(2,128)S(1)} %get-tuple-element.51.tiles.refs_1_, s32[3]{0:T(128)S(1)} %get-tuple-element.52.refs_1_.sizes.refs_2_, f32[128,3,8,128]{3,2,1,0:T(8,128)S(1)} %get-tuple-element.60.factors.refs_6_, bf16[128,256,128]{2,1,0:T(8,128)(2,1)S(1)} %get-tuple-element.66.matrix.refs_8_, ...), custom_call_target="tpu_custom_call" | custom-call | flops 4000000000 | tf_op jit(solution)/shard_map/pallas_call | solution.py:624
  54.6 3.4 %collective-permute-start.12 = (f32[3,6,4,128]{3,2,1,0:T(4,128)S(1)}, f32[3,6,4,128]{3,2,1,0:T(4,128)S(1)}, u32[]{:S(2)}, u32[]{:S(2)}) collective-permute-start(f32[3,6,4,128]{3,2,1,0:T(4,128)S(1)} %pad_maximum_fusion.7), channel_id=1, source_target_pairs={{0,4},{4,0},{1,5},{5,1},{2,6},{6,2},{3,7},{7,3},{8,12},{12,8},{9,1... | collective-permute-start | bytes 110600 | tf_op jit(solution)/shard_map/ppermute | solution.py:525
  57.9 1.9 %collective-permute-done.12 = f32[3,6,4,128]{3,2,1,0:T(4,128)S(1)} collective-permute-done((f32[3,6,4,128]{3,2,1,0:T(4,128)S(1)}, f32[3,6,4,128]{3,2,1,0:T(4,128)S(1)}, u32[]{:S(2)}, u32[]{:S(2)}) %collective-permute-start.12) | collective-permute-done | bytes 36896 | tf_op jit(solution)/shard_map/ppermute | solution.py:525
  59.9 0.1 collective-permute-start.13
  60.0 1.7 %collective-permute-start.14 = (f32[2,3,6,4,128]{4,3,2,1,0:T(4,128)S(1)}, f32[2,3,6,4,128]{4,3,2,1,0:T(4,128)S(1)}, u32[]{:S(2)}, u32[]{:S(2)}) collective-permute-start(f32[2,3,6,4,128]{4,3,2,1,0:T(4,128)S(1)} %pad_maximum_fusion.2.refs_10_), channel_id=1, source_target_pairs={{1,0},{2,1},{3,2},{0,3},{5,4},{6,5},{7,6},{4,7},{9,8},{10,9},{11,1... | collective-permute-start | bytes 221192 | tf_op jit(solution)/shard_map/ppermute | solution.py:528
  61.7 2.2 %shard_map.99 = (f32[6,16,128]{2,1,0:T(8,128)S(1)}, f32[6,16,128]{2,1,0:T(8,128)S(1)}) custom-call(s32[2,144]{1,0:T(2,128)S(1)} %get-tuple-element.51.tiles.refs_1_, s32[3]{0:T(128)S(1)} %get-tuple-element.52.refs_1_.sizes.refs_2_, f32[3,16,128]{2,1,0:T(8,128)S(1)} %get-tuple-element.53.place.refs_3_, ...), custom_call_target="tpu_custom_call" | custom-call | flops 4000000000 | tf_op jit(solution)/shard_map/pallas_call | solution.py:628
  63.9 0.1 collective-permute-done.13.refs_9_
  64.0 1.8 %shard_map.100 = (f32[6,4,128]{2,1,0:T(4,128)S(1)}, f32[6,128,128]{2,1,0:T(8,128)S(1)}, f32[768,128]{1,0:T(8,128)S(1)}) custom-call(s32[2,144]{1,0:T(2,128)S(1)} %get-tuple-element.50.refs_0_, s32[3]{0:T(128)S(1)} %get-tuple-element.52.refs_1_.sizes.refs_2_, s32[4]{0:T(128)S(1)} %bitcast.49, f32[3,16,128]{2,1,0:T(8,128)S(1)} %get-tuple-element.53.place.refs_3_, ...), custom_call_target="tpu_custom_call" | custom-call | tf_op jit(solution)/shard_map/pallas_call | solution.py:619
  65.7 0.1 collective-permute-start.15
  65.8 3.8 %collective-permute-start.16 = (f32[6,4,128]{2,1,0:T(4,128)S(1)}, f32[6,4,128]{2,1,0:T(4,128)S(1)}, u32[]{:S(2)}, u32[]{:S(2)}) collective-permute-start(f32[6,4,128]{2,1,0:T(4,128)S(1)} %get-tuple-element.81), channel_id=1, source_target_pairs={{8,0},{16,8},{24,16},{0,24},{9,1},{17,9},{25,17},{1,25},{10,2},{18... | collective-permute-start | bytes 36872 | tf_op jit(solution)/shard_map/ppermute | solution.py:528
  69.6 2.1 %shard_map.101.sums_in = f32[768,128]{1,0:T(8,128)S(1)} custom-call(s32[2,144]{1,0:T(2,128)S(1)} %get-tuple-element.51.tiles.refs_1_, s32[3]{0:T(128)S(1)} %get-tuple-element.52.refs_1_.sizes.refs_2_, f32[128,3,8,128]{3,2,1,0:T(8,128)S(1)} %get-tuple-element.60.factors.refs_6_, bf16[128,256,128]{2,1,0:T(8,128)(2,1)S(1)} %get-tuple-element.66.matrix.refs_8_, ...), custom_call_target="tpu_custom_call" | custom-call | flops 4000000000 | tf_op jit(solution)/shard_map/pallas_call | solution.py:624
  71.7 3.0 %collective-permute-start.17 = (f32[3,6,4,128]{3,2,1,0:T(4,128)S(1)}, f32[3,6,4,128]{3,2,1,0:T(4,128)S(1)}, u32[]{:S(2)}, u32[]{:S(2)}) collective-permute-start(f32[3,6,4,128]{3,2,1,0:T(4,128)S(1)} %pad_maximum_fusion.8), channel_id=1, source_target_pairs={{0,4},{4,0},{1,5},{5,1},{2,6},{6,2},{3,7},{7,3},{8,12},{12,8},{9,1... | collective-permute-start | bytes 110600 | tf_op jit(solution)/shard_map/ppermute | solution.py:525
  74.7 1.9 %collective-permute-done.17 = f32[3,6,4,128]{3,2,1,0:T(4,128)S(1)} collective-permute-done((f32[3,6,4,128]{3,2,1,0:T(4,128)S(1)}, f32[3,6,4,128]{3,2,1,0:T(4,128)S(1)}, u32[]{:S(2)}, u32[]{:S(2)}) %collective-permute-start.17) | collective-permute-done | bytes 36896 | tf_op jit(solution)/shard_map/ppermute | solution.py:525
  76.7 0.1 collective-permute-start.18
  76.8 1.7 %collective-permute-start.19 = (f32[2,3,6,4,128]{4,3,2,1,0:T(4,128)S(1)}, f32[2,3,6,4,128]{4,3,2,1,0:T(4,128)S(1)}, u32[]{:S(2)}, u32[]{:S(2)}) collective-permute-start(f32[2,3,6,4,128]{4,3,2,1,0:T(4,128)S(1)} %pad_maximum_fusion.3.refs_10_), channel_id=1, source_target_pairs={{1,0},{2,1},{3,2},{0,3},{5,4},{6,5},{7,6},{4,7},{9,8},{10,9},{11,1... | collective-permute-start | bytes 221192 | tf_op jit(solution)/shard_map/ppermute | solution.py:528
  78.5 2.2 %shard_map.102 = (f32[6,16,128]{2,1,0:T(8,128)S(1)}, f32[6,16,128]{2,1,0:T(8,128)S(1)}) custom-call(s32[2,144]{1,0:T(2,128)S(1)} %get-tuple-element.51.tiles.refs_1_, s32[3]{0:T(128)S(1)} %get-tuple-element.52.refs_1_.sizes.refs_2_, f32[3,16,128]{2,1,0:T(8,128)S(1)} %get-tuple-element.53.place.refs_3_, ...), custom_call_target="tpu_custom_call" | custom-call | flops 4000000000 | tf_op jit(solution)/shard_map/pallas_call | solution.py:628
  80.7 0.2 collective-permute-done.18.refs_9_
  80.9 0.0 collective-permute-done.19.refs_11_
  80.9 1.8 %shard_map.103 = (f32[6,4,128]{2,1,0:T(4,128)S(1)}, f32[6,128,128]{2,1,0:T(8,128)S(1)}, f32[768,128]{1,0:T(8,128)S(1)}) custom-call(s32[2,144]{1,0:T(2,128)S(1)} %get-tuple-element.50.refs_0_, s32[3]{0:T(128)S(1)} %get-tuple-element.52.refs_1_.sizes.refs_2_, s32[4]{0:T(128)S(1)} %bitcast.50, f32[3,16,128]{2,1,0:T(8,128)S(1)} %get-tuple-element.53.place.refs_3_, ...), custom_call_target="tpu_custom_call" | custom-call | tf_op jit(solution)/shard_map/pallas_call | solution.py:619
  82.7 0.1 collective-permute-start.20
  82.8 3.8 %collective-permute-start.21 = (f32[6,4,128]{2,1,0:T(4,128)S(1)}, f32[6,4,128]{2,1,0:T(4,128)S(1)}, u32[]{:S(2)}, u32[]{:S(2)}) collective-permute-start(f32[6,4,128]{2,1,0:T(4,128)S(1)} %get-tuple-element.88), channel_id=1, source_target_pairs={{8,0},{16,8},{24,16},{0,24},{9,1},{17,9},{25,17},{1,25},{10,2},{18... | collective-permute-start | bytes 36872 | tf_op jit(solution)/shard_map/ppermute | solution.py:528
  86.6 2.1 %shard_map.104.sums_in = f32[768,128]{1,0:T(8,128)S(1)} custom-call(s32[2,144]{1,0:T(2,128)S(1)} %get-tuple-element.51.tiles.refs_1_, s32[3]{0:T(128)S(1)} %get-tuple-element.52.refs_1_.sizes.refs_2_, f32[128,3,8,128]{3,2,1,0:T(8,128)S(1)} %get-tuple-element.60.factors.refs_6_, bf16[128,256,128]{2,1,0:T(8,128)(2,1)S(1)} %get-tuple-element.66.matrix.refs_8_, ...), custom_call_target="tpu_custom_call" | custom-call | flops 4000000000 | tf_op jit(solution)/shard_map/pallas_call | solution.py:624
  88.6 0.0 collective-permute-done.20
  88.7 2.4 %collective-permute-start.22 = (f32[3,6,4,128]{3,2,1,0:T(4,128)S(1)}, f32[3,6,4,128]{3,2,1,0:T(4,128)S(1)}, u32[]{:S(2)}, u32[]{:S(2)}) collective-permute-start(f32[3,6,4,128]{3,2,1,0:T(4,128)S(1)} %pad_maximum_fusion.9), channel_id=1, source_target_pairs={{0,4},{4,0},{1,5},{5,1},{2,6},{6,2},{3,7},{7,3},{8,12},{12,8},{9,1... | collective-permute-start | bytes 110600 | tf_op jit(solution)/shard_map/ppermute | solution.py:525
  91.1 1.9 %collective-permute-done.22 = f32[3,6,4,128]{3,2,1,0:T(4,128)S(1)} collective-permute-done((f32[3,6,4,128]{3,2,1,0:T(4,128)S(1)}, f32[3,6,4,128]{3,2,1,0:T(4,128)S(1)}, u32[]{:S(2)}, u32[]{:S(2)}) %collective-permute-start.22) | collective-permute-done | bytes 36896 | tf_op jit(solution)/shard_map/ppermute | solution.py:525
  93.0 0.1 collective-permute-start.23
  93.1 1.7 %collective-permute-start.24 = (f32[2,3,6,4,128]{4,3,2,1,0:T(4,128)S(1)}, f32[2,3,6,4,128]{4,3,2,1,0:T(4,128)S(1)}, u32[]{:S(2)}, u32[]{:S(2)}) collective-permute-start(f32[2,3,6,4,128]{4,3,2,1,0:T(4,128)S(1)} %pad_maximum_fusion.4.refs_16_), channel_id=1, source_target_pairs={{1,0},{2,1},{3,2},{0,3},{5,4},{6,5},{7,6},{4,7},{9,8},{10,9},{11,1... | collective-permute-start | bytes 221192 | tf_op jit(solution)/shard_map/ppermute | solution.py:528
  94.8 2.2 %shard_map.105 = (f32[6,16,128]{2,1,0:T(8,128)S(1)}, f32[6,16,128]{2,1,0:T(8,128)S(1)}) custom-call(s32[2,144]{1,0:T(2,128)S(1)} %get-tuple-element.51.tiles.refs_1_, s32[3]{0:T(128)S(1)} %get-tuple-element.52.refs_1_.sizes.refs_2_, f32[3,16,128]{2,1,0:T(8,128)S(1)} %get-tuple-element.53.place.refs_3_, ...), custom_call_target="tpu_custom_call" | custom-call | flops 4000000000 | tf_op jit(solution)/shard_map/pallas_call | solution.py:628
  97.0 0.0 collective-permute-done.23.refs_15_
  97.1 0.0 collective-permute-done.24.refs_17_
  97.1 5.7 %shard_map.106 = f32[32,128]{1,0:T(8,128)} custom-call(s32[2,144]{1,0:T(2,128)S(1)} %get-tuple-element.50.refs_0_, s32[2,144]{1,0:T(2,128)S(1)} %get-tuple-element.51.tiles.refs_1_, s32[3]{0:T(128)S(1)} %get-tuple-element.52.refs_1_.sizes.refs_2_, f32[3,16,128]{2,1,0:T(8,128)S(1)} %get-tuple-element.53.place.refs_3_, ...), custom_call_target="tpu_custom_call" | custom-call | tf_op jit(solution)/shard_map/pallas_call | solution.py:634
  102.7 6.2 %all-to-all-start = ((f32[32,1,128]{2,1,0:T(1,128)}), f32[32,1,128]{2,1,0:T(1,128)S(1)}, u32[]{:S(2)}, u32[]{:S(2)}) async-start(f32[32,1,128]{2,1,0:T(1,128)} %bitcast.35), calls=%async_computation | async-start | bytes 32768 | tf_op jit(solution)/shard_map/all_to_all | solution.py:642
  108.9 2.4 %shard_map.107.refs_3_ = s32[16,128]{1,0:T(8,128)S(1)} custom-call(s32[16,128]{1,0:T(8,128)S(1)} %get-tuple-element.94.order), custom_call_target="tpu_custom_call" | custom-call | flops 4000000000 | tf_op jit(solution)/shard_map/pallas_call | solution.py:595
  111.4 4.6 %all-to-all-done = f32[32,1,128]{2,1,0:T(1,128)S(1)} async-done(((f32[32,1,128]{2,1,0:T(1,128)}), f32[32,1,128]{2,1,0:T(1,128)S(1)}, u32[]{:S(2)}, u32[]{:S(2)}) %all-to-all-start) | async-done | bytes 16416 | tf_op jit(solution)/shard_map/all_to_all | solution.py:642
  116.0 1.3 %shard_map.108 = f32[6,16,128]{2,1,0:T(8,128)} custom-call(f32[32,128]{1,0:T(8,128)S(1)} %bitcast.43, f32[6,16,128]{2,1,0:T(8,128)S(1)} %shard_map.96.refs_8_.own.induced, f32[6,16,128]{2,1,0:T(8,128)S(1)} %get-tuple-element.78.refs_8_.own.refs_12_.refs_0_, f32[6,16,128]{2,1,0:T(8,128)S(1)} %get-tuple-element.85.refs_8_.own.refs_13_.refs_1_, ...), custom_call_target="tpu_custom_call" | custom-call | tf_op jit(solution)/shard_map/pallas_call | solution.py:643
  (22 shorter events, 0.2 us)
Async XLA Ops:
  0.0 18.5 %copy-start = (s32[1,1,1,4]{3,2,1,0:T(1,128)S(1)}, s32[1,1,1,4]{3,2,1,0:T(1,128)}, u32[]{:S(2)}) copy-start(s32[1,1,1,4]{3,2,1,0:T(1,128)} %param.15) | copy-start | bytes 52
  0.0 13.8 %copy-start.1 = (s32[3,1,1,1,128]{4,3,2,1,0:T(1,128)S(1)}, s32[3,1,1,1,128]{4,3,2,1,0:T(1,128)}, u32[]{:S(2)}) copy-start(s32[3,1,1,1,128]{4,3,2,1,0:T(1,128)} %param.16) | copy-start | bytes 4612
  1.5 6.6 %collective-permute-start.1 = (f32[11,4,128]{2,1,0:T(4,128)S(1)}, f32[11,4,128]{2,1,0:T(4,128)S(1)}, u32[]{:S(2)}, u32[]{:S(2)}) collective-permute-start(f32[11,4,128]{2,1,0:T(4,128)S(1)} %get-tuple-element.57), channel_id=1, source_target_pairs={{8,0},{16,8},{24,16},{0,24},{9,1},{17,9},{25,17},{1,25},{10,2},{18... | collective-permute-start | bytes 67592 | tf_op jit(solution)/shard_map/ppermute | solution.py:528
  6.7 5.6 %collective-permute-start = (f32[11,4,128]{2,1,0:T(4,128)S(1)}, f32[11,4,128]{2,1,0:T(4,128)S(1)}, u32[]{:S(2)}, u32[]{:S(2)}) collective-permute-start(f32[11,4,128]{2,1,0:T(4,128)S(1)} %get-tuple-element.57), channel_id=1, source_target_pairs={{0,8},{8,16},{16,24},{24,0},{1,9},{9,17},{17,25},{25,1},{2,10},{10... | collective-permute-start | bytes 67592 | tf_op jit(solution)/shard_map/ppermute | solution.py:525
  12.3 4.4 %collective-permute-start.2 = (f32[3,11,4,128]{3,2,1,0:T(4,128)S(1)}, f32[3,11,4,128]{3,2,1,0:T(4,128)S(1)}, u32[]{:S(2)}, u32[]{:S(2)}) collective-permute-start(f32[3,11,4,128]{3,2,1,0:T(4,128)S(1)} %pad_maximum_fusion.5), channel_id=1, source_target_pairs={{0,4},{4,0},{1,5},{5,1},{2,6},{6,2},{3,7},{7,3},{8,12},{12,8},{9,1... | collective-permute-start | bytes 202760 | tf_op jit(solution)/shard_map/ppermute | solution.py:525
  16.7 5.5 %collective-permute-start.3 = (f32[2,3,11,4,128]{4,3,2,1,0:T(4,128)S(1)}, f32[2,3,11,4,128]{4,3,2,1,0:T(4,128)S(1)}, u32[]{:S(2)}, u32[]{:S(2)}) collective-permute-start(f32[2,3,11,4,128]{4,3,2,1,0:T(4,128)S(1)} %pad_maximum_fusion.refs_9_), channel_id=1, source_target_pairs={{0,1},{1,2},{2,3},{3,0},{4,5},{5,6},{6,7},{7,4},{8,9},{9,10},{10,1... | collective-permute-start | bytes 405512 | tf_op jit(solution)/shard_map/ppermute | solution.py:525
  16.7 5.4 %collective-permute-start.4 = (f32[2,3,11,4,128]{4,3,2,1,0:T(4,128)S(1)}, f32[2,3,11,4,128]{4,3,2,1,0:T(4,128)S(1)}, u32[]{:S(2)}, u32[]{:S(2)}) collective-permute-start(f32[2,3,11,4,128]{4,3,2,1,0:T(4,128)S(1)} %pad_maximum_fusion.refs_9_), channel_id=1, source_target_pairs={{1,0},{2,1},{3,2},{0,3},{5,4},{6,5},{7,6},{4,7},{9,8},{10,9},{11,1... | collective-permute-start | bytes 405512 | tf_op jit(solution)/shard_map/ppermute | solution.py:528
  26.6 8.6 %collective-permute-start.5 = (f32[6,4,128]{2,1,0:T(4,128)S(1)}, f32[6,4,128]{2,1,0:T(4,128)S(1)}, u32[]{:S(2)}, u32[]{:S(2)}) collective-permute-start(f32[6,4,128]{2,1,0:T(4,128)S(1)} %get-tuple-element.62), channel_id=1, source_target_pairs={{0,8},{8,16},{16,24},{24,0},{1,9},{9,17},{17,25},{25,1},{2,10},{10... | collective-permute-start | bytes 36872 | tf_op jit(solution)/shard_map/ppermute | solution.py:525
  26.7 8.6 %collective-permute-start.6 = (f32[6,4,128]{2,1,0:T(4,128)S(1)}, f32[6,4,128]{2,1,0:T(4,128)S(1)}, u32[]{:S(2)}, u32[]{:S(2)}) collective-permute-start(f32[6,4,128]{2,1,0:T(4,128)S(1)} %get-tuple-element.62), channel_id=1, source_target_pairs={{8,0},{16,8},{24,16},{0,24},{9,1},{17,9},{25,17},{1,25},{10,2},{18... | collective-permute-start | bytes 36872 | tf_op jit(solution)/shard_map/ppermute | solution.py:528
  35.2 4.2 %collective-permute-start.7 = (f32[3,6,4,128]{3,2,1,0:T(4,128)S(1)}, f32[3,6,4,128]{3,2,1,0:T(4,128)S(1)}, u32[]{:S(2)}, u32[]{:S(2)}) collective-permute-start(f32[3,6,4,128]{3,2,1,0:T(4,128)S(1)} %pad_maximum_fusion.6), channel_id=1, source_target_pairs={{0,4},{4,0},{1,5},{5,1},{2,6},{6,2},{3,7},{7,3},{8,12},{12,8},{9,1... | collective-permute-start | bytes 110600 | tf_op jit(solution)/shard_map/ppermute | solution.py:525
  39.4 7.3 %collective-permute-start.8 = (f32[2,3,6,4,128]{4,3,2,1,0:T(4,128)S(1)}, f32[2,3,6,4,128]{4,3,2,1,0:T(4,128)S(1)}, u32[]{:S(2)}, u32[]{:S(2)}) collective-permute-start(f32[2,3,6,4,128]{4,3,2,1,0:T(4,128)S(1)} %pad_maximum_fusion.1.refs_10_), channel_id=1, source_target_pairs={{0,1},{1,2},{2,3},{3,0},{4,5},{5,6},{6,7},{7,4},{8,9},{9,10},{10,1... | collective-permute-start | bytes 221192 | tf_op jit(solution)/shard_map/ppermute | solution.py:525
  39.5 7.3 %collective-permute-start.9 = (f32[2,3,6,4,128]{4,3,2,1,0:T(4,128)S(1)}, f32[2,3,6,4,128]{4,3,2,1,0:T(4,128)S(1)}, u32[]{:S(2)}, u32[]{:S(2)}) collective-permute-start(f32[2,3,6,4,128]{4,3,2,1,0:T(4,128)S(1)} %pad_maximum_fusion.1.refs_10_), channel_id=1, source_target_pairs={{1,0},{2,1},{3,2},{0,3},{5,4},{6,5},{7,6},{4,7},{9,8},{10,9},{11,1... | collective-permute-start | bytes 221192 | tf_op jit(solution)/shard_map/ppermute | solution.py:528
  48.6 6.0 %collective-permute-start.10 = (f32[6,4,128]{2,1,0:T(4,128)S(1)}, f32[6,4,128]{2,1,0:T(4,128)S(1)}, u32[]{:S(2)}, u32[]{:S(2)}) collective-permute-start(f32[6,4,128]{2,1,0:T(4,128)S(1)} %get-tuple-element.74), channel_id=1, source_target_pairs={{0,8},{8,16},{16,24},{24,0},{1,9},{9,17},{17,25},{25,1},{2,10},{10... | collective-permute-start | bytes 36872 | tf_op jit(solution)/shard_map/ppermute | solution.py:525
  48.6 5.9 %collective-permute-start.11 = (f32[6,4,128]{2,1,0:T(4,128)S(1)}, f32[6,4,128]{2,1,0:T(4,128)S(1)}, u32[]{:S(2)}, u32[]{:S(2)}) collective-permute-start(f32[6,4,128]{2,1,0:T(4,128)S(1)} %get-tuple-element.74), channel_id=1, source_target_pairs={{8,0},{16,8},{24,16},{0,24},{9,1},{17,9},{25,17},{1,25},{10,2},{18... | collective-permute-start | bytes 36872 | tf_op jit(solution)/shard_map/ppermute | solution.py:528
  54.6 5.3 %collective-permute-start.12 = (f32[3,6,4,128]{3,2,1,0:T(4,128)S(1)}, f32[3,6,4,128]{3,2,1,0:T(4,128)S(1)}, u32[]{:S(2)}, u32[]{:S(2)}) collective-permute-start(f32[3,6,4,128]{3,2,1,0:T(4,128)S(1)} %pad_maximum_fusion.7), channel_id=1, source_target_pairs={{0,4},{4,0},{1,5},{5,1},{2,6},{6,2},{3,7},{7,3},{8,12},{12,8},{9,1... | collective-permute-start | bytes 110600 | tf_op jit(solution)/shard_map/ppermute | solution.py:525
  59.9 4.1 %collective-permute-start.13 = (f32[2,3,6,4,128]{4,3,2,1,0:T(4,128)S(1)}, f32[2,3,6,4,128]{4,3,2,1,0:T(4,128)S(1)}, u32[]{:S(2)}, u32[]{:S(2)}) collective-permute-start(f32[2,3,6,4,128]{4,3,2,1,0:T(4,128)S(1)} %pad_maximum_fusion.2.refs_10_), channel_id=1, source_target_pairs={{0,1},{1,2},{2,3},{3,0},{4,5},{5,6},{6,7},{7,4},{8,9},{9,10},{10,1... | collective-permute-start | bytes 221192 | tf_op jit(solution)/shard_map/ppermute | solution.py:525
  60.0 4.0 %collective-permute-start.14 = (f32[2,3,6,4,128]{4,3,2,1,0:T(4,128)S(1)}, f32[2,3,6,4,128]{4,3,2,1,0:T(4,128)S(1)}, u32[]{:S(2)}, u32[]{:S(2)}) collective-permute-start(f32[2,3,6,4,128]{4,3,2,1,0:T(4,128)S(1)} %pad_maximum_fusion.2.refs_10_), channel_id=1, source_target_pairs={{1,0},{2,1},{3,2},{0,3},{5,4},{6,5},{7,6},{4,7},{9,8},{10,9},{11,1... | collective-permute-start | bytes 221192 | tf_op jit(solution)/shard_map/ppermute | solution.py:528
  65.7 6.0 %collective-permute-start.15 = (f32[6,4,128]{2,1,0:T(4,128)S(1)}, f32[6,4,128]{2,1,0:T(4,128)S(1)}, u32[]{:S(2)}, u32[]{:S(2)}) collective-permute-start(f32[6,4,128]{2,1,0:T(4,128)S(1)} %get-tuple-element.81), channel_id=1, source_target_pairs={{0,8},{8,16},{16,24},{24,0},{1,9},{9,17},{17,25},{25,1},{2,10},{10... | collective-permute-start | bytes 36872 | tf_op jit(solution)/shard_map/ppermute | solution.py:525
  65.8 5.9 %collective-permute-start.16 = (f32[6,4,128]{2,1,0:T(4,128)S(1)}, f32[6,4,128]{2,1,0:T(4,128)S(1)}, u32[]{:S(2)}, u32[]{:S(2)}) collective-permute-start(f32[6,4,128]{2,1,0:T(4,128)S(1)} %get-tuple-element.81), channel_id=1, source_target_pairs={{8,0},{16,8},{24,16},{0,24},{9,1},{17,9},{25,17},{1,25},{10,2},{18... | collective-permute-start | bytes 36872 | tf_op jit(solution)/shard_map/ppermute | solution.py:528
  71.7 4.9 %collective-permute-start.17 = (f32[3,6,4,128]{3,2,1,0:T(4,128)S(1)}, f32[3,6,4,128]{3,2,1,0:T(4,128)S(1)}, u32[]{:S(2)}, u32[]{:S(2)}) collective-permute-start(f32[3,6,4,128]{3,2,1,0:T(4,128)S(1)} %pad_maximum_fusion.8), channel_id=1, source_target_pairs={{0,4},{4,0},{1,5},{5,1},{2,6},{6,2},{3,7},{7,3},{8,12},{12,8},{9,1... | collective-permute-start | bytes 110600 | tf_op jit(solution)/shard_map/ppermute | solution.py:525
  76.7 4.2 %collective-permute-start.18 = (f32[2,3,6,4,128]{4,3,2,1,0:T(4,128)S(1)}, f32[2,3,6,4,128]{4,3,2,1,0:T(4,128)S(1)}, u32[]{:S(2)}, u32[]{:S(2)}) collective-permute-start(f32[2,3,6,4,128]{4,3,2,1,0:T(4,128)S(1)} %pad_maximum_fusion.3.refs_10_), channel_id=1, source_target_pairs={{0,1},{1,2},{2,3},{3,0},{4,5},{5,6},{6,7},{7,4},{8,9},{9,10},{10,1... | collective-permute-start | bytes 221192 | tf_op jit(solution)/shard_map/ppermute | solution.py:525
  76.8 4.1 %collective-permute-start.19 = (f32[2,3,6,4,128]{4,3,2,1,0:T(4,128)S(1)}, f32[2,3,6,4,128]{4,3,2,1,0:T(4,128)S(1)}, u32[]{:S(2)}, u32[]{:S(2)}) collective-permute-start(f32[2,3,6,4,128]{4,3,2,1,0:T(4,128)S(1)} %pad_maximum_fusion.3.refs_10_), channel_id=1, source_target_pairs={{1,0},{2,1},{3,2},{0,3},{5,4},{6,5},{7,6},{4,7},{9,8},{10,9},{11,1... | collective-permute-start | bytes 221192 | tf_op jit(solution)/shard_map/ppermute | solution.py:528
  82.7 6.0 %collective-permute-start.20 = (f32[6,4,128]{2,1,0:T(4,128)S(1)}, f32[6,4,128]{2,1,0:T(4,128)S(1)}, u32[]{:S(2)}, u32[]{:S(2)}) collective-permute-start(f32[6,4,128]{2,1,0:T(4,128)S(1)} %get-tuple-element.88), channel_id=1, source_target_pairs={{0,8},{8,16},{16,24},{24,0},{1,9},{9,17},{17,25},{25,1},{2,10},{10... | collective-permute-start | bytes 36872 | tf_op jit(solution)/shard_map/ppermute | solution.py:525
  82.8 5.9 %collective-permute-start.21 = (f32[6,4,128]{2,1,0:T(4,128)S(1)}, f32[6,4,128]{2,1,0:T(4,128)S(1)}, u32[]{:S(2)}, u32[]{:S(2)}) collective-permute-start(f32[6,4,128]{2,1,0:T(4,128)S(1)} %get-tuple-element.88), channel_id=1, source_target_pairs={{8,0},{16,8},{24,16},{0,24},{9,1},{17,9},{25,17},{1,25},{10,2},{18... | collective-permute-start | bytes 36872 | tf_op jit(solution)/shard_map/ppermute | solution.py:528
  88.7 4.3 %collective-permute-start.22 = (f32[3,6,4,128]{3,2,1,0:T(4,128)S(1)}, f32[3,6,4,128]{3,2,1,0:T(4,128)S(1)}, u32[]{:S(2)}, u32[]{:S(2)}) collective-permute-start(f32[3,6,4,128]{3,2,1,0:T(4,128)S(1)} %pad_maximum_fusion.9), channel_id=1, source_target_pairs={{0,4},{4,0},{1,5},{5,1},{2,6},{6,2},{3,7},{7,3},{8,12},{12,8},{9,1... | collective-permute-start | bytes 110600 | tf_op jit(solution)/shard_map/ppermute | solution.py:525
  93.0 4.0 %collective-permute-start.23 = (f32[2,3,6,4,128]{4,3,2,1,0:T(4,128)S(1)}, f32[2,3,6,4,128]{4,3,2,1,0:T(4,128)S(1)}, u32[]{:S(2)}, u32[]{:S(2)}) collective-permute-start(f32[2,3,6,4,128]{4,3,2,1,0:T(4,128)S(1)} %pad_maximum_fusion.4.refs_16_), channel_id=1, source_target_pairs={{0,1},{1,2},{2,3},{3,0},{4,5},{5,6},{6,7},{7,4},{8,9},{9,10},{10,1... | collective-permute-start | bytes 221192 | tf_op jit(solution)/shard_map/ppermute | solution.py:525
  93.1 4.0 %collective-permute-start.24 = (f32[2,3,6,4,128]{4,3,2,1,0:T(4,128)S(1)}, f32[2,3,6,4,128]{4,3,2,1,0:T(4,128)S(1)}, u32[]{:S(2)}, u32[]{:S(2)}) collective-permute-start(f32[2,3,6,4,128]{4,3,2,1,0:T(4,128)S(1)} %pad_maximum_fusion.4.refs_16_), channel_id=1, source_target_pairs={{1,0},{2,1},{3,2},{0,3},{5,4},{6,5},{7,6},{4,7},{9,8},{10,9},{11,1... | collective-permute-start | bytes 221192 | tf_op jit(solution)/shard_map/ppermute | solution.py:528
  102.7 13.3 %all-to-all-start = ((f32[32,1,128]{2,1,0:T(1,128)}), f32[32,1,128]{2,1,0:T(1,128)S(1)}, u32[]{:S(2)}, u32[]{:S(2)}) async-start(f32[32,1,128]{2,1,0:T(1,128)} %bitcast.35), calls=%async_computation | async-start | bytes 32768 | tf_op jit(solution)/shard_map/all_to_all | solution.py:642

commit v3 on v2

--- a/solution.py
+++ b/solution.py
@@ -10,10 +10,10 @@
 BRICK = 6.0
 STATES = 2
 WIDTH = STATES * 3 * 8
-QWIDTH = STATES * 8
+QWIDTH = STATES * 4
 PARTS = 12
 UNROLL = 16
-WEIGH_UNROLL = 8
+WIDE = 32
 HIDDEN = 4_000_000_000
 F32 = jnp.float32
 BF16 = jnp.bfloat16
@@ -149,6 +149,10 @@
         for b in range(3):
             value = line * jnp.where(outer, 3.0 * ys[b], 1.0)
             factors[r, b] = value - jnp.where(sub == 4 + b, far, 0.0)
+        line = jnp.ones_like(line)
+        for k in range(3):
+            line = jnp.where(sub % 4 == 1 + k, ys[k], line)
+        factors[r, 3] = line
         return carry
 
     lax.fori_loop(0, y.shape[1], one, None, unroll=4)
@@ -162,9 +166,10 @@
 
 
 def charge_columns(factors, charges, row):
-    line = factors[row, 0]
-    block = jnp.concatenate([line * spread_row(charges, s, row) for s in range(STATES)], axis=0)
-    return jnp.concatenate(thirds(block), axis=0).astype(BF16)
+    sub = lax.broadcasted_iota(jnp.int32, (8, LANES), 0)
+    both = jnp.where(sub < 4, spread_row(charges, 0, row), spread_row(charges, 1, row))
+    pieces = thirds(factors[row, 3] * both) + (jnp.zeros_like(both),)
+    return jnp.concatenate(pieces, axis=0).astype(BF16)
 
 
 def apply(left, right, width):
@@ -239,7 +244,7 @@
     return jnp.concatenate(groups, axis=0).astype(BF16)
 
 
-def plan_kernel(tiles, count, border_ids, near, rest, sizes, selves, flags, pairs):
+def plan_kernel(tiles, count, border_ids, sign, near, rest, sizes, selves, flags, pairs):
     clusters = selves.shape[0]
     border = border_ids.shape[0]
     tile_num = tiles.shape[1]
@@ -250,9 +255,14 @@
     for b in range(border):
         flags[border_ids[b]] = 1
 
+    middle = 13 + 9 * sign[0] + 3 * sign[1] + sign[2]
+    of_ninth, of_third = 9 * (sign[0] - sign[1]), 3 * (sign[1] - sign[2])
+
     def place_tile(t, ends):
         recv, slot, source = tiles[0, t], tiles[1, t], tiles[2, t]
-        row = jnp.where(slot == 13, source, clusters + slot * border + source)
+        ninth, third = (slot * 57) >> 9, (slot * 43) >> 7
+        spot = middle - of_ninth * ninth - of_third * third - sign[2] * slot
+        row = jnp.where(slot == 13, source, clusters + spot * border + source)
         used = (t < count[0]).astype(jnp.int32)
         seen = flags[recv]
         for which, target in enumerate((near, rest)):
@@ -262,12 +272,13 @@
         pairs[recv] = pairs[recv] + used * same
         return ends[0] + used * seen, ends[1] + used * (1 - seen)
 
-    ends = lax.fori_loop(0, tile_num, place_tile, (jnp.int32(0), jnp.int32(0)))
+    ends = lax.fori_loop(0, tile_num, place_tile, (jnp.int32(0), jnp.int32(0)), unroll=4)
     for which, target in enumerate((near, rest)):
-        for u in range(UNROLL):
+        for u in range(WIDE):
             target[0, ends[which] + u] = 0
             target[1, ends[which] + u] = dummy
-        sizes[which] = (ends[which] + UNROLL - 1) // UNROLL
+        step = (UNROLL, WIDE)[which]
+        sizes[which] = (ends[which] + step - 1) // step
     sizes[2] = (sizes[1] + 1) // 2
     for c in range(clusters):
         selves[c : c + 1, :] = jnp.full((1, LANES), pairs[c].astype(F32))
@@ -289,17 +300,17 @@
     lax.fori_loop(0, place.shape[1], turn, None, unroll=8)
 
 
-def over_tiles(groups, body, unroll=UNROLL):
+def over_tiles(groups, body, step, unroll):
     def one(i, carry):
         for u in range(unroll):
             body(i * unroll + u)
         return carry
 
     first, end = groups if isinstance(groups, tuple) else (0, groups)
-    lax.fori_loop(first * (UNROLL // unroll), end * (UNROLL // unroll), one, None)
-
-
-def weigh_tiles(tiles, groups, turned, pieces, matrix, cubes):
+    lax.fori_loop(first * (step // unroll), end * (step // unroll), one, None)
+
+
+def weigh_tiles(tiles, groups, step, turned, pieces, matrix, cubes):
     def one(t):
         recv, row = tiles[0, t], tiles[1, t]
         squared = jnp.dot(
@@ -314,10 +325,10 @@
             target[t, 0:LANES, :] = high
             target[t, LANES:, :] = (value - high.astype(F32)).astype(BF16)
 
-    over_tiles(groups, one, WEIGH_UNROLL)
-
-
-def apply_tiles(tiles, groups, factors, sources, matrix, sums, charges=None, cubes=None, sums_q=None):
+    over_tiles(groups, one, step, UNROLL)
+
+
+def apply_tiles(tiles, groups, step, factors, sources, matrix, sums, charges=None, cubes=None, sums_q=None):
     def one(t):
         recv, row = tiles[0, t], tiles[1, t]
         add_tile(sums, recv, WIDTH, apply(columns(factors, sources, row), matrix[t], WIDTH))
@@ -325,7 +336,7 @@
             left = charge_columns(factors, charges, row)
             add_tile(sums_q, recv, QWIDTH, apply(left, cubes[t], QWIDTH))
 
-    over_tiles(groups, one)
+    over_tiles(groups, one, step, step)
 
 
 def permanent(sums, sums_q, place, multi, selves):
@@ -334,7 +345,7 @@
     fields = combine(sums, x, [multi[2 + k] for k in range(6)], selves[...])
     for s in range(STATES):
         def col(c):
-            return sums_q[pl.ds(s * 8 + c, clusters, stride=QWIDTH), :]
+            return sums_q[pl.ds(s * 4 + c, clusters, stride=QWIDTH), :]
 
         whole = col(0)
         for b in range(3):
@@ -361,13 +372,14 @@
 
 
 def first_near_kernel(where, parts_of, *refs):
-    tiles, sizes, border_ids, place, multi, response, turned, selves = refs[:8]
-    halo = refs[8 : 8 + parts_of]
+    tiles, sizes, border_ids, sign, place, multi, response, turned, selves = refs[:9]
+    halo = refs[9 : 9 + parts_of]
     (outgoing, matrix, factors, pieces, moments, charges, sums, sums_q,
-     y, cubes, held) = refs[8 + parts_of :]
+     y, cubes, held) = refs[9 + parts_of :]
     border = outgoing.shape[1]
+    reach = [BRICK * sign[a].astype(F32) for a in range(3)]
     moves = [
-        tuple(BRICK * o for o in (slot // 9 - 1, slot // 3 % 3 - 1, slot % 3 - 1))
+        [reach[a] * (1 - slot // scale % 3) for a, scale in enumerate((9, 3, 1))]
         for slot in range(27)
     ]
     own = Stack([place[k] for k in range(3)] + [multi[k] for k in range(8)])
@@ -378,8 +390,8 @@
     write_parts(pieces, y)
     sums[...] = jnp.zeros_like(sums)
     sums_q[...] = jnp.zeros_like(sums_q)
-    weigh_tiles(tiles, sizes[0], turned, pieces, matrix, cubes)
-    apply_tiles(tiles, sizes[0], factors, moments, matrix, sums, charges, cubes, sums_q)
+    weigh_tiles(tiles, sizes[0], UNROLL, turned, pieces, matrix, cubes)
+    apply_tiles(tiles, sizes[0], UNROLL, factors, moments, matrix, sums, charges, cubes, sums_q)
     fields = permanent(sums, sums_q, place, multi, selves)
     send_border(
         [response[k // 3] * fields[k] for k in range(6)], held, outgoing, border_ids
@@ -387,14 +399,14 @@
 
 
 def first_weigh_kernel(tiles, sizes, turned, pieces, matrix, cubes):
-    weigh_tiles(tiles, sizes[1], turned, pieces, matrix, cubes)
+    weigh_tiles(tiles, sizes[1], WIDE, turned, pieces, matrix, cubes)
 
 
 def first_rest_kernel(tiles, sizes, place, multi, response, selves, factors,
                       moments, charges, matrix, cubes, sums_in, sums_q_in, induced, sums, sums_q):
     sums[...] = sums_in[...]
     sums_q[...] = sums_q_in[...]
-    apply_tiles(tiles, sizes[1], factors, moments, matrix, sums, charges, cubes, sums_q)
+    apply_tiles(tiles, sizes[1], WIDE, factors, moments, matrix, sums, charges, cubes, sums_q)
     fields = permanent(sums, sums_q, place, multi, selves)
     for k in range(6):
         induced[k] = response[k // 3] * fields[k]
@@ -406,7 +418,7 @@
     outgoing, sources, sums, held = refs[9 + parts_of :]
     collect(sources, 0, own, halo, where, outgoing.shape[1])
     sums[...] = jnp.zeros_like(sums)
-    apply_tiles(tiles, sizes[0], factors, sources, matrix, sums)
+    apply_tiles(tiles, sizes[0], UNROLL, factors, sources, matrix, sums)
     x = [place[k] for k in range(3)]
     fields = combine(sums, x, [own[k] for k in range(6)], selves[...])
     send_border(
@@ -416,13 +428,13 @@
 
 def middle_kernel(tiles, sizes, factors, matrix, sources, sums_in, sums):
     sums[...] = sums_in[...]
-    apply_tiles(tiles, sizes[2], factors, sources, matrix, sums)
+    apply_tiles(tiles, sizes[2], WIDE, factors, sources, matrix, sums)
 
 
 def rest_kernel(tiles, sizes, place, response, selves, factors, matrix, own, sources, sums_in,
                 plain, scaled, sums):
     sums[...] = sums_in[...]
-    apply_tiles(tiles, (sizes[2], sizes[1]), factors, sources, matrix, sums)
+    apply_tiles(tiles, (sizes[2], sizes[1]), WIDE, factors, sources, matrix, sums)
     x = [place[k] for k in range(3)]
     fields = combine(sums, x, [own[k] for k in range(6)], selves[...])
     for k in range(6):
@@ -440,8 +452,8 @@
     own = scaleds[-1]
     collect(sources, 0, own, halo, where, border)
     sums[...] = jnp.zeros_like(sums)
-    apply_tiles(near, sizes[0], factors, sources, matrix_near, sums)
-    apply_tiles(rest, sizes[1], factors, sources, matrix_rest, sums)
+    apply_tiles(near, sizes[0], UNROLL, factors, sources, matrix_near, sums)
+    apply_tiles(rest, sizes[1], WIDE, factors, sources, matrix_rest, sums)
     x = [place[k] for k in range(3)]
     fields = combine(sums, x, [own[k] for k in range(6)], selves[...])
     lane = lax.broadcasted_iota(jnp.int32, (1, LANES), 1)
@@ -522,11 +534,27 @@
     count = lax.axis_size(axis)
     if count == 1:
         return [cells], (0, 0, 0)
-    below = lax.ppermute(cells, axis, [(i, (i + 1) % count) for i in range(count)])
     if count == 2:
-        return [cells, below], (1, 0, 1)
-    above = lax.ppermute(cells, axis, [((i + 1) % count, i) for i in range(count)])
-    return [below, cells, above], (0, 1, 2)
+        return [cells, lax.ppermute(cells, axis, [(0, 1), (1, 0)])], (1, 0, 1)
+    steps = [1 - 2 * (i % 2) if count % 2 == 0 else 1 for i in range(count)]
+    back = lax.ppermute(cells, axis, [((i - steps[i]) % count, i) for i in range(count)])
+    ahead = lax.ppermute(cells, axis, [((i + steps[i]) % count, i) for i in range(count)])
+    return [ahead, cells, back], (0, 1, 2)
+
+
+def signs():
+    which = lax.iota(jnp.int32, len(AXES))
+    out = jnp.zeros_like(which)
+    for a, axis in enumerate(AXES):
+        count = lax.axis_size(axis)
+        if count <= 2:
+            sign = -1
+        elif count % 2:
+            sign = 1
+        else:
+            sign = 1 - 2 * (lax.axis_index(axis) % 2)
+        out = jnp.where(which == a, sign, out)
+    return out
 
 
 def neighbours(cells, beside):
@@ -551,6 +579,7 @@
 
     border_ids = border_clusters.reshape(border)
     tiles = tile_list.reshape(3, tile_num)
+    sign = signs()
     count = tile_count.reshape(1)
     devices = 1
     for axis in AXES:
@@ -559,12 +588,12 @@
     cell = (clusters, LANES)
     vector = ((6,) + cell, F32)
     leave = ((6, border, LANES), F32)
-    listed = -(-tile_num // UNROLL) * UNROLL
+    listed = -(-tile_num // WIDE) * WIDE
     matrix = ((listed, 2 * LANES, LANES), BF16)
     table = ((6, padded, LANES), F32)
     sums = ((clusters * WIDTH, LANES), F32)
     sums_q = ((clusters * QWIDTH, LANES), F32)
-    listing = ((2, listed + UNROLL), jnp.int32)
+    listing = ((2, listed + WIDE), jnp.int32)
 
     whole, at = {}, 0
     for array in (coords, charges, dipoles, polar, perturbed, cluster_order, border_ids):
@@ -584,11 +613,11 @@
     near, rest, sizes, selves = call(
         plan_kernel,
         [listing, listing, ((3,), jnp.int32), (cell, F32)],
-        [SMEM] * 3,
+        [SMEM] * 4,
         [pltpu.SMEM((clusters,), jnp.int32)] * 2,
         outs=[SMEM] * 3 + [VMEM],
         flops=HIDDEN,
-    )(tiles, count, border_ids)
+    )(tiles, count, border_ids, sign)
     (turned,) = call(
         turn_kernel, [((clusters, LANES, LANES), BF16)], [VMEM], flops=HIDDEN
     )(place)
@@ -597,12 +626,12 @@
     halo, where, (turned,) = neighbours(outgoing, (turned,))
     (leaving, matrix_near, factors, pieces, moments, charge_rows, partial, partial_q) = call(
         lambda *refs: first_near_kernel(where, len(halo), *refs),
-        [leave, matrix, ((padded, 3, 8, LANES), F32), ((PARTS, padded, LANES), F32), table,
+        [leave, matrix, ((padded, 4, 8, LANES), F32), ((PARTS, padded, LANES), F32), table,
          ((2, padded, LANES), F32), sums, sums_q],
-        [SMEM] * 3 + [VMEM] * (5 + len(halo)),
+        [SMEM] * 4 + [VMEM] * (5 + len(halo)),
         [pltpu.VMEM((3, padded, LANES), F32), pltpu.VMEM(*matrix), pltpu.VMEM(*vector)],
         16,
-    )(near, sizes, border_ids, place, multi, response, turned, selves, *halo)
+    )(near, sizes, border_ids, sign, place, multi, response, turned, selves, *halo)
     matrix_rest, cubes = call(
         first_weigh_kernel, [matrix, matrix], [SMEM] * 2 + [VMEM] * 2, flops=HIDDEN
     )(rest, sizes, turned, pieces)

time: 117 us -> 108 us (0.923)
  starting transfers between devices: 48.3 us -> 24.1 us
  waiting for transfers between devices: 19.8 us -> 35.7 us
    ppermute x25, starting transfers between devices: 42.1 us -> 21.5 us  [the longest x10 14.4 us: ring(): lax.ppermute(cells, axis, [((i - steps[i]) % count, i) for i in range(cou...]
    ppermute x25, waiting for transfers between devices: 15.2 us -> 31 us  [the longest x5 15.1 us: ring(): return ([cells, lax.ppermute(cells, axis, [(0, 1), (1, 0)])], (1, 0, 1))]
    all_to_all x1, starting transfers between devices: 6.18 us -> 2.62 us  [shards(): grams = lax.all_to_all(gram, AXES, 0, 0, tiled=True)]
    pallas_call x3, Pallas kernels: 6.6 us -> 4.53 us  [shards(): call(rest_kernel, [vector, vector], [SMEM] * 2 + [VMEM] * 8, [pltpu.VMEM(...]
    pallas_call x3, Pallas kernels: 5.35 us -> 7.02 us  [shards(): call(lambda *refs, where=where, parts=len(halo): near_kernel(where, parts...]
  transfers between devices with their start and end apart: 26 -> 26, of which waited for: 10 -> 16; matrix products, arithmetic and copies ran while one was open for 0% -> 0% of each run, Pallas kernels for 25% -> 24%
where the time goes in v3:
time: 108 us
  Pallas kernels  46.1 us (43%)
  waiting for transfers between devices  35.7 us (33%)
  starting transfers between devices  24.1 us (22%)
    ppermute x5, waiting for transfers between devices, ring(): return ([cells, lax.ppermute(cells, axis, [(0, 1), (1, 0)])], (1, 0, 1))  15.1 us
    ppermute x10, starting transfers between devices, ring(): lax.ppermute(cells, axis, [((i - steps[i]) % count, i) for i in range(cou...  14.4 us
    ppermute x10, waiting for transfers between devices, ring(): lax.ppermute(cells, axis, [((i - steps[i]) % count, i) for i in range(cou...  13.5 us
    pallas_call x3, Pallas kernels, shards(): call(lambda *refs, where=where, parts=len(halo): near_kernel(where, parts...  7.02 us
    pallas_call x3, Pallas kernels, shards(): call(middle_kernel, [sums], [SMEM] * 2 + [VMEM] * 4, flops=HIDDEN)  6.6 us
    pallas_call x1, Pallas kernels, shards(): call(lambda *refs: last_kernel(where, len(halo), border, *refs), [((devic...  5.43 us
    pallas_call x1, Pallas kernels, shards(): call(lambda *refs: first_near_kernel(where, len(halo), *refs), [leave, ma...  5.35 us
    ppermute x5, starting transfers between devices, ring(): return ([cells, lax.ppermute(cells, axis, [(0, 1), (1, 0)])], (1, 0, 1))  5.31 us
  transfers between devices with their start and end apart: 26, of which 16 were waited for; matrix products, arithmetic and copies ran while one was open for 0% of the time, Pallas kernels for 24%

profile of v3, /device:TPU:0, one launch (start us, length us, event | category | flops | bytes accessed | tf_op | source)
XLA Modules:
  0.0 107.9 jit_solution(1270918526427831875)
XLA Ops:
  0.0 0.9 convert_add_fusion.packed
  0.9 0.6 shard_map.92
  1.5 5.1 %collective-permute-start.1 = (f32[11,4,128]{2,1,0:T(4,128)S(1)}, f32[11,4,128]{2,1,0:T(4,128)S(1)}, u32[]{:S(2)}, u32[]{:S(2)}) collective-permute-start(f32[11,4,128]{2,1,0:T(4,128)S(1)} %get-tuple-element.57), channel_id=1, source_target_pairs={{24,0},{16,8},{8,16},{0,24},{25,1},{17,9},{9,17},{1,25},{26,2},{18... | collective-permute-start | bytes 67592 | tf_op jit(solution)/shard_map/ppermute | solution.py:540
  6.7 0.6 shard_map.93.refs_7_.turned
  8.0 0.5 collective-permute-done.1
  8.4 2.0 %collective-permute-done = f32[11,4,128]{2,1,0:T(4,128)S(1)} collective-permute-done((f32[11,4,128]{2,1,0:T(4,128)S(1)}, f32[11,4,128]{2,1,0:T(4,128)S(1)}, u32[]{:S(2)}, u32[]{:S(2)}) %collective-permute-start) | collective-permute-done | bytes 22560 | tf_op jit(solution)/shard_map/ppermute | solution.py:541
  10.5 1.6 %collective-permute-start.2 = (f32[3,11,4,128]{3,2,1,0:T(4,128)S(1)}, f32[3,11,4,128]{3,2,1,0:T(4,128)S(1)}, u32[]{:S(2)}, u32[]{:S(2)}) collective-permute-start(f32[3,11,4,128]{3,2,1,0:T(4,128)S(1)} %pad_maximum_fusion.5), channel_id=1, source_target_pairs={{0,4},{4,0},{1,5},{5,1},{2,6},{6,2},{3,7},{7,3},{8,12},{12,8},{9,1... | collective-permute-start | bytes 202760 | tf_op jit(solution)/shard_map/ppermute | solution.py:538
  12.1 2.8 %collective-permute-done.2 = f32[3,11,4,128]{3,2,1,0:T(4,128)S(1)} collective-permute-done((f32[3,11,4,128]{3,2,1,0:T(4,128)S(1)}, f32[3,11,4,128]{3,2,1,0:T(4,128)S(1)}, u32[]{:S(2)}, u32[]{:S(2)}) %collective-permute-start.2) | collective-permute-done | bytes 67616 | tf_op jit(solution)/shard_map/ppermute | solution.py:538
  14.9 0.1 collective-permute-start.3
  15.0 1.6 %collective-permute-start.4 = (f32[2,3,11,4,128]{4,3,2,1,0:T(4,128)S(1)}, f32[2,3,11,4,128]{4,3,2,1,0:T(4,128)S(1)}, u32[]{:S(2)}, u32[]{:S(2)}) collective-permute-start(f32[2,3,11,4,128]{4,3,2,1,0:T(4,128)S(1)} %pad_maximum_fusion.refs_10_), channel_id=1, source_target_pairs={{3,0},{2,1},{1,2},{0,3},{7,4},{6,5},{5,6},{4,7},{11,8},{10,9},{9,1... | collective-permute-start | bytes 405512 | tf_op jit(solution)/shard_map/ppermute | solution.py:540
  16.6 3.7 %shard_map.91 = (s32[2,160]{1,0:T(2,128)S(1)}, s32[2,160]{1,0:T(2,128)S(1)}, s32[3]{0:T(128)S(1)}, f32[16,128]{1,0:T(8,128)S(1)}) custom-call(s32[3,128]{1,0:T(4,128)S(1)} %bitcast.55, s32[1]{0:T(128)} %bitcast.42.count, s32[4]{0:T(128)S(1)} %bitcast.46, s32[3]{0:T(128)S(1)} %compare_select_fusion.2.sign.refs_3_), custom_call_target="tpu_custom_call" | custom-call | flops 4000000000 | tf_op jit(solution)/shard_map/pallas_call | solution.py:613
  20.2 0.0 collective-permute-done.3.refs_9_
  20.3 0.0 collective-permute-done.4.refs_11_
  20.3 5.3 %shard_map.94 = (f32[6,4,128]{2,1,0:T(4,128)S(1)}, bf16[128,256,128]{2,1,0:T(8,128)(2,1)S(1)}, f32[128,4,8,128]{3,2,1,0:T(8,128)S(1)}, f32[12,128,128]{2,1,0:T(8...) custom-call(s32[2,160]{1,0:T(2,128)S(1)} %get-tuple-element.50.refs_, ...), custom_call_target="tpu_custom_call" | custom-call | tf_op jit(solution)/shard_map/pallas_call | solution.py:627
  25.6 0.1 collective-permute-start.5
  25.7 0.6 collective-permute-start.6
  26.3 3.8 %shard_map.95 = (bf16[128,256,128]{2,1,0:T(8,128)(2,1)S(1)}, bf16[128,256,128]{2,1,0:T(8,128)(2,1)S(1)}) custom-call(s32[2,160]{1,0:T(2,128)S(1)} %get-tuple-element.51.tiles.refs_1_, s32[3]{0:T(128)S(1)} %get-tuple-element.52.refs_1_.sizes.refs_2_, bf16[16,128,128]{2,1,0:T(8,128)(2,1)S(1)} %shard_map.93.refs_7_.turned, ...), custom_call_target="tpu_custom_call" | custom-call | flops 4000000000 | tf_op jit(solution)/shard_map/pallas_call | solution.py:635
  30.1 0.0 collective-permute-done.5
  30.1 1.2 %collective-permute-done.6 = f32[6,4,128]{2,1,0:T(4,128)S(1)} collective-permute-done((f32[6,4,128]{2,1,0:T(4,128)S(1)}, f32[6,4,128]{2,1,0:T(4,128)S(1)}, u32[]{:S(2)}, u32[]{:S(2)}) %collective-permute-start.6) | collective-permute-done | bytes 12320 | tf_op jit(solution)/shard_map/ppermute | solution.py:540
  31.3 1.6 %collective-permute-start.7 = (f32[3,6,4,128]{3,2,1,0:T(4,128)S(1)}, f32[3,6,4,128]{3,2,1,0:T(4,128)S(1)}, u32[]{:S(2)}, u32[]{:S(2)}) collective-permute-start(f32[3,6,4,128]{3,2,1,0:T(4,128)S(1)} %pad_maximum_fusion.6), channel_id=1, source_target_pairs={{0,4},{4,0},{1,5},{5,1},{2,6},{6,2},{3,7},{7,3},{8,12},{12,8},{9,1... | collective-permute-start | bytes 110600 | tf_op jit(solution)/shard_map/ppermute | solution.py:538
  32.9 2.5 %collective-permute-done.7 = f32[3,6,4,128]{3,2,1,0:T(4,128)S(1)} collective-permute-done((f32[3,6,4,128]{3,2,1,0:T(4,128)S(1)}, f32[3,6,4,128]{3,2,1,0:T(4,128)S(1)}, u32[]{:S(2)}, u32[]{:S(2)}) %collective-permute-start.7) | collective-permute-done | bytes 36896 | tf_op jit(solution)/shard_map/ppermute | solution.py:538
  35.3 0.1 collective-permute-start.8
  35.4 1.8 %collective-permute-start.9 = (f32[2,3,6,4,128]{4,3,2,1,0:T(4,128)S(1)}, f32[2,3,6,4,128]{4,3,2,1,0:T(4,128)S(1)}, u32[]{:S(2)}, u32[]{:S(2)}) collective-permute-start(f32[2,3,6,4,128]{4,3,2,1,0:T(4,128)S(1)} %pad_maximum_fusion.1.refs_10_), channel_id=1, source_target_pairs={{3,0},{2,1},{1,2},{0,3},{7,4},{6,5},{5,6},{4,7},{11,8},{10,9},{9,1... | collective-permute-start | bytes 221192 | tf_op jit(solution)/shard_map/ppermute | solution.py:540
  37.2 4.8 %shard_map.96.refs_8_.own.induced = f32[6,16,128]{2,1,0:T(8,128)S(1)} custom-call(s32[2,160]{1,0:T(2,128)S(1)} %get-tuple-element.51.tiles.refs_1_, s32[3]{0:T(128)S(1)} %get-tuple-element.52.refs_1_.sizes.refs_2_, f32[3,16,128]{2,1,0:T(8,128)S(1)} %get-tuple-element.53.place.refs_4_.refs_3_, f32[8,16,128]{2,1,0:T(8,128)S(1)} %get-tuple-element.56.refs_5_.multi, ...), custom_call_target="tpu_custom_call" | custom-call | flops 4000000000 | tf_op jit(solution)/shard_map/pallas_call | solution.py:639
  42.0 0.0 collective-permute-done.8.refs_9_
  42.0 2.3 %shard_map.97 = (f32[6,4,128]{2,1,0:T(4,128)S(1)}, f32[6,128,128]{2,1,0:T(8,128)S(1)}, f32[768,128]{1,0:T(8,128)S(1)}) custom-call(s32[2,160]{1,0:T(2,128)S(1)} %get-tuple-element.50.refs_0_, s32[3]{0:T(128)S(1)} %get-tuple-element.52.refs_1_.sizes.refs_2_, s32[4]{0:T(128)S(1)} %bitcast.48, f32[3,16,128]{2,1,0:T(8,128)S(1)} %get-tuple-element.53.place.refs_4_.refs_3_, ...), custom_call_target="tpu_custom_call" | custom-call | tf_op jit(solution)/shard_map/pallas_call | solution.py:648
  44.3 1.2 %collective-permute-start.10 = (f32[6,4,128]{2,1,0:T(4,128)S(1)}, f32[6,4,128]{2,1,0:T(4,128)S(1)}, u32[]{:S(2)}, u32[]{:S(2)}) collective-permute-start(f32[6,4,128]{2,1,0:T(4,128)S(1)} %get-tuple-element.74), channel_id=1, source_target_pairs={{8,0},{0,8},{24,16},{16,24},{9,1},{1,9},{25,17},{17,25},{10,2},{2,... | collective-permute-start | bytes 36872 | tf_op jit(solution)/shard_map/ppermute | solution.py:541
  45.5 1.2 %collective-permute-start.11 = (f32[6,4,128]{2,1,0:T(4,128)S(1)}, f32[6,4,128]{2,1,0:T(4,128)S(1)}, u32[]{:S(2)}, u32[]{:S(2)}) collective-permute-start(f32[6,4,128]{2,1,0:T(4,128)S(1)} %get-tuple-element.74), channel_id=1, source_target_pairs={{24,0},{16,8},{8,16},{0,24},{25,1},{17,9},{9,17},{1,25},{26,2},{18... | collective-permute-start | bytes 36872 | tf_op jit(solution)/shard_map/ppermute | solution.py:540
  46.7 2.2 %shard_map.98.sums_in = f32[768,128]{1,0:T(8,128)S(1)} custom-call(s32[2,160]{1,0:T(2,128)S(1)} %get-tuple-element.51.tiles.refs_1_, s32[3]{0:T(128)S(1)} %get-tuple-element.52.refs_1_.sizes.refs_2_, f32[128,4,8,128]{3,2,1,0:T(8,128)S(1)} %get-tuple-element.60.factors.refs_6_, bf16[128,256,128]{2,1,0:T(8,128)(2,1)S(1)} %get-tuple-element.66.matrix.refs_8_, ...), custom_call_target="tpu_custom_call" | custom-call | flops 4000000000 | tf_op jit(solution)/shard_map/pallas_call | solution.py:653
  48.9 2.1 %collective-permute-done.11 = f32[6,4,128]{2,1,0:T(4,128)S(1)} collective-permute-done((f32[6,4,128]{2,1,0:T(4,128)S(1)}, f32[6,4,128]{2,1,0:T(4,128)S(1)}, u32[]{:S(2)}, u32[]{:S(2)}) %collective-permute-start.11) | collective-permute-done | bytes 12320 | tf_op jit(solution)/shard_map/ppermute | solution.py:540
  51.0 0.7 collective-permute-start.12
  51.7 3.3 %collective-permute-done.12 = f32[3,6,4,128]{3,2,1,0:T(4,128)S(1)} collective-permute-done((f32[3,6,4,128]{3,2,1,0:T(4,128)S(1)}, f32[3,6,4,128]{3,2,1,0:T(4,128)S(1)}, u32[]{:S(2)}, u32[]{:S(2)}) %collective-permute-start.12) | collective-permute-done | bytes 36896 | tf_op jit(solution)/shard_map/ppermute | solution.py:538
  55.0 0.1 collective-permute-start.13
  55.1 0.7 collective-permute-start.14
  55.8 1.5 %shard_map.99 = (f32[6,16,128]{2,1,0:T(8,128)S(1)}, f32[6,16,128]{2,1,0:T(8,128)S(1)}) custom-call(s32[2,160]{1,0:T(2,128)S(1)} %get-tuple-element.51.tiles.refs_1_, s32[3]{0:T(128)S(1)} %get-tuple-element.52.refs_1_.sizes.refs_2_, f32[3,16,128]{2,1,0:T(8,128)S(1)} %get-tuple-element.53.place.refs_4_.refs_3_, ...), custom_call_target="tpu_custom_call" | custom-call | flops 4000000000 | tf_op jit(solution)/shard_map/pallas_call | solution.py:657
  57.4 1.8 %collective-permute-done.14.refs_11_ = f32[2,3,6,4,128]{4,3,2,1,0:T(4,128)S(1)} collective-permute-done((f32[2,3,6,4,128]{4,3,2,1,0:T(4,128)S(1)}, f32[2,3,6,4,128]{4,3,2,1,0:T(4,128)S(1)}, u32[]{:S(2)}, u32[]{:S(2)}) %collective-permute-start.14) | collective-permute-done | bytes 73760 | tf_op jit(solution)/shard_map/ppermute | solution.py:540
  59.1 2.3 %shard_map.100 = (f32[6,4,128]{2,1,0:T(4,128)S(1)}, f32[6,128,128]{2,1,0:T(8,128)S(1)}, f32[768,128]{1,0:T(8,128)S(1)}) custom-call(s32[2,160]{1,0:T(2,128)S(1)} %get-tuple-element.50.refs_0_, s32[3]{0:T(128)S(1)} %get-tuple-element.52.refs_1_.sizes.refs_2_, s32[4]{0:T(128)S(1)} %bitcast.49, f32[3,16,128]{2,1,0:T(8,128)S(1)} %get-tuple-element.53.place.refs_4_.refs_3_, ...), custom_call_target="tpu_custom_call" | custom-call | tf_op jit(solution)/shard_map/pallas_call | solution.py:648
  61.4 0.1 collective-permute-start.15
  61.5 1.5 %collective-permute-start.16 = (f32[6,4,128]{2,1,0:T(4,128)S(1)}, f32[6,4,128]{2,1,0:T(4,128)S(1)}, u32[]{:S(2)}, u32[]{:S(2)}) collective-permute-start(f32[6,4,128]{2,1,0:T(4,128)S(1)} %get-tuple-element.81), channel_id=1, source_target_pairs={{24,0},{16,8},{8,16},{0,24},{25,1},{17,9},{9,17},{1,25},{26,2},{18... | collective-permute-start | bytes 36872 | tf_op jit(solution)/shard_map/ppermute | solution.py:540
  63.0 2.2 %shard_map.101.sums_in = f32[768,128]{1,0:T(8,128)S(1)} custom-call(s32[2,160]{1,0:T(2,128)S(1)} %get-tuple-element.51.tiles.refs_1_, s32[3]{0:T(128)S(1)} %get-tuple-element.52.refs_1_.sizes.refs_2_, f32[128,4,8,128]{3,2,1,0:T(8,128)S(1)} %get-tuple-element.60.factors.refs_6_, bf16[128,256,128]{2,1,0:T(8,128)(2,1)S(1)} %get-tuple-element.66.matrix.refs_8_, ...), custom_call_target="tpu_custom_call" | custom-call | flops 4000000000 | tf_op jit(solution)/shard_map/pallas_call | solution.py:653
  65.2 1.8 %collective-permute-done.16 = f32[6,4,128]{2,1,0:T(4,128)S(1)} collective-permute-done((f32[6,4,128]{2,1,0:T(4,128)S(1)}, f32[6,4,128]{2,1,0:T(4,128)S(1)}, u32[]{:S(2)}, u32[]{:S(2)}) %collective-permute-start.16) | collective-permute-done | bytes 12320 | tf_op jit(solution)/shard_map/ppermute | solution.py:540
  67.1 0.7 collective-permute-start.17
  67.8 3.3 %collective-permute-done.17 = f32[3,6,4,128]{3,2,1,0:T(4,128)S(1)} collective-permute-done((f32[3,6,4,128]{3,2,1,0:T(4,128)S(1)}, f32[3,6,4,128]{3,2,1,0:T(4,128)S(1)}, u32[]{:S(2)}, u32[]{:S(2)}) %collective-permute-start.17) | collective-permute-done | bytes 36896 | tf_op jit(solution)/shard_map/ppermute | solution.py:538
  71.1 0.1 collective-permute-start.18
  71.2 0.2 collective-permute-start.19
  71.4 1.5 %shard_map.102 = (f32[6,16,128]{2,1,0:T(8,128)S(1)}, f32[6,16,128]{2,1,0:T(8,128)S(1)}) custom-call(s32[2,160]{1,0:T(2,128)S(1)} %get-tuple-element.51.tiles.refs_1_, s32[3]{0:T(128)S(1)} %get-tuple-element.52.refs_1_.sizes.refs_2_, f32[3,16,128]{2,1,0:T(8,128)S(1)} %get-tuple-element.53.place.refs_4_.refs_3_, ...), custom_call_target="tpu_custom_call" | custom-call | flops 4000000000 | tf_op jit(solution)/shard_map/pallas_call | solution.py:657
  72.9 2.3 %collective-permute-done.19.refs_11_ = f32[2,3,6,4,128]{4,3,2,1,0:T(4,128)S(1)} collective-permute-done((f32[2,3,6,4,128]{4,3,2,1,0:T(4,128)S(1)}, f32[2,3,6,4,128]{4,3,2,1,0:T(4,128)S(1)}, u32[]{:S(2)}, u32[]{:S(2)}) %collective-permute-start.19) | collective-permute-done | bytes 73760 | tf_op jit(solution)/shard_map/ppermute | solution.py:540
  75.2 2.5 %shard_map.103 = (f32[6,4,128]{2,1,0:T(4,128)S(1)}, f32[6,128,128]{2,1,0:T(8,128)S(1)}, f32[768,128]{1,0:T(8,128)S(1)}) custom-call(s32[2,160]{1,0:T(2,128)S(1)} %get-tuple-element.50.refs_0_, s32[3]{0:T(128)S(1)} %get-tuple-element.52.refs_1_.sizes.refs_2_, s32[4]{0:T(128)S(1)} %bitcast.50, f32[3,16,128]{2,1,0:T(8,128)S(1)} %get-tuple-element.53.place.refs_4_.refs_3_, ...), custom_call_target="tpu_custom_call" | custom-call | tf_op jit(solution)/shard_map/pallas_call | solution.py:648
  77.7 0.1 collective-permute-start.20
  77.8 1.1 %collective-permute-start.21 = (f32[6,4,128]{2,1,0:T(4,128)S(1)}, f32[6,4,128]{2,1,0:T(4,128)S(1)}, u32[]{:S(2)}, u32[]{:S(2)}) collective-permute-start(f32[6,4,128]{2,1,0:T(4,128)S(1)} %get-tuple-element.88), channel_id=1, source_target_pairs={{24,0},{16,8},{8,16},{0,24},{25,1},{17,9},{9,17},{1,25},{26,2},{18... | collective-permute-start | bytes 36872 | tf_op jit(solution)/shard_map/ppermute | solution.py:540
  78.9 2.2 %shard_map.104.sums_in = f32[768,128]{1,0:T(8,128)S(1)} custom-call(s32[2,160]{1,0:T(2,128)S(1)} %get-tuple-element.51.tiles.refs_1_, s32[3]{0:T(128)S(1)} %get-tuple-element.52.refs_1_.sizes.refs_2_, f32[128,4,8,128]{3,2,1,0:T(8,128)S(1)} %get-tuple-element.60.factors.refs_6_, bf16[128,256,128]{2,1,0:T(8,128)(2,1)S(1)} %get-tuple-element.66.matrix.refs_8_, ...), custom_call_target="tpu_custom_call" | custom-call | flops 4000000000 | tf_op jit(solution)/shard_map/pallas_call | solution.py:653
  81.1 0.4 collective-permute-done.20
  81.4 1.9 %collective-permute-done.21 = f32[6,4,128]{2,1,0:T(4,128)S(1)} collective-permute-done((f32[6,4,128]{2,1,0:T(4,128)S(1)}, f32[6,4,128]{2,1,0:T(4,128)S(1)}, u32[]{:S(2)}, u32[]{:S(2)}) %collective-permute-start.21) | collective-permute-done | bytes 12320 | tf_op jit(solution)/shard_map/ppermute | solution.py:540
  83.3 0.7 collective-permute-start.22
  84.1 3.3 %collective-permute-done.22 = f32[3,6,4,128]{3,2,1,0:T(4,128)S(1)} collective-permute-done((f32[3,6,4,128]{3,2,1,0:T(4,128)S(1)}, f32[3,6,4,128]{3,2,1,0:T(4,128)S(1)}, u32[]{:S(2)}, u32[]{:S(2)}) %collective-permute-start.22) | collective-permute-done | bytes 36896 | tf_op jit(solution)/shard_map/ppermute | solution.py:538
  87.4 0.1 collective-permute-start.23
  87.5 0.6 collective-permute-start.24
  88.1 1.5 %shard_map.105 = (f32[6,16,128]{2,1,0:T(8,128)S(1)}, f32[6,16,128]{2,1,0:T(8,128)S(1)}) custom-call(s32[2,160]{1,0:T(2,128)S(1)} %get-tuple-element.51.tiles.refs_1_, s32[3]{0:T(128)S(1)} %get-tuple-element.52.refs_1_.sizes.refs_2_, f32[3,16,128]{2,1,0:T(8,128)S(1)} %get-tuple-element.53.place.refs_4_.refs_3_, ...), custom_call_target="tpu_custom_call" | custom-call | flops 4000000000 | tf_op jit(solution)/shard_map/pallas_call | solution.py:657
  89.6 1.9 %collective-permute-done.24.refs_17_ = f32[2,3,6,4,128]{4,3,2,1,0:T(4,128)S(1)} collective-permute-done((f32[2,3,6,4,128]{4,3,2,1,0:T(4,128)S(1)}, f32[2,3,6,4,128]{4,3,2,1,0:T(4,128)S(1)}, u32[]{:S(2)}, u32[]{:S(2)}) %collective-permute-start.24) | collective-permute-done | bytes 73760 | tf_op jit(solution)/shard_map/ppermute | solution.py:540
  91.5 5.4 %shard_map.106 = f32[32,128]{1,0:T(8,128)} custom-call(s32[2,160]{1,0:T(2,128)S(1)} %get-tuple-element.50.refs_0_, s32[2,160]{1,0:T(2,128)S(1)} %get-tuple-element.51.tiles.refs_1_, s32[3]{0:T(128)S(1)} %get-tuple-element.52.refs_1_.sizes.refs_2_, f32[3,16,128]{2,1,0:T(8,128)S(1)} %get-tuple-element.53.place.refs_4_.refs_3_, ...), custom_call_target="tpu_custom_call" | custom-call | tf_op jit(solution)/shard_map/pallas_call | solution.py:663
  96.9 2.6 %all-to-all-start = ((f32[32,1,128]{2,1,0:T(1,128)}), f32[32,1,128]{2,1,0:T(1,128)S(1)}, u32[]{:S(2)}, u32[]{:S(2)}) async-start(f32[32,1,128]{2,1,0:T(1,128)} %bitcast.35), calls=%async_computation | async-start | bytes 32768 | tf_op jit(solution)/shard_map/all_to_all | solution.py:671
  99.5 2.4 %shard_map.107.refs_3_ = s32[16,128]{1,0:T(8,128)S(1)} custom-call(s32[16,128]{1,0:T(8,128)S(1)} %get-tuple-element.94.order), custom_call_target="tpu_custom_call" | custom-call | flops 4000000000 | tf_op jit(solution)/shard_map/pallas_call | solution.py:624
  102.0 4.6 %all-to-all-done = f32[32,1,128]{2,1,0:T(1,128)S(1)} async-done(((f32[32,1,128]{2,1,0:T(1,128)}), f32[32,1,128]{2,1,0:T(1,128)S(1)}, u32[]{:S(2)}, u32[]{:S(2)}) %all-to-all-start) | async-done | bytes 16416 | tf_op jit(solution)/shard_map/all_to_all | solution.py:671
  106.6 1.3 %shard_map.108 = f32[6,16,128]{2,1,0:T(8,128)} custom-call(f32[32,128]{1,0:T(8,128)S(1)} %bitcast.43, f32[6,16,128]{2,1,0:T(8,128)S(1)} %shard_map.96.refs_8_.own.induced, f32[6,16,128]{2,1,0:T(8,128)S(1)} %get-tuple-element.78.refs_8_.own.refs_12_.refs_0_, f32[6,16,128]{2,1,0:T(8,128)S(1)} %get-tuple-element.85.refs_8_.own.refs_13_.refs_1_, ...), custom_call_target="tpu_custom_call" | custom-call | tf_op jit(solution)/shard_map/pallas_call | solution.py:672
  (23 shorter events, 0.2 us)
Async XLA Ops:
  0.0 16.6 %copy-start = (s32[1,1,1,4]{3,2,1,0:T(1,128)S(1)}, s32[1,1,1,4]{3,2,1,0:T(1,128)}, u32[]{:S(2)}) copy-start(s32[1,1,1,4]{3,2,1,0:T(1,128)} %param.15) | copy-start | bytes 52
  0.0 7.3 %copy-start.1 = (s32[3,1,1,1,128]{4,3,2,1,0:T(1,128)S(1)}, s32[3,1,1,1,128]{4,3,2,1,0:T(1,128)}, u32[]{:S(2)}) copy-start(s32[3,1,1,1,128]{4,3,2,1,0:T(1,128)} %param.16) | copy-start | bytes 4612
  1.5 6.9 %collective-permute-start.1 = (f32[11,4,128]{2,1,0:T(4,128)S(1)}, f32[11,4,128]{2,1,0:T(4,128)S(1)}, u32[]{:S(2)}, u32[]{:S(2)}) collective-permute-start(f32[11,4,128]{2,1,0:T(4,128)S(1)} %get-tuple-element.57), channel_id=1, source_target_pairs={{24,0},{16,8},{8,16},{0,24},{25,1},{17,9},{9,17},{1,25},{26,2},{18... | collective-permute-start | bytes 67592 | tf_op jit(solution)/shard_map/ppermute | solution.py:540
  6.7 3.8 %collective-permute-start = (f32[11,4,128]{2,1,0:T(4,128)S(1)}, f32[11,4,128]{2,1,0:T(4,128)S(1)}, u32[]{:S(2)}, u32[]{:S(2)}) collective-permute-start(f32[11,4,128]{2,1,0:T(4,128)S(1)} %get-tuple-element.57), channel_id=1, source_target_pairs={{8,0},{0,8},{24,16},{16,24},{9,1},{1,9},{25,17},{17,25},{10,2},{2,... | collective-permute-start | bytes 67592 | tf_op jit(solution)/shard_map/ppermute | solution.py:541
  10.5 4.4 %collective-permute-start.2 = (f32[3,11,4,128]{3,2,1,0:T(4,128)S(1)}, f32[3,11,4,128]{3,2,1,0:T(4,128)S(1)}, u32[]{:S(2)}, u32[]{:S(2)}) collective-permute-start(f32[3,11,4,128]{3,2,1,0:T(4,128)S(1)} %pad_maximum_fusion.5), channel_id=1, source_target_pairs={{0,4},{4,0},{1,5},{5,1},{2,6},{6,2},{3,7},{7,3},{8,12},{12,8},{9,1... | collective-permute-start | bytes 202760 | tf_op jit(solution)/shard_map/ppermute | solution.py:538
  14.9 5.4 %collective-permute-start.3 = (f32[2,3,11,4,128]{4,3,2,1,0:T(4,128)S(1)}, f32[2,3,11,4,128]{4,3,2,1,0:T(4,128)S(1)}, u32[]{:S(2)}, u32[]{:S(2)}) collective-permute-start(f32[2,3,11,4,128]{4,3,2,1,0:T(4,128)S(1)} %pad_maximum_fusion.refs_10_), channel_id=1, source_target_pairs={{1,0},{0,1},{3,2},{2,3},{5,4},{4,5},{7,6},{6,7},{9,8},{8,9},{11,10... | collective-permute-start | bytes 405512 | tf_op jit(solution)/shard_map/ppermute | solution.py:541
  15.0 5.3 %collective-permute-start.4 = (f32[2,3,11,4,128]{4,3,2,1,0:T(4,128)S(1)}, f32[2,3,11,4,128]{4,3,2,1,0:T(4,128)S(1)}, u32[]{:S(2)}, u32[]{:S(2)}) collective-permute-start(f32[2,3,11,4,128]{4,3,2,1,0:T(4,128)S(1)} %pad_maximum_fusion.refs_10_), channel_id=1, source_target_pairs={{3,0},{2,1},{1,2},{0,3},{7,4},{6,5},{5,6},{4,7},{11,8},{10,9},{9,1... | collective-permute-start | bytes 405512 | tf_op jit(solution)/shard_map/ppermute | solution.py:540
  25.6 4.4 %collective-permute-start.5 = (f32[6,4,128]{2,1,0:T(4,128)S(1)}, f32[6,4,128]{2,1,0:T(4,128)S(1)}, u32[]{:S(2)}, u32[]{:S(2)}) collective-permute-start(f32[6,4,128]{2,1,0:T(4,128)S(1)} %get-tuple-element.62), channel_id=1, source_target_pairs={{8,0},{0,8},{24,16},{16,24},{9,1},{1,9},{25,17},{17,25},{10,2},{2,... | collective-permute-start | bytes 36872 | tf_op jit(solution)/shard_map/ppermute | solution.py:541
  25.7 5.6 %collective-permute-start.6 = (f32[6,4,128]{2,1,0:T(4,128)S(1)}, f32[6,4,128]{2,1,0:T(4,128)S(1)}, u32[]{:S(2)}, u32[]{:S(2)}) collective-permute-start(f32[6,4,128]{2,1,0:T(4,128)S(1)} %get-tuple-element.62), channel_id=1, source_target_pairs={{24,0},{16,8},{8,16},{0,24},{25,1},{17,9},{9,17},{1,25},{26,2},{18... | collective-permute-start | bytes 36872 | tf_op jit(solution)/shard_map/ppermute | solution.py:540
  31.3 4.0 %collective-permute-start.7 = (f32[3,6,4,128]{3,2,1,0:T(4,128)S(1)}, f32[3,6,4,128]{3,2,1,0:T(4,128)S(1)}, u32[]{:S(2)}, u32[]{:S(2)}) collective-permute-start(f32[3,6,4,128]{3,2,1,0:T(4,128)S(1)} %pad_maximum_fusion.6), channel_id=1, source_target_pairs={{0,4},{4,0},{1,5},{5,1},{2,6},{6,2},{3,7},{7,3},{8,12},{12,8},{9,1... | collective-permute-start | bytes 110600 | tf_op jit(solution)/shard_map/ppermute | solution.py:538
  35.3 6.7 %collective-permute-start.8 = (f32[2,3,6,4,128]{4,3,2,1,0:T(4,128)S(1)}, f32[2,3,6,4,128]{4,3,2,1,0:T(4,128)S(1)}, u32[]{:S(2)}, u32[]{:S(2)}) collective-permute-start(f32[2,3,6,4,128]{4,3,2,1,0:T(4,128)S(1)} %pad_maximum_fusion.1.refs_10_), channel_id=1, source_target_pairs={{1,0},{0,1},{3,2},{2,3},{5,4},{4,5},{7,6},{6,7},{9,8},{8,9},{11,10... | collective-permute-start | bytes 221192 | tf_op jit(solution)/shard_map/ppermute | solution.py:541
  35.4 6.6 %collective-permute-start.9 = (f32[2,3,6,4,128]{4,3,2,1,0:T(4,128)S(1)}, f32[2,3,6,4,128]{4,3,2,1,0:T(4,128)S(1)}, u32[]{:S(2)}, u32[]{:S(2)}) collective-permute-start(f32[2,3,6,4,128]{4,3,2,1,0:T(4,128)S(1)} %pad_maximum_fusion.1.refs_10_), channel_id=1, source_target_pairs={{3,0},{2,1},{1,2},{0,3},{7,4},{6,5},{5,6},{4,7},{11,8},{10,9},{9,1... | collective-permute-start | bytes 221192 | tf_op jit(solution)/shard_map/ppermute | solution.py:540
  44.3 4.6 %collective-permute-start.10 = (f32[6,4,128]{2,1,0:T(4,128)S(1)}, f32[6,4,128]{2,1,0:T(4,128)S(1)}, u32[]{:S(2)}, u32[]{:S(2)}) collective-permute-start(f32[6,4,128]{2,1,0:T(4,128)S(1)} %get-tuple-element.74), channel_id=1, source_target_pairs={{8,0},{0,8},{24,16},{16,24},{9,1},{1,9},{25,17},{17,25},{10,2},{2,... | collective-permute-start | bytes 36872 | tf_op jit(solution)/shard_map/ppermute | solution.py:541
  45.5 5.5 %collective-permute-start.11 = (f32[6,4,128]{2,1,0:T(4,128)S(1)}, f32[6,4,128]{2,1,0:T(4,128)S(1)}, u32[]{:S(2)}, u32[]{:S(2)}) collective-permute-start(f32[6,4,128]{2,1,0:T(4,128)S(1)} %get-tuple-element.74), channel_id=1, source_target_pairs={{24,0},{16,8},{8,16},{0,24},{25,1},{17,9},{9,17},{1,25},{26,2},{18... | collective-permute-start | bytes 36872 | tf_op jit(solution)/shard_map/ppermute | solution.py:540
  51.0 4.0 %collective-permute-start.12 = (f32[3,6,4,128]{3,2,1,0:T(4,128)S(1)}, f32[3,6,4,128]{3,2,1,0:T(4,128)S(1)}, u32[]{:S(2)}, u32[]{:S(2)}) collective-permute-start(f32[3,6,4,128]{3,2,1,0:T(4,128)S(1)} %pad_maximum_fusion.7), channel_id=1, source_target_pairs={{0,4},{4,0},{1,5},{5,1},{2,6},{6,2},{3,7},{7,3},{8,12},{12,8},{9,1... | collective-permute-start | bytes 110600 | tf_op jit(solution)/shard_map/ppermute | solution.py:538
  55.0 2.3 %collective-permute-start.13 = (f32[2,3,6,4,128]{4,3,2,1,0:T(4,128)S(1)}, f32[2,3,6,4,128]{4,3,2,1,0:T(4,128)S(1)}, u32[]{:S(2)}, u32[]{:S(2)}) collective-permute-start(f32[2,3,6,4,128]{4,3,2,1,0:T(4,128)S(1)} %pad_maximum_fusion.2.refs_10_), channel_id=1, source_target_pairs={{1,0},{0,1},{3,2},{2,3},{5,4},{4,5},{7,6},{6,7},{9,8},{8,9},{11,10... | collective-permute-start | bytes 221192 | tf_op jit(solution)/shard_map/ppermute | solution.py:541
  55.1 4.0 %collective-permute-start.14 = (f32[2,3,6,4,128]{4,3,2,1,0:T(4,128)S(1)}, f32[2,3,6,4,128]{4,3,2,1,0:T(4,128)S(1)}, u32[]{:S(2)}, u32[]{:S(2)}) collective-permute-start(f32[2,3,6,4,128]{4,3,2,1,0:T(4,128)S(1)} %pad_maximum_fusion.2.refs_10_), channel_id=1, source_target_pairs={{3,0},{2,1},{1,2},{0,3},{7,4},{6,5},{5,6},{4,7},{11,8},{10,9},{9,1... | collective-permute-start | bytes 221192 | tf_op jit(solution)/shard_map/ppermute | solution.py:540
  61.4 3.8 %collective-permute-start.15 = (f32[6,4,128]{2,1,0:T(4,128)S(1)}, f32[6,4,128]{2,1,0:T(4,128)S(1)}, u32[]{:S(2)}, u32[]{:S(2)}) collective-permute-start(f32[6,4,128]{2,1,0:T(4,128)S(1)} %get-tuple-element.81), channel_id=1, source_target_pairs={{8,0},{0,8},{24,16},{16,24},{9,1},{1,9},{25,17},{17,25},{10,2},{2,... | collective-permute-start | bytes 36872 | tf_op jit(solution)/shard_map/ppermute | solution.py:541
  61.5 5.6 %collective-permute-start.16 = (f32[6,4,128]{2,1,0:T(4,128)S(1)}, f32[6,4,128]{2,1,0:T(4,128)S(1)}, u32[]{:S(2)}, u32[]{:S(2)}) collective-permute-start(f32[6,4,128]{2,1,0:T(4,128)S(1)} %get-tuple-element.81), channel_id=1, source_target_pairs={{24,0},{16,8},{8,16},{0,24},{25,1},{17,9},{9,17},{1,25},{26,2},{18... | collective-permute-start | bytes 36872 | tf_op jit(solution)/shard_map/ppermute | solution.py:540
  67.1 4.0 %collective-permute-start.17 = (f32[3,6,4,128]{3,2,1,0:T(4,128)S(1)}, f32[3,6,4,128]{3,2,1,0:T(4,128)S(1)}, u32[]{:S(2)}, u32[]{:S(2)}) collective-permute-start(f32[3,6,4,128]{3,2,1,0:T(4,128)S(1)} %pad_maximum_fusion.8), channel_id=1, source_target_pairs={{0,4},{4,0},{1,5},{5,1},{2,6},{6,2},{3,7},{7,3},{8,12},{12,8},{9,1... | collective-permute-start | bytes 110600 | tf_op jit(solution)/shard_map/ppermute | solution.py:538
  71.1 1.8 %collective-permute-start.18 = (f32[2,3,6,4,128]{4,3,2,1,0:T(4,128)S(1)}, f32[2,3,6,4,128]{4,3,2,1,0:T(4,128)S(1)}, u32[]{:S(2)}, u32[]{:S(2)}) collective-permute-start(f32[2,3,6,4,128]{4,3,2,1,0:T(4,128)S(1)} %pad_maximum_fusion.3.refs_10_), channel_id=1, source_target_pairs={{1,0},{0,1},{3,2},{2,3},{5,4},{4,5},{7,6},{6,7},{9,8},{8,9},{11,10... | collective-permute-start | bytes 221192 | tf_op jit(solution)/shard_map/ppermute | solution.py:541
  71.2 4.0 %collective-permute-start.19 = (f32[2,3,6,4,128]{4,3,2,1,0:T(4,128)S(1)}, f32[2,3,6,4,128]{4,3,2,1,0:T(4,128)S(1)}, u32[]{:S(2)}, u32[]{:S(2)}) collective-permute-start(f32[2,3,6,4,128]{4,3,2,1,0:T(4,128)S(1)} %pad_maximum_fusion.3.refs_10_), channel_id=1, source_target_pairs={{3,0},{2,1},{1,2},{0,3},{7,4},{6,5},{5,6},{4,7},{11,8},{10,9},{9,1... | collective-permute-start | bytes 221192 | tf_op jit(solution)/shard_map/ppermute | solution.py:540
  77.7 3.8 %collective-permute-start.20 = (f32[6,4,128]{2,1,0:T(4,128)S(1)}, f32[6,4,128]{2,1,0:T(4,128)S(1)}, u32[]{:S(2)}, u32[]{:S(2)}) collective-permute-start(f32[6,4,128]{2,1,0:T(4,128)S(1)} %get-tuple-element.88), channel_id=1, source_target_pairs={{8,0},{0,8},{24,16},{16,24},{9,1},{1,9},{25,17},{17,25},{10,2},{2,... | collective-permute-start | bytes 36872 | tf_op jit(solution)/shard_map/ppermute | solution.py:541
  77.8 5.6 %collective-permute-start.21 = (f32[6,4,128]{2,1,0:T(4,128)S(1)}, f32[6,4,128]{2,1,0:T(4,128)S(1)}, u32[]{:S(2)}, u32[]{:S(2)}) collective-permute-start(f32[6,4,128]{2,1,0:T(4,128)S(1)} %get-tuple-element.88), channel_id=1, source_target_pairs={{24,0},{16,8},{8,16},{0,24},{25,1},{17,9},{9,17},{1,25},{26,2},{18... | collective-permute-start | bytes 36872 | tf_op jit(solution)/shard_map/ppermute | solution.py:540
  83.3 4.0 %collective-permute-start.22 = (f32[3,6,4,128]{3,2,1,0:T(4,128)S(1)}, f32[3,6,4,128]{3,2,1,0:T(4,128)S(1)}, u32[]{:S(2)}, u32[]{:S(2)}) collective-permute-start(f32[3,6,4,128]{3,2,1,0:T(4,128)S(1)} %pad_maximum_fusion.9), channel_id=1, source_target_pairs={{0,4},{4,0},{1,5},{5,1},{2,6},{6,2},{3,7},{7,3},{8,12},{12,8},{9,1... | collective-permute-start | bytes 110600 | tf_op jit(solution)/shard_map/ppermute | solution.py:538
  87.4 2.2 %collective-permute-start.23 = (f32[2,3,6,4,128]{4,3,2,1,0:T(4,128)S(1)}, f32[2,3,6,4,128]{4,3,2,1,0:T(4,128)S(1)}, u32[]{:S(2)}, u32[]{:S(2)}) collective-permute-start(f32[2,3,6,4,128]{4,3,2,1,0:T(4,128)S(1)} %pad_maximum_fusion.4.refs_16_), channel_id=1, source_target_pairs={{1,0},{0,1},{3,2},{2,3},{5,4},{4,5},{7,6},{6,7},{9,8},{8,9},{11,10... | collective-permute-start | bytes 221192 | tf_op jit(solution)/shard_map/ppermute | solution.py:541
  87.5 4.0 %collective-permute-start.24 = (f32[2,3,6,4,128]{4,3,2,1,0:T(4,128)S(1)}, f32[2,3,6,4,128]{4,3,2,1,0:T(4,128)S(1)}, u32[]{:S(2)}, u32[]{:S(2)}) collective-permute-start(f32[2,3,6,4,128]{4,3,2,1,0:T(4,128)S(1)} %pad_maximum_fusion.4.refs_16_), channel_id=1, source_target_pairs={{3,0},{2,1},{1,2},{0,3},{7,4},{6,5},{5,6},{4,7},{11,8},{10,9},{9,1... | collective-permute-start | bytes 221192 | tf_op jit(solution)/shard_map/ppermute | solution.py:540
  96.9 9.7 %all-to-all-start = ((f32[32,1,128]{2,1,0:T(1,128)}), f32[32,1,128]{2,1,0:T(1,128)S(1)}, u32[]{:S(2)}, u32[]{:S(2)}) async-start(f32[32,1,128]{2,1,0:T(1,128)} %bitcast.35), calls=%async_computation | async-start | bytes 32768 | tf_op jit(solution)/shard_map/all_to_all | solution.py:671
